TPU v7x, 32 devices: a whole 2x2x4 slice. The times are simulated.
32 devices in a mesh: groups: 1, seq: 32 (over z, y, x, core).
Axes of the slice: x: 2, y: 2, z: 4, core: 2. Of those that a mesh axis runs over, the one named last changes fastest.
Arguments:
- features: bfloat16 [4096, 768], P(('groups', 'seq')), may hold values from -6 to 6
- first_layer_taps: bfloat16 [3, 768, 768], replicated, may hold values from -0.125 to 0.125
- second_layer_taps: bfloat16 [3, 768, 768], replicated, may hold values from -0.125 to 0.125
- upstream: bfloat16 [4096, 768], P(('groups', 'seq')), may hold values from -6 to 6
Outputs:
- second_layer_output: bfloat16 [4096, 768], P(('groups', 'seq'))
- input_gradient: bfloat16 [4096, 768], P(('groups', 'seq'))
- first_taps_gradient: float32 [3, 768, 768], P(None, 'groups', 'seq')
All inputs are finite; a program needn't handle non-finite values.
Results may differ from a plain program's by a relative error of at most 0.0095.
Values may be sent and summed in bfloat16 or wider, within the bound.
No kernel may reach another device: no remote copies, remote signals or barrier semaphores. Data moves between devices by JAX's collectives and lax.ppermute only.
A program may use at most 128 MiB of HBM per device.

v0:
```python
import jax
import jax.numpy as jnp
from jax import lax
from jax.sharding import PartitionSpec as P

DILATION_ONE = 256
DILATION_TWO = 2048


def from_behind(array, axis, by):
    size = lax.axis_size(axis)
    pairs = [(i, i + by) for i in range(size) if 0 <= i + by < size]
    return lax.ppermute(array, axis, pairs)


def gelu_pair(values):
    wide = values.astype(jnp.float32)
    return jax.jvp(jax.nn.gelu, (wide,), (jnp.ones_like(wide),))


def reach(values, offset, move_main):
    rows = values.shape[0]
    blocks = abs(offset) // rows
    if offset > 0:
        main = move_main(values, -blocks)
        return main
    main = move_main(values, blocks)
    return main


def reach_acts(values, offset):
    return reach(values, offset, lambda piece, steps: from_behind(piece, "seq", steps))


def reach_cots(values, offset):
    return reach(values, offset, lambda piece, steps: from_behind(piece, "seq", steps))


def residual_layer_forward(inputs, kernel, dilation):
    acts = gelu_pair(inputs)[0].astype(jnp.bfloat16)
    conv = jnp.dot(acts, kernel[1], preferred_element_type=jnp.float32)
    conv = conv + jnp.dot(
        reach_acts(acts, -dilation), kernel[0], preferred_element_type=jnp.float32
    )
    conv = conv + jnp.dot(reach_acts(acts, dilation), kernel[2], preferred_element_type=jnp.float32)
    outputs = (inputs.astype(jnp.float32) + conv).astype(jnp.bfloat16)
    return (acts, outputs)


def moved_cotangents(cotan, dilation):
    moved_list = []
    for k in range(3):
        offset = -(k - 1) * dilation
        moved_list.append(cotan if offset == 0 else reach_cots(cotan, offset))
    return moved_list


def cotangent_products(inputs, kernel, cotan, moved_list):
    back = jnp.zeros(inputs.shape, jnp.float32)
    for k in range(3):
        back = back + jnp.einsum(
            "bo,io->bi", moved_list[k], kernel[k], preferred_element_type=jnp.float32
        )
    slope = gelu_pair(inputs)[1]
    return (cotan.astype(jnp.float32) + slope * back).astype(jnp.bfloat16)


def kernel_terms(acts, moved_list):
    grads = []
    for k in range(3):
        grads.append(
            jnp.einsum("bi,bo->io", acts, moved_list[k], preferred_element_type=jnp.float32)
        )
    return jnp.stack(grads, 0)


def local(features, first_layer_taps, second_layer_taps, upstream):
    first_dilation = DILATION_ONE
    second_dilation = DILATION_TWO
    first_layer_activations, first_layer_output = residual_layer_forward(
        features, first_layer_taps, first_dilation
    )
    second_layer_activations, second_layer_output = residual_layer_forward(
        first_layer_output, second_layer_taps, second_dilation
    )
    second_moved = moved_cotangents(upstream, second_dilation)
    middle_gradient = cotangent_products(
        first_layer_output, second_layer_taps, upstream, second_moved
    )
    first_moved = moved_cotangents(middle_gradient, first_dilation)
    terms_first = kernel_terms(first_layer_activations, first_moved)
    input_gradient = cotangent_products(features, first_layer_taps, middle_gradient, first_moved)
    first_taps_gradient = lax.psum_scatter(terms_first, "seq", scatter_dimension=2, tiled=True)
    return (second_layer_output, input_gradient, first_taps_gradient)


def solution(mesh):
    placed = (P(("groups", "seq"), None), P(), P(), P(("groups", "seq"), None))
    return jax.shard_map(
        local,
        mesh=mesh,
        in_specs=placed,
        out_specs=(
            P(("groups", "seq"), None),
            P(("groups", "seq"), None),
            P(None, "groups", "seq"),
        ),
        check_vma=False,
    )
```

profile of v0, /device:TPU:16, one launch (start us, length us, event | category | flops | bytes accessed | tf_op | source)
XLA Modules:
  0.0 267.7 jit_solution(14771515241460963075)
XLA Ops:
  7.2 1.2 fusion.65
  8.5 3.4 %collective-permute-start = (bf16[128,768]{1,0:T(8,128)(2,1)S(1)}, bf16[128,768]{1,0:T(8,128)(2,1)S(1)}, u32[]{:S(2)}, u32[]{:S(2)}) collective-permute-start(bf16[128,768]{1,0:T(8,128)(2,1)S(1)} %fusion.65), channel_id=1, source_target_pairs={{0,2},{1,3},{2,4},{3,5},{4,6},{5,7},{6,8},{7,9},{8,10},{9,11},{10,... | collective-permute-start | bytes 589832 | tf_op jit(solution)/shard_map/ppermute | solution.py:13
  11.9 4.2 %collective-permute-start.1 = (bf16[128,768]{1,0:T(8,128)(2,1)S(1)}, bf16[128,768]{1,0:T(8,128)(2,1)S(1)}, u32[]{:S(2)}, u32[]{:S(2)}) collective-permute-start(bf16[128,768]{1,0:T(8,128)(2,1)S(1)} %fusion.65), channel_id=1, source_target_pairs={{2,0},{3,1},{4,2},{5,3},{6,4},{7,5},{8,6},{9,7},{10,8},{11,9},{12,... | collective-permute-start | bytes 589832 | tf_op jit(solution)/shard_map/ppermute | solution.py:13
  16.1 1.3 collective-permute-start.5
  17.4 5.5 %collective-permute-start.4 = (bf16[128,768]{1,0:T(8,128)(2,1)}, bf16[128,768]{1,0:T(8,128)(2,1)S(1)}, u32[]{:S(2)}, u32[]{:S(2)}) collective-permute-start(bf16[128,768]{1,0:T(8,128)(2,1)} %param.7), channel_id=1, source_target_pairs={{16,0},{17,1},{18,2},{19,3},{20,4},{21,5},{22,6},{23,7},{24,8},{25... | collective-permute-start | bytes 589832 | tf_op jit(solution)/shard_map/ppermute | solution.py:13
  22.9 1.8 fusion.21
  24.7 2.0 fusion.10
  27.5 0.5 fusion.5
  28.0 2.7 %collective-permute-done.4 = bf16[128,768]{1,0:T(8,128)(2,1)S(1)} collective-permute-done((bf16[128,768]{1,0:T(8,128)(2,1)}, bf16[128,768]{1,0:T(8,128)(2,1)S(1)}, u32[]{:S(2)}, u32[]{:S(2)}) %collective-permute-start.4) | collective-permute-done | bytes 196640 | tf_op jit(solution)/shard_map/ppermute | solution.py:13
  30.7 1.3 fusion.57
  32.0 1.9 collective-permute-start.7
  33.9 5.7 %collective-permute-start.6 = (bf16[128,768]{1,0:T(8,128)(2,1)S(1)}, bf16[128,768]{1,0:T(8,128)(2,1)S(1)}, u32[]{:S(2)}, u32[]{:S(2)}) collective-permute-start(bf16[128,768]{1,0:T(8,128)(2,1)S(1)} %get-tuple-element.9), channel_id=1, source_target_pairs={{2,0},{3,1},{4,2},{5,3},{6,4},{7,5},{8,6},{9,7},{10,8},{11,9},{12,... | collective-permute-start | bytes 589832 | tf_op jit(solution)/shard_map/ppermute | solution.py:13
  39.6 0.6 convolution_bitcast_fusion.1
  40.2 1.3 collective-permute-done.7
  41.5 0.6 convolution_bitcast_fusion
  42.1 1.8 collective-permute-done.6
  43.9 0.7 copy-done.12
  44.6 0.6 convolution_bitcast_fusion.2
  45.2 3.3 %pad_maximum_fusion = f32[3,768,768]{2,1,0:T(8,128)} fusion(f32[1,768,768]{2,1,0:T(8,128)S(1)} %convolution_bitcast_fusion, f32[1,768,768]{2,1,0:T(8,128)S(1)} %convolution_bitcast_fusion.1, f32[1,768,768]{2,1,0:T(8,128)S(1)} %convolution_bitcast_fusion.2), kind=kLoop, calls=%fused_computation | loop fusion | flops 3538944 | bytes 14155776 | tf_op jit(solution)/shard_map/stack | solution.py:74
  48.4 11.0 %copy.8 = f32[3,768,768]{1,0,2:T(4,128)} copy(f32[3,768,768]{2,1,0:T(8,128)} %pad_maximum_fusion) | data formatting | bytes 14155776 | tf_op jit(solution)/shard_map/stack | solution.py:74
  59.5 1.6 collective-permute-start.2
  61.1 5.6 %collective-permute-start.3 = (bf16[128,768]{1,0:T(8,128)(2,1)}, bf16[128,768]{1,0:T(8,128)(2,1)S(1)}, u32[]{:S(2)}, u32[]{:S(2)}) collective-permute-start(bf16[128,768]{1,0:T(8,128)(2,1)} %get-tuple-element.10), channel_id=1, source_target_pairs={{16,0},{17,1},{18,2},{19,3},{20,4},{21,5},{22,6},{23,7},{24,8},{25... | collective-permute-start | bytes 589832 | tf_op jit(solution)/shard_map/ppermute | solution.py:13
  66.7 1.3 fusion.12
  68.0 2.0 fusion.19
  70.0 1.8 collective-permute-done.2
  72.1 0.5 fusion.14
  72.6 5.3 %collective-permute-done.3 = bf16[128,768]{1,0:T(8,128)(2,1)S(1)} collective-permute-done((bf16[128,768]{1,0:T(8,128)(2,1)}, bf16[128,768]{1,0:T(8,128)(2,1)S(1)}, u32[]{:S(2)}, u32[]{:S(2)}) %collective-permute-start.3) | collective-permute-done | bytes 196640 | tf_op jit(solution)/shard_map/ppermute | solution.py:13
  78.0 1.0 fusion.23
  79.0 1.3 add_convert_fusion
  80.3 178.8 %all-reduce.3.cloned.1.call-done = f32[3,768,768]{1,0,2:T(4,128)} async-done(((f32[3,768,768]{1,0,2:T(4,128)}), f32[3,768,768]{1,0,2:T(4,128)}) %all-reduce.3.cloned.1.call-update) | async-done | bytes 7077904
  259.1 1.0 constant_dynamic-slice_fusion
  260.1 0.7 copy.9
  (35 shorter events, 1.1 us)
Async XLA Ops:
  7.2 251.9 %all-reduce.3.cloned.1.call-start = ((), (), s32[]{:S(2)}) async-start(), calls=%async_computation | async-start | bytes 18874368
  7.2 19.5 %copy-start.1 = (bf16[3,768,768]{2,1,0:T(8,128)(2,1)S(1)}, bf16[3,768,768]{2,1,0:T(8,128)(2,1)}, u32[]{:S(2)}) copy-start(bf16[3,768,768]{2,1,0:T(8,128)(2,1)} %param.5) | copy-start | bytes 10616836
  7.2 19.9 %copy-start.3 = (bf16[128,768]{1,0:T(8,128)(2,1)S(1)}, bf16[128,768]{1,0:T(8,128)(2,1)}, u32[]{:S(2)}) copy-start(bf16[128,768]{1,0:T(8,128)(2,1)} %param.4) | copy-start | bytes 589828
  8.5 18.3 %collective-permute-start = (bf16[128,768]{1,0:T(8,128)(2,1)S(1)}, bf16[128,768]{1,0:T(8,128)(2,1)S(1)}, u32[]{:S(2)}, u32[]{:S(2)}) collective-permute-start(bf16[128,768]{1,0:T(8,128)(2,1)S(1)} %fusion.65), channel_id=1, source_target_pairs={{0,2},{1,3},{2,4},{3,5},{4,6},{5,7},{6,8},{7,9},{8,10},{9,11},{10,... | collective-permute-start | bytes 589832 | tf_op jit(solution)/shard_map/ppermute | solution.py:13
  11.9 15.2 %collective-permute-start.1 = (bf16[128,768]{1,0:T(8,128)(2,1)S(1)}, bf16[128,768]{1,0:T(8,128)(2,1)S(1)}, u32[]{:S(2)}, u32[]{:S(2)}) collective-permute-start(bf16[128,768]{1,0:T(8,128)(2,1)S(1)} %fusion.65), channel_id=1, source_target_pairs={{2,0},{3,1},{4,2},{5,3},{6,4},{7,5},{8,6},{9,7},{10,8},{11,9},{12,... | collective-permute-start | bytes 589832 | tf_op jit(solution)/shard_map/ppermute | solution.py:13
  16.1 11.3 %collective-permute-start.5 = (bf16[128,768]{1,0:T(8,128)(2,1)}, bf16[128,768]{1,0:T(8,128)(2,1)S(1)}, u32[]{:S(2)}, u32[]{:S(2)}) collective-permute-start(bf16[128,768]{1,0:T(8,128)(2,1)} %param.7), channel_id=1, source_target_pairs={{0,16},{1,17},{2,18},{3,19},{4,20},{5,21},{6,22},{7,23},{8,24},{9,... | collective-permute-start | bytes 589832 | tf_op jit(solution)/shard_map/ppermute | solution.py:13
  17.4 13.3 %collective-permute-start.4 = (bf16[128,768]{1,0:T(8,128)(2,1)}, bf16[128,768]{1,0:T(8,128)(2,1)S(1)}, u32[]{:S(2)}, u32[]{:S(2)}) collective-permute-start(bf16[128,768]{1,0:T(8,128)(2,1)} %param.7), channel_id=1, source_target_pairs={{16,0},{17,1},{18,2},{19,3},{20,4},{21,5},{22,6},{23,7},{24,8},{25... | collective-permute-start | bytes 589832 | tf_op jit(solution)/shard_map/ppermute | solution.py:13
  24.6 2.8 %copy-start = (bf16[3,768,768]{2,1,0:T(8,128)(2,1)S(1)}, bf16[3,768,768]{2,1,0:T(8,128)(2,1)}, u32[]{:S(2)}) copy-start(bf16[3,768,768]{2,1,0:T(8,128)(2,1)} %param.6) | copy-start | bytes 10616836
  26.7 4.0 %copy-start.11 = (bf16[128,768]{1,0:T(8,128)(2,1)S(1)}, bf16[128,768]{1,0:T(8,128)(2,1)}, u32[]{:S(2)}) copy-start(bf16[128,768]{1,0:T(8,128)(2,1)} %param.7) | copy-start | bytes 589828
  27.4 12.8 %copy-start.5 = (f32[128,768]{1,0:T(8,128)}, f32[128,768]{1,0:T(8,128)S(1)}, u32[]{:S(2)}) copy-start(f32[128,768]{1,0:T(8,128)S(1)} %fusion.29) | copy-start | bytes 1179652
  32.0 10.1 %copy-start.7 = (bf16[128,768]{1,0:T(8,128)(2,1)}, bf16[128,768]{1,0:T(8,128)(2,1)S(1)}, u32[]{:S(2)}) copy-start(bf16[128,768]{1,0:T(8,128)(2,1)S(1)} %get-tuple-element.9) | copy-start | bytes 589828
  32.0 9.5 %collective-permute-start.7 = (bf16[128,768]{1,0:T(8,128)(2,1)S(1)}, bf16[128,768]{1,0:T(8,128)(2,1)S(1)}, u32[]{:S(2)}, u32[]{:S(2)}) collective-permute-start(bf16[128,768]{1,0:T(8,128)(2,1)S(1)} %get-tuple-element.9), channel_id=1, source_target_pairs={{0,2},{1,3},{2,4},{3,5},{4,6},{5,7},{6,8},{7,9},{8,10},{9,11},{10,... | collective-permute-start | bytes 589832 | tf_op jit(solution)/shard_map/ppermute | solution.py:13
  33.9 10.0 %collective-permute-start.6 = (bf16[128,768]{1,0:T(8,128)(2,1)S(1)}, bf16[128,768]{1,0:T(8,128)(2,1)S(1)}, u32[]{:S(2)}, u32[]{:S(2)}) collective-permute-start(bf16[128,768]{1,0:T(8,128)(2,1)S(1)} %get-tuple-element.9), channel_id=1, source_target_pairs={{2,0},{3,1},{4,2},{5,3},{6,4},{7,5},{8,6},{9,7},{10,8},{11,9},{12,... | collective-permute-start | bytes 589832 | tf_op jit(solution)/shard_map/ppermute | solution.py:13
  41.5 2.4 copy-start.9
  43.9 0.7 copy-start.12
  59.5 12.6 %copy-start.2 = (bf16[3,768,768]{2,1,0:T(8,128)(2,1)S(1)}, bf16[3,768,768]{2,1,0:T(8,128)(2,1)}, u32[]{:S(2)}) copy-start(bf16[3,768,768]{2,1,0:T(8,128)(2,1)} %param.5) | copy-start | bytes 10616836
  59.5 12.6 %copy-start.10 = (bf16[128,768]{1,0:T(8,128)(2,1)S(1)}, bf16[128,768]{1,0:T(8,128)(2,1)}, u32[]{:S(2)}) copy-start(bf16[128,768]{1,0:T(8,128)(2,1)} %copy-done.9) | copy-start | bytes 589828
  59.5 18.5 %copy-start.6 = (f32[128,768]{1,0:T(8,128)S(1)}, f32[128,768]{1,0:T(8,128)}, u32[]{:S(2)}) copy-start(f32[128,768]{1,0:T(8,128)} %copy-done.5) | copy-start | bytes 1179652
  59.5 12.2 %collective-permute-start.2 = (bf16[128,768]{1,0:T(8,128)(2,1)}, bf16[128,768]{1,0:T(8,128)(2,1)S(1)}, u32[]{:S(2)}, u32[]{:S(2)}) collective-permute-start(bf16[128,768]{1,0:T(8,128)(2,1)} %get-tuple-element.10), channel_id=1, source_target_pairs={{0,16},{1,17},{2,18},{3,19},{4,20},{5,21},{6,22},{7,23},{8,24},{9,... | collective-permute-start | bytes 589832 | tf_op jit(solution)/shard_map/ppermute | solution.py:13
  61.1 16.9 %collective-permute-start.3 = (bf16[128,768]{1,0:T(8,128)(2,1)}, bf16[128,768]{1,0:T(8,128)(2,1)S(1)}, u32[]{:S(2)}, u32[]{:S(2)}) collective-permute-start(bf16[128,768]{1,0:T(8,128)(2,1)} %get-tuple-element.10), channel_id=1, source_target_pairs={{16,0},{17,1},{18,2},{19,3},{20,4},{21,5},{22,6},{23,7},{24,8},{25... | collective-permute-start | bytes 589832 | tf_op jit(solution)/shard_map/ppermute | solution.py:13
  70.0 9.0 %copy-start.4 = (bf16[128,768]{1,0:T(8,128)(2,1)S(1)}, bf16[128,768]{1,0:T(8,128)(2,1)}, u32[]{:S(2)}) copy-start(bf16[128,768]{1,0:T(8,128)(2,1)} %param.4) | copy-start | bytes 589828
  70.0 9.0 %copy-start.8 = (bf16[128,768]{1,0:T(8,128)(2,1)S(1)}, bf16[128,768]{1,0:T(8,128)(2,1)}, u32[]{:S(2)}) copy-start(bf16[128,768]{1,0:T(8,128)(2,1)} %copy-done.7) | copy-start | bytes 589828
  70.0 9.0 %copy-start.13 = (bf16[128,768]{1,0:T(8,128)(2,1)S(1)}, bf16[128,768]{1,0:T(8,128)(2,1)}, u32[]{:S(2)}) copy-start(bf16[128,768]{1,0:T(8,128)(2,1)} %copy-done.12) | copy-start | bytes 589828
Sparse Core Ops, SparseCore 0:
  59.6 199.4 all-reduce.2
where the time goes:
time: 270 us; the launch traced here: 268 us
  waiting for transfers between devices  192 us (71%)
  starting transfers between devices  29.2 us (11%)
  matrix products  14.4 us (5%)
  between operations  14.3 us (5%)
  local copies, waits for them, and re-layouts  13.5 us (5%)
  other arithmetic  4.51 us (2%)
    unnamed x2, waiting for transfers between devices  179 us
    ppermute x8, starting transfers between devices, from_behind(): return lax.ppermute(array, axis, pairs)  29.2 us
    ppermute x8, waiting for transfers between devices, from_behind(): return lax.ppermute(array, axis, pairs)  12.9 us
    another operation x1, local copies, waits for them, and re-layouts, kernel_terms(): return jnp.stack(grads, 0)  11 us
    dot_general x6, matrix products, cotangent_products(): jnp.einsum('bo,io->bi', moved_list[k], kernel[k], preferred_element_type=...  7.64 us
  transfers between devices with their start and end apart: 9, of which 6 were waited for; matrix products, arithmetic and copies ran while one was open for 5% of the time, Pallas kernels for 0%

commit v1 on v0

v1 whole, which is shorter than its diff:
```python
import jax
import jax.numpy as jnp
from jax import lax
from jax.sharding import PartitionSpec as P

DILATION_ONE = 256
DILATION_TWO = 2048
PLANE = 8


def moved(array, target):
    size = lax.axis_size("seq")
    pairs = [(i, target(i)) for i in range(size)]
    pairs = [(i, t) for i, t in pairs if t is not None and 0 <= t < size]
    return lax.ppermute(array, "seq", pairs)


def gelu_pair(values):
    wide = values.astype(jnp.float32)
    return jax.jvp(jax.nn.gelu, (wide,), (jnp.ones_like(wide),))


def dot(a, b):
    return jnp.dot(a, b, preferred_element_type=jnp.float32)


def dot_t(a, b):
    return jnp.einsum("bo,io->bi", a, b, preferred_element_type=jnp.float32)


def far_terms(values, taps, sign, product):
    size = lax.axis_size("seq")
    steps = DILATION_TWO // values.shape[0]
    if 2 * steps == size:
        other = moved(values, lambda i: i ^ steps)
        first = lax.axis_index("seq") < steps
        tap = jnp.where(first, 1 + sign, 1 - sign)
        return product(other, lax.dynamic_index_in_dim(taps, tap, 0, keepdims=False))
    behind = moved(values, lambda i: i + steps)
    ahead = moved(values, lambda i: i - steps)
    return product(behind, taps[1 - sign]) + product(ahead, taps[1 + sign])


def pick(stack, at):
    return lax.dynamic_index_in_dim(stack, at, 0, keepdims=False)


def local(features, first_taps, second_taps, upstream):
    size = lax.axis_size("seq")
    planes = size // PLANE
    rows, width = features.shape
    own_cols = width // size
    index = lax.axis_index("seq")
    plane, chip, core = index // PLANE, (index // 2) % 4, index % 2

    acts, slope_first = gelu_pair(features)
    acts = acts.astype(jnp.bfloat16)
    far_up = far_terms(upstream, second_taps, -1, dot_t)

    near = [acts] + [moved(acts, lambda i, s=s: i ^ (2 * s)) for s in (1, 3, 2)]
    near = jnp.stack([near[0], near[1], near[3], near[2]])
    edge = moved(acts, lambda i: {0: i - 2, 3: i + 2}.get((i // 2) % 4))
    acts_back = jnp.where(chip == 0, edge, pick(near, (chip - 1) % 4 ^ chip))
    acts_ahead = jnp.where(chip == 3, edge, pick(near, (chip + 1) % 4 ^ chip))

    conv = dot(acts, first_taps[1]) + dot(acts_back, first_taps[0]) + dot(acts_ahead, first_taps[2])
    output_first = (features.astype(jnp.float32) + conv).astype(jnp.bfloat16)
    acts_second, slope_second = gelu_pair(output_first)
    acts_second = acts_second.astype(jnp.bfloat16)

    back = dot_t(upstream, second_taps[1]) + far_up
    middle = (upstream.astype(jnp.float32) + slope_second * back).astype(jnp.bfloat16)

    turned = middle.T.reshape(planes, 4, 2, own_cols, rows).transpose(1, 2, 0, 3, 4)
    parts = [pick(turned, chip ^ s) for s in range(4)]
    parts = [parts[0]] + [moved(parts[s], lambda i, s=s: i ^ (2 * s)) for s in (1, 2, 3)]
    parts = jnp.stack(parts)
    other_cols = moved(lax.dynamic_index_in_dim(parts, 1 - core, 1, keepdims=False), lambda i: i ^ 1)
    own_parts = lax.dynamic_index_in_dim(parts, core, 1, keepdims=False)

    ordered = [pick(near, s ^ chip) for s in range(4)]
    halo_back = moved(ordered[3], lambda i: i + PLANE)
    halo_ahead = moved(ordered[0], lambda i: i - PLANE)
    line = jnp.concatenate([halo_back] + ordered + [halo_ahead])
    other_line = moved(line, lambda i: i ^ 1)

    def side(cols):
        ordered_cols = [pick(cols, s ^ chip).reshape(-1, rows) for s in range(4)]
        return jnp.concatenate(ordered_cols, 1)

    own_side, other_side = side(own_parts), side(other_cols)
    terms = []
    for k in range(3):
        span = slice(k * rows, (k + 4) * rows)
        terms.append(dot(own_side, line[span]) + dot(other_side, other_line[span]))
    terms = jnp.stack(terms).reshape(3, planes, own_cols, width)

    if planes == 4:
        total = lax.dynamic_index_in_dim(terms, plane, 1, keepdims=False)
        for s in (3, 2, 1):
            piece = lax.dynamic_index_in_dim(terms, plane ^ s, 1, keepdims=False)
            got = moved(piece.astype(jnp.bfloat16), lambda i, s=s: i ^ (PLANE * s))
            total = total + got.astype(jnp.float32)
    else:
        lines = [list(range(r, size, PLANE)) for r in range(PLANE)]
        total = lax.psum_scatter(terms, "seq", scatter_dimension=1, axis_index_groups=lines)
    first_taps_gradient = jnp.swapaxes(total, 1, 2)

    conv_second = dot(acts_second, second_taps[1]) + far_terms(acts_second, second_taps, 1, dot)
    second_layer_output = (output_first.astype(jnp.float32) + conv_second).astype(jnp.bfloat16)

    behind = moved(middle, lambda i: i + 2)
    ahead = moved(middle, lambda i: i - 2)
    back_first = (
        dot_t(middle, first_taps[1]) + dot_t(ahead, first_taps[0]) + dot_t(behind, first_taps[2])
    )
    input_gradient = (middle.astype(jnp.float32) + slope_first * back_first).astype(jnp.bfloat16)
    return second_layer_output, input_gradient, first_taps_gradient


def solution(mesh):
    placed = (P(("groups", "seq"), None), P(), P(), P(("groups", "seq"), None))
    return jax.shard_map(
        local,
        mesh=mesh,
        in_specs=placed,
        out_specs=(
            P(("groups", "seq"), None),
            P(("groups", "seq"), None),
            P(None, "groups", "seq"),
        ),
        check_vma=False,
    )
```

time: 270 us -> 81.5 us (0.30)
  the two profiles are of different devices: /device:TPU:16 before, /device:TPU:0 now
where the time goes in v1:
time: 81.5 us; the launch traced here: 81.1 us
  starting transfers between devices  35.7 us (44%)
  waiting for transfers between devices  25 us (31%)
  matrix products  16.7 us (20%)
  other arithmetic  2.2 us (3%)
  between operations  1 us (1%)
    ppermute x18, starting transfers between devices, moved(): return lax.ppermute(array, 'seq', pairs)  35.7 us
    ppermute x18, waiting for transfers between devices, moved(): return lax.ppermute(array, 'seq', pairs)  25 us
    dot_general x11, matrix products, dot(): return jnp.dot(a, b, preferred_element_type=jnp.float32)  10.6 us
    dot_general x5, matrix products, dot_t(): return jnp.einsum('bo,io->bi', a, b, preferred_element_type=jnp.float32)  6.12 us
  transfers between devices with their start and end apart: 18, of which 6 were waited for; matrix products, arithmetic and copies ran while one was open for 22% of the time, Pallas kernels for 0%

profile of v1, /device:TPU:0, one launch (start us, length us, event | category | flops | bytes accessed | tf_op | source)
XLA Modules:
  0.0 81.1 jit_solution(14340781105205646214)
XLA Ops:
  0.6 1.1 %fusion.87 = bf16[128,768]{1,0:T(8,128)(2,1)S(1)} fusion(bf16[128,768]{1,0:T(8,128)(2,1)} %param.4), kind=kLoop, calls=%fused_computation.97 | loop fusion | flops 983040 | bytes 393216 | tf_op jit(solution)/shard_map/convert_element_type | solution.py:57
  1.8 3.0 %collective-permute-start.1 = (bf16[128,768]{1,0:T(8,128)(2,1)S(1)}, bf16[128,768]{1,0:T(8,128)(2,1)S(1)}, u32[]{:S(2)}, u32[]{:S(2)}) collective-permute-start(bf16[128,768]{1,0:T(8,128)(2,1)S(1)} %fusion.87), channel_id=1, source_target_pairs={{0,2},{1,3},{2,0},{3,1},{4,6},{5,7},{6,4},{7,5},{8,10},{9,11},{10,... | collective-permute-start | bytes 589832 | tf_op jit(solution)/shard_map/ppermute | solution.py:15
  4.8 1.5 %collective-permute-start.3 = (bf16[128,768]{1,0:T(8,128)(2,1)S(1)}, bf16[128,768]{1,0:T(8,128)(2,1)S(1)}, u32[]{:S(2)}, u32[]{:S(2)}) collective-permute-start(bf16[128,768]{1,0:T(8,128)(2,1)S(1)} %fusion.87), channel_id=1, source_target_pairs={{0,6},{1,7},{2,4},{3,5},{4,2},{5,3},{6,0},{7,1},{8,14},{9,15},{10,... | collective-permute-start | bytes 589832 | tf_op jit(solution)/shard_map/ppermute | solution.py:15
  6.3 0.7 collective-permute-start
  7.1 5.2 %collective-permute-start.5 = (bf16[128,768]{1,0:T(8,128)(2,1)}, bf16[128,768]{1,0:T(8,128)(2,1)S(1)}, u32[]{:S(2)}, u32[]{:S(2)}) collective-permute-start(bf16[128,768]{1,0:T(8,128)(2,1)} %param.7), channel_id=1, source_target_pairs={{0,16},{1,17},{2,18},{3,19},{4,20},{5,21},{6,22},{7,23},{8,24},{9,... | collective-permute-start | bytes 589832 | tf_op jit(solution)/shard_map/ppermute | solution.py:15
  12.2 1.9 %fusion.8 = f32[128,768]{1,0:T(8,128)S(1)} fusion(bf16[128,768]{1,0:T(8,128)(2,1)} %param.7, bf16[3,768,768]{2,1,0:T(8,128)(2,1)} %param.6), kind=kOutput, calls=%fused_computation.14 | convolution fusion | flops 150994944 | bytes 1769472 | tf_op jit(solution)/shard_map/bo,io->bi/dot_general | solution.py:28
  14.1 1.6 %fusion.18 = f32[128,768]{1,0:T(8,128)S(1)} fusion(bf16[3,768,768]{2,1,0:T(8,128)(2,1)} %param.5, bf16[128,768]{1,0:T(8,128)(2,1)S(1)} %copy-done.1), kind=kOutput, calls=%fused_computation.24 | convolution fusion | flops 151977984 | bytes 1769472 | tf_op jit(solution)/shard_map/dot_general | solution.py:24
  16.0 1.4 %collective-permute-done.3 = bf16[128,768]{1,0:T(8,128)(2,1)S(1)} collective-permute-done((bf16[128,768]{1,0:T(8,128)(2,1)S(1)}, bf16[128,768]{1,0:T(8,128)(2,1)S(1)}, u32[]{:S(2)}, u32[]{:S(2)}) %collective-permute-start.3) | collective-permute-done | bytes 196640 | tf_op jit(solution)/shard_map/ppermute | solution.py:15
  17.5 9.2 %collective-permute-start.11 = (bf16[128,768]{1,0:T(8,128)(2,1)S(1)}, bf16[128,768]{1,0:T(8,128)(2,1)S(1)}, u32[]{:S(2)}, u32[]{:S(2)}) collective-permute-start(bf16[128,768]{1,0:T(8,128)(2,1)S(1)} %dynamic-slice_bitcast_fusion.3), channel_id=1, source_target_pairs={{0,8},{1,9},{2,10},{3,11},{4,12},{5,13},{6,14},{7,15},{8,16},{9,17... | collective-permute-start | bytes 589832 | tf_op jit(solution)/shard_map/ppermute | solution.py:15
  26.7 1.6 %convolution_add_fusion.4 = f32[128,768]{1,0:T(8,128)S(1)} fusion(f32[128,768]{1,0:T(8,128)S(1)} %fusion.18, bf16[3,768,768]{2,1,0:T(8,128)(2,1)} %param.5, bf16[128,768]{1,0:T(8,128)(2,1)S(1)} %collective-permute-done, bf16[4,128,768]{2,1,0:T(8,128)(2,1)S(1)} %pad_maximum_fusion.1, s32[]{:T(128)S(6)} %select_n.117, pred[]{:T(512)S(6)} %eq.11), kind=kOutput, calls=%fused_computation.6 | convolution fusion | flops 151191552 | bytes 2359301 | tf_op jit(solution)/shard_map/dot_general | solution.py:24
  28.3 1.7 %multiply_convert_fusion = (bf16[128,768]{1,0:T(8,128)(2,1)S(1)}, f32[128,768]{1,0:T(8,128)S(1)}) fusion(f32[128,768]{1,0:T(8,128)S(1)} %convolution_add_fusion.4, bf16[3,768,768]{2,1,0:T(8,128)(2,1)} %param.5, bf16[128,768]{1,0:T(8,128)(2,1)S(1)} %collective-permute-done, bf16[4,128,768]{2,1,0:T(8,128)(2,1)S(1)} %pad_maximum_fusion.1, s32[]{:T(128)S(6)} %select_n.121, ...), kind=kOutput, calls=%fused_computation.100 | convolution fusion | flops 152469504 | bytes 2752517 | tf_op jit(solution)/shard_map/dot_general | solution.py:24
  30.1 1.9 %fusion.28 = bf16[128,768]{1,0:T(8,128)(2,1)S(1)} fusion(f32[128,768]{1,0:T(8,128)S(1)} %fusion.8, bf16[128,768]{1,0:T(8,128)(2,1)S(1)} %collective-permute-done.5, bf16[3,768,768]{2,1,0:T(8,128)(2,1)} %param.6, s32[]{:T(128)S(6)} %select_n.124, f32[128,768]{1,0:T(8,128)S(1)} %get-tuple-element.25, bf16[128,768]{1,0:T(8,128)(2,1)S(1)} %copy-done.2), kind=kOutput, calls=%fused_computation.30 | convolution fusion | flops 153059328 | bytes 2555908 | tf_op jit(solution)/shard_map/bo,io->bi/dot_general | solution.py:28
  32.2 1.9 %collective-permute-start.10 = (bf16[2,4,24,128]{3,2,0,1:T(8,128)(2,1)S(1)}, bf16[2,4,24,128]{3,2,0,1:T(8,128)(2,1)S(1)}, u32[]{:S(2)}, u32[]{:S(2)}) collective-permute-start(bf16[2,4,24,128]{3,2,0,1:T(8,128)(2,1)S(1)} %get-tuple-element.18), channel_id=1, source_target_pairs={{0,6},{1,7},{2,4},{3,5},{4,2},{5,3},{6,0},{7,1},{8,14},{9,15},{10,... | collective-permute-start | bytes 147464 | tf_op jit(solution)/shard_map/ppermute | solution.py:15
  34.1 1.6 %collective-permute-start.9 = (bf16[2,4,24,128]{3,2,0,1:T(8,128)(2,1)S(1)}, bf16[2,4,24,128]{3,2,0,1:T(8,128)(2,1)S(1)}, u32[]{:S(2)}, u32[]{:S(2)}) collective-permute-start(bf16[2,4,24,128]{3,2,0,1:T(8,128)(2,1)S(1)} %get-tuple-element.19), channel_id=1, source_target_pairs={{0,4},{1,5},{2,6},{3,7},{4,0},{5,1},{6,2},{7,3},{8,12},{9,13},{10,... | collective-permute-start | bytes 147464 | tf_op jit(solution)/shard_map/ppermute | solution.py:15
  35.7 2.6 %collective-permute-start.4 = (bf16[128,768]{1,0:T(8,128)(2,1)S(1)}, bf16[128,768]{1,0:T(8,128)(2,1)S(1)}, u32[]{:S(2)}, u32[]{:S(2)}) collective-permute-start(bf16[128,768]{1,0:T(8,128)(2,1)S(1)} %get-tuple-element.24), channel_id=1, source_target_pairs={{0,16},{1,17},{2,18},{3,19},{4,20},{5,21},{6,22},{7,23},{8,24},{9,... | collective-permute-start | bytes 589832 | tf_op jit(solution)/shard_map/ppermute | solution.py:15
  38.3 1.7 %fusion.10 = f32[128,768]{1,0:T(8,128)S(1)} fusion(bf16[128,768]{1,0:T(8,128)(2,1)S(1)} %get-tuple-element.24, bf16[3,768,768]{2,1,0:T(8,128)(2,1)} %param.6), kind=kOutput, calls=%fused_computation.16 | convolution fusion | flops 150994944 | bytes 1769472 | tf_op jit(solution)/shard_map/dot_general | solution.py:24
  40.2 1.3 %collective-permute-start.13 = (bf16[128,768]{1,0:T(8,128)(2,1)S(1)}, bf16[128,768]{1,0:T(8,128)(2,1)S(1)}, u32[]{:S(2)}, u32[]{:S(2)}) collective-permute-start(bf16[128,768]{1,0:T(8,128)(2,1)S(1)} %get-tuple-element.8), channel_id=1, source_target_pairs={{8,0},{9,1},{10,2},{11,3},{12,4},{13,5},{14,6},{15,7},{16,8},{17,9... | collective-permute-start | bytes 589832 | tf_op jit(solution)/shard_map/ppermute | solution.py:15
  41.5 8.3 %collective-permute-done.13 = bf16[128,768]{1,0:T(8,128)(2,1)S(1)} collective-permute-done((bf16[128,768]{1,0:T(8,128)(2,1)S(1)}, bf16[128,768]{1,0:T(8,128)(2,1)S(1)}, u32[]{:S(2)}, u32[]{:S(2)}) %collective-permute-start.13) | collective-permute-done | bytes 196640 | tf_op jit(solution)/shard_map/ppermute | solution.py:15
  49.9 0.5 fusion.16
  50.5 2.6 %collective-permute-start.7 = (bf16[128,768]{1,0:T(8,128)(2,1)S(1)}, bf16[128,768]{1,0:T(8,128)(2,1)S(1)}, u32[]{:S(2)}, u32[]{:S(2)}) collective-permute-start(bf16[128,768]{1,0:T(8,128)(2,1)S(1)} %fusion.28), channel_id=1, source_target_pairs={{0,2},{1,3},{2,4},{3,5},{4,6},{5,7},{6,8},{7,9},{8,10},{9,11},{10,... | collective-permute-start | bytes 589832 | tf_op jit(solution)/shard_map/ppermute | solution.py:15
  53.1 1.3 %collective-permute-start.6 = (bf16[128,768]{1,0:T(8,128)(2,1)S(1)}, bf16[128,768]{1,0:T(8,128)(2,1)S(1)}, u32[]{:S(2)}, u32[]{:S(2)}) collective-permute-start(bf16[128,768]{1,0:T(8,128)(2,1)S(1)} %fusion.28), channel_id=1, source_target_pairs={{2,0},{3,1},{4,2},{5,3},{6,4},{7,5},{8,6},{9,7},{10,8},{11,9},{12,... | collective-permute-start | bytes 589832 | tf_op jit(solution)/shard_map/ppermute | solution.py:15
  54.5 0.3 collective-permute-start.12
  54.8 1.1 %collective-permute-done.12 = bf16[4,4,24,128]{3,2,1,0:T(8,128)(2,1)S(1)} collective-permute-done((bf16[4,4,24,128]{3,2,1,0:T(8,128)(2,1)S(1)}, bf16[4,4,24,128]{3,2,1,0:T(8,128)(2,1)S(1)}, u32[]{:S(2)}, u32[]{:S(2)}) %collective-permute-start.12) | collective-permute-done | bytes 98336 | tf_op jit(solution)/shard_map/ppermute | solution.py:15
  55.9 8.1 %collective-permute-done.6 = bf16[128,768]{1,0:T(8,128)(2,1)S(1)} collective-permute-done((bf16[128,768]{1,0:T(8,128)(2,1)S(1)}, bf16[128,768]{1,0:T(8,128)(2,1)S(1)}, u32[]{:S(2)}, u32[]{:S(2)}) %collective-permute-start.6) | collective-permute-done | bytes 196640 | tf_op jit(solution)/shard_map/ppermute | solution.py:15
  64.0 0.5 convolution_add_fusion.1
  64.8 1.3 %add_convert_fusion = bf16[128,768]{1,0:T(8,128)(2,1)} fusion(bf16[128,768]{1,0:T(8,128)(2,1)S(1)} %fusion.28, f32[128,768]{1,0:T(8,128)S(1)} %convolution_add_fusion.1, bf16[128,768]{1,0:T(8,128)(2,1)S(1)} %collective-permute-done.7, bf16[3,768,768]{2,1,0:T(8,128)(2,1)S(1)} %copy-done, bf16[128,768]{1,0:T(8,128)(2,1)S(1)} %copy-done.1), kind=kOutput, calls=%fused_computation.99 | convolution fusion | flops 153157632 | bytes 2359296 | tf_op jit(solution)/shard_map/bo,io->bi/dot_general | solution.py:28
  67.6 1.7 %collective-permute-start.17 = (bf16[3,24,768]{2,1,0:T(8,128)(2,1)S(1)}, bf16[3,24,768]{2,1,0:T(8,128)(2,1)S(1)}, u32[]{:S(2)}, u32[]{:S(2)}) collective-permute-start(bf16[3,24,768]{2,1,0:T(8,128)(2,1)S(1)} %get-tuple-element.10), channel_id=1, source_target_pairs={{0,8},{1,9},{2,10},{3,11},{4,12},{5,13},{6,14},{7,15},{8,0},{9,1},... | collective-permute-start | bytes 331784 | tf_op jit(solution)/shard_map/ppermute | solution.py:15
  69.2 2.7 %collective-permute-start.16 = (bf16[3,24,768]{2,1,0:T(8,128)(2,1)S(1)}, bf16[3,24,768]{2,1,0:T(8,128)(2,1)S(1)}, u32[]{:S(2)}, u32[]{:S(2)}) collective-permute-start(bf16[3,24,768]{2,1,0:T(8,128)(2,1)S(1)} %get-tuple-element.11), channel_id=1, source_target_pairs={{0,16},{1,17},{2,18},{3,19},{4,20},{5,21},{6,22},{7,23},{8,24},{9,... | collective-permute-start | bytes 331784 | tf_op jit(solution)/shard_map/ppermute | solution.py:15
  71.9 2.3 %fusion.31 = bf16[128,768]{1,0:T(8,128)(2,1)} fusion(f32[128,768]{1,0:T(8,128)S(1)} %get-tuple-element.25, f32[128,768]{1,0:T(8,128)S(1)} %fusion.10, bf16[128,768]{1,0:T(8,128)(2,1)S(1)} %collective-permute-done.4, bf16[3,768,768]{2,1,0:T(8,128)(2,1)} %param.6, s32[]{:T(128)S(6)} %select_n.123), kind=kOutput, calls=%fused_computation.31 | convolution fusion | flops 151289856 | bytes 2359300 | tf_op jit(solution)/shard_map/dot_general | solution.py:24
  74.2 1.1 %collective-permute-done.15 = bf16[3,24,768]{2,1,0:T(8,128)(2,1)S(1)} collective-permute-done((bf16[3,24,768]{2,1,0:T(8,128)(2,1)S(1)}, bf16[3,24,768]{2,1,0:T(8,128)(2,1)S(1)}, u32[]{:S(2)}, u32[]{:S(2)}) %collective-permute-start.15) | collective-permute-done | bytes 110624 | tf_op jit(solution)/shard_map/ppermute | solution.py:15
  75.3 5.1 %collective-permute-done.16 = bf16[3,24,768]{2,1,0:T(8,128)(2,1)S(1)} collective-permute-done((bf16[3,24,768]{2,1,0:T(8,128)(2,1)S(1)}, bf16[3,24,768]{2,1,0:T(8,128)(2,1)S(1)}, u32[]{:S(2)}, u32[]{:S(2)}) %collective-permute-start.16) | collective-permute-done | bytes 110624 | tf_op jit(solution)/shard_map/ppermute | solution.py:15
  80.4 0.7 fusion.93
  (45 shorter events, 2.8 us)
Async XLA Ops:
  0.6 13.5 %copy-start.1 = (bf16[128,768]{1,0:T(8,128)(2,1)S(1)}, bf16[128,768]{1,0:T(8,128)(2,1)}, u32[]{:S(2)}) copy-start(bf16[128,768]{1,0:T(8,128)(2,1)} %param.4) | copy-start | bytes 589828
  1.8 14.2 %collective-permute-start.1 = (bf16[128,768]{1,0:T(8,128)(2,1)S(1)}, bf16[128,768]{1,0:T(8,128)(2,1)S(1)}, u32[]{:S(2)}, u32[]{:S(2)}) collective-permute-start(bf16[128,768]{1,0:T(8,128)(2,1)S(1)} %fusion.87), channel_id=1, source_target_pairs={{0,2},{1,3},{2,0},{3,1},{4,6},{5,7},{6,4},{7,5},{8,10},{9,11},{10,... | collective-permute-start | bytes 589832 | tf_op jit(solution)/shard_map/ppermute | solution.py:15
  4.8 12.6 %collective-permute-start.3 = (bf16[128,768]{1,0:T(8,128)(2,1)S(1)}, bf16[128,768]{1,0:T(8,128)(2,1)S(1)}, u32[]{:S(2)}, u32[]{:S(2)}) collective-permute-start(bf16[128,768]{1,0:T(8,128)(2,1)S(1)} %fusion.87), channel_id=1, source_target_pairs={{0,6},{1,7},{2,4},{3,5},{4,2},{5,3},{6,0},{7,1},{8,14},{9,15},{10,... | collective-permute-start | bytes 589832 | tf_op jit(solution)/shard_map/ppermute | solution.py:15
  6.3 20.4 %collective-permute-start = (bf16[128,768]{1,0:T(8,128)(2,1)S(1)}, bf16[128,768]{1,0:T(8,128)(2,1)S(1)}, u32[]{:S(2)}, u32[]{:S(2)}) collective-permute-start(bf16[128,768]{1,0:T(8,128)(2,1)S(1)} %fusion.87), channel_id=1, source_target_pairs={{6,8},{7,9},{8,6},{9,7},{14,16},{15,17},{16,14},{17,15},{22,24},{2... | collective-permute-start | bytes 589832 | tf_op jit(solution)/shard_map/ppermute | solution.py:15
  6.9 10.5 %collective-permute-start.2 = (bf16[128,768]{1,0:T(8,128)(2,1)S(1)}, bf16[128,768]{1,0:T(8,128)(2,1)S(1)}, u32[]{:S(2)}, u32[]{:S(2)}) collective-permute-start(bf16[128,768]{1,0:T(8,128)(2,1)S(1)} %fusion.87), channel_id=1, source_target_pairs={{0,4},{1,5},{2,6},{3,7},{4,0},{5,1},{6,2},{7,3},{8,12},{9,13},{10,... | collective-permute-start | bytes 589832 | tf_op jit(solution)/shard_map/ppermute | solution.py:15
  7.1 23.0 %collective-permute-start.5 = (bf16[128,768]{1,0:T(8,128)(2,1)}, bf16[128,768]{1,0:T(8,128)(2,1)S(1)}, u32[]{:S(2)}, u32[]{:S(2)}) collective-permute-start(bf16[128,768]{1,0:T(8,128)(2,1)} %param.7), channel_id=1, source_target_pairs={{0,16},{1,17},{2,18},{3,19},{4,20},{5,21},{6,22},{7,23},{8,24},{9,... | collective-permute-start | bytes 589832 | tf_op jit(solution)/shard_map/ppermute | solution.py:15
  17.5 22.5 %collective-permute-start.11 = (bf16[128,768]{1,0:T(8,128)(2,1)S(1)}, bf16[128,768]{1,0:T(8,128)(2,1)S(1)}, u32[]{:S(2)}, u32[]{:S(2)}) collective-permute-start(bf16[128,768]{1,0:T(8,128)(2,1)S(1)} %dynamic-slice_bitcast_fusion.3), channel_id=1, source_target_pairs={{0,8},{1,9},{2,10},{3,11},{4,12},{5,13},{6,14},{7,15},{8,16},{9,17... | collective-permute-start | bytes 589832 | tf_op jit(solution)/shard_map/ppermute | solution.py:15
  28.3 1.7 %copy-start.2 = (bf16[128,768]{1,0:T(8,128)(2,1)S(1)}, bf16[128,768]{1,0:T(8,128)(2,1)}, u32[]{:S(2)}) copy-start(bf16[128,768]{1,0:T(8,128)(2,1)} %param.7) | copy-start | bytes 589828
  32.2 18.3 %collective-permute-start.8 = (bf16[2,4,24,128]{3,2,0,1:T(8,128)(2,1)S(1)}, bf16[2,4,24,128]{3,2,0,1:T(8,128)(2,1)S(1)}, u32[]{:S(2)}, u32[]{:S(2)}) collective-permute-start(bf16[2,4,24,128]{3,2,0,1:T(8,128)(2,1)S(1)} %get-tuple-element.17), channel_id=1, source_target_pairs={{0,2},{1,3},{2,0},{3,1},{4,6},{5,7},{6,4},{7,5},{8,10},{9,11},{10,... | collective-permute-start | bytes 147464 | tf_op jit(solution)/shard_map/ppermute | solution.py:15
  32.2 20.9 %collective-permute-start.10 = (bf16[2,4,24,128]{3,2,0,1:T(8,128)(2,1)S(1)}, bf16[2,4,24,128]{3,2,0,1:T(8,128)(2,1)S(1)}, u32[]{:S(2)}, u32[]{:S(2)}) collective-permute-start(bf16[2,4,24,128]{3,2,0,1:T(8,128)(2,1)S(1)} %get-tuple-element.18), channel_id=1, source_target_pairs={{0,6},{1,7},{2,4},{3,5},{4,2},{5,3},{6,0},{7,1},{8,14},{9,15},{10,... | collective-permute-start | bytes 147464 | tf_op jit(solution)/shard_map/ppermute | solution.py:15
  34.1 20.3 %collective-permute-start.9 = (bf16[2,4,24,128]{3,2,0,1:T(8,128)(2,1)S(1)}, bf16[2,4,24,128]{3,2,0,1:T(8,128)(2,1)S(1)}, u32[]{:S(2)}, u32[]{:S(2)}) collective-permute-start(bf16[2,4,24,128]{3,2,0,1:T(8,128)(2,1)S(1)} %get-tuple-element.19), channel_id=1, source_target_pairs={{0,4},{1,5},{2,6},{3,7},{4,0},{5,1},{6,2},{7,3},{8,12},{9,13},{10,... | collective-permute-start | bytes 147464 | tf_op jit(solution)/shard_map/ppermute | solution.py:15
  35.7 36.2 %collective-permute-start.4 = (bf16[128,768]{1,0:T(8,128)(2,1)S(1)}, bf16[128,768]{1,0:T(8,128)(2,1)S(1)}, u32[]{:S(2)}, u32[]{:S(2)}) collective-permute-start(bf16[128,768]{1,0:T(8,128)(2,1)S(1)} %get-tuple-element.24), channel_id=1, source_target_pairs={{0,16},{1,17},{2,18},{3,19},{4,20},{5,21},{6,22},{7,23},{8,24},{9,... | collective-permute-start | bytes 589832 | tf_op jit(solution)/shard_map/ppermute | solution.py:15
  38.3 11.6 %copy-start = (bf16[3,768,768]{2,1,0:T(8,128)(2,1)S(1)}, bf16[3,768,768]{2,1,0:T(8,128)(2,1)}, u32[]{:S(2)}) copy-start(bf16[3,768,768]{2,1,0:T(8,128)(2,1)} %param.5) | copy-start | bytes 10616836
  40.2 9.7 %collective-permute-start.13 = (bf16[128,768]{1,0:T(8,128)(2,1)S(1)}, bf16[128,768]{1,0:T(8,128)(2,1)S(1)}, u32[]{:S(2)}, u32[]{:S(2)}) collective-permute-start(bf16[128,768]{1,0:T(8,128)(2,1)S(1)} %get-tuple-element.8), channel_id=1, source_target_pairs={{8,0},{9,1},{10,2},{11,3},{12,4},{13,5},{14,6},{15,7},{16,8},{17,9... | collective-permute-start | bytes 589832 | tf_op jit(solution)/shard_map/ppermute | solution.py:15
  49.8 16.2 %collective-permute-start.14 = (bf16[768,768]{1,0:T(8,128)(2,1)S(1)}, bf16[768,768]{1,0:T(8,128)(2,1)S(1)}, u32[]{:S(2)}, u32[]{:S(2)}) collective-permute-start(bf16[768,768]{1,0:T(8,128)(2,1)S(1)} %constant_dynamic-update-slice_fusion), channel_id=1, source_target_pairs={{0,1},{1,0},{2,3},{3,2},{4,5},{5,4},{6,7},{7,6},{8,9},{9,8},{10,11... | collective-permute-start | bytes 3538952 | tf_op jit(solution)/shard_map/ppermute | solution.py:15
  50.5 14.3 %collective-permute-start.7 = (bf16[128,768]{1,0:T(8,128)(2,1)S(1)}, bf16[128,768]{1,0:T(8,128)(2,1)S(1)}, u32[]{:S(2)}, u32[]{:S(2)}) collective-permute-start(bf16[128,768]{1,0:T(8,128)(2,1)S(1)} %fusion.28), channel_id=1, source_target_pairs={{0,2},{1,3},{2,4},{3,5},{4,6},{5,7},{6,8},{7,9},{8,10},{9,11},{10,... | collective-permute-start | bytes 589832 | tf_op jit(solution)/shard_map/ppermute | solution.py:15
  53.1 10.8 %collective-permute-start.6 = (bf16[128,768]{1,0:T(8,128)(2,1)S(1)}, bf16[128,768]{1,0:T(8,128)(2,1)S(1)}, u32[]{:S(2)}, u32[]{:S(2)}) collective-permute-start(bf16[128,768]{1,0:T(8,128)(2,1)S(1)} %fusion.28), channel_id=1, source_target_pairs={{2,0},{3,1},{4,2},{5,3},{6,4},{7,5},{8,6},{9,7},{10,8},{11,9},{12,... | collective-permute-start | bytes 589832 | tf_op jit(solution)/shard_map/ppermute | solution.py:15
  54.5 1.4 %collective-permute-start.12 = (bf16[4,4,24,128]{3,2,1,0:T(8,128)(2,1)S(1)}, bf16[4,4,24,128]{3,2,1,0:T(8,128)(2,1)S(1)}, u32[]{:S(2)}, u32[]{:S(2)}) collective-permute-start(bf16[4,4,24,128]{3,2,1,0:T(8,128)(2,1)S(1)} %dynamic-slice_bitcast_fusion.4), channel_id=1, source_target_pairs={{0,1},{1,0},{2,3},{3,2},{4,5},{5,4},{6,7},{7,6},{8,9},{9,8},{10,11... | collective-permute-start | bytes 294920 | tf_op jit(solution)/shard_map/ppermute | solution.py:15
  67.5 7.8 %collective-permute-start.15 = (bf16[3,24,768]{2,1,0:T(8,128)(2,1)S(1)}, bf16[3,24,768]{2,1,0:T(8,128)(2,1)S(1)}, u32[]{:S(2)}, u32[]{:S(2)}) collective-permute-start(bf16[3,24,768]{2,1,0:T(8,128)(2,1)S(1)} %get-tuple-element.9), channel_id=1, source_target_pairs={{0,24},{1,25},{2,26},{3,27},{4,28},{5,29},{6,30},{7,31},{8,16},{9,... | collective-permute-start | bytes 331784 | tf_op jit(solution)/shard_map/ppermute | solution.py:15
  67.6 7.7 %collective-permute-start.17 = (bf16[3,24,768]{2,1,0:T(8,128)(2,1)S(1)}, bf16[3,24,768]{2,1,0:T(8,128)(2,1)S(1)}, u32[]{:S(2)}, u32[]{:S(2)}) collective-permute-start(bf16[3,24,768]{2,1,0:T(8,128)(2,1)S(1)} %get-tuple-element.10), channel_id=1, source_target_pairs={{0,8},{1,9},{2,10},{3,11},{4,12},{5,13},{6,14},{7,15},{8,0},{9,1},... | collective-permute-start | bytes 331784 | tf_op jit(solution)/shard_map/ppermute | solution.py:15
  69.2 11.1 %collective-permute-start.16 = (bf16[3,24,768]{2,1,0:T(8,128)(2,1)S(1)}, bf16[3,24,768]{2,1,0:T(8,128)(2,1)S(1)}, u32[]{:S(2)}, u32[]{:S(2)}) collective-permute-start(bf16[3,24,768]{2,1,0:T(8,128)(2,1)S(1)} %get-tuple-element.11), channel_id=1, source_target_pairs={{0,16},{1,17},{2,18},{3,19},{4,20},{5,21},{6,22},{7,23},{8,24},{9,... | collective-permute-start | bytes 331784 | tf_op jit(solution)/shard_map/ppermute | solution.py:15

commit v2 on v1

v2 whole, which is shorter than its diff:
```python
import functools

import jax
import jax.numpy as jnp
from jax import lax
from jax.experimental import pallas as pl
from jax.experimental.pallas import tpu as pltpu
from jax.sharding import PartitionSpec as P

DILATION_ONE = 256
DILATION_TWO = 2048
PLANE = 8
LIMIT = 8 * 2**20
F32 = jnp.float32
BF16 = jnp.bfloat16


def moved(array, target):
    size = lax.axis_size("seq")
    pairs = [(i, target(i)) for i in range(size)]
    pairs = [(i, t) for i, t in pairs if t is not None and 0 <= t < size]
    return lax.ppermute(array, "seq", pairs)


def after(value, *first):
    return lax.optimization_barrier((value, *first))[0]


def gelu_pair(values):
    wide = values.astype(F32)
    return jax.jvp(jax.nn.gelu, (wide,), (jnp.ones_like(wide),))


def dot(a, b):
    return jnp.dot(a, b, preferred_element_type=F32)


def dot_t(a, b):
    return lax.dot_general(a, b, (((1,), (1,)), ((), ())), preferred_element_type=F32)


def call(body, name, outs, *arrays, scratch=()):
    vmem = pl.BlockSpec(memory_space=pltpu.VMEM)
    return pl.pallas_call(
        body,
        name=name,
        out_shape=[jax.ShapeDtypeStruct(shape, kind) for shape, kind in outs],
        in_specs=[vmem] * len(arrays),
        out_specs=[vmem] * len(outs),
        scratch_shapes=list(scratch),
        compiler_params=pltpu.CompilerParams(vmem_limit_bytes=LIMIT),
    )(*arrays)


def position(rows):
    index = lax.axis_index("seq")
    lower = (index < DILATION_TWO // rows).astype(jnp.int32)
    return (index >> 1) & 3, index & 1, index >> 3, lower


def center_body(features, acts, up, taps, second_taps, conv, back, slope):
    conv[...] = features[...].astype(F32) + dot(acts[...], taps[1])
    back[...] = dot_t(up[...], second_taps[1])
    slope[...] = gelu_pair(features[...])[1]


def line_body(acts, flip, turn, cross, line, line_first, line_last):
    rows = acts.shape[0]
    chip = position(rows)[0]
    for slot, piece in enumerate((acts, flip, cross, turn)):
        value = piece[...]
        line[pl.ds((chip ^ slot) * rows, rows)] = value

        @pl.when(chip == slot)
        def _():
            line_first[...] = value

        @pl.when(chip == (slot ^ 3))
        def _():
            line_last[...] = value


def middle_body(far, *refs, planes):
    *others, line, edge, conv, up, back, taps, second_taps = refs[:-9]
    output, acts_second, middle, own, one, two, three, turned, near = refs[-9:]
    rows = edge.shape[0]
    chip, own_core, _, first = position(rows)
    near[0] = line[pl.ds(jnp.maximum(chip - 1, 0) * rows, rows)]
    near[1] = line[pl.ds(jnp.minimum(chip + 1, 3) * rows, rows)]

    @pl.when(chip == 0)
    def _():
        near[0] = edge[...]

    @pl.when(chip == 3)
    def _():
        near[1] = edge[...]

    result = (conv[...] + dot(near[0], taps[0]) + dot(near[1], taps[2])).astype(BF16)
    output[...] = result
    activated, slope = gelu_pair(result)
    acts_second[...] = activated.astype(BF16)
    total = back[...]
    if others:
        total = total + dot_t(others[0][...], second_taps[0]) + dot_t(far[...], second_taps[2])
    else:
        total = total + dot_t(far[...], second_taps[2 - 2 * first])
    value = (up[...].astype(F32) + slope * total).astype(BF16)
    middle[...] = value
    flat = value.astype(F32).T
    own_cols = turned.shape[1] // planes
    for z in range(planes):
        for owner in range(PLANE):
            start = (z * PLANE + owner) * own_cols
            turned[owner, z * own_cols : (z + 1) * own_cols] = flat[start : start + own_cols]
    for slot, out in enumerate((own, one, two, three)):
        for other in range(2):
            out[other] = turned[2 * (chip ^ slot) + (own_core ^ other)].astype(BF16)


def terms_body(*refs, planes):
    parts = refs[0:4]
    other_parts, line, other_line = refs[4:7]
    halo_back, halo_ahead, other_back, other_ahead = refs[7:11]
    outs, (cols, whole, sums) = refs[11:-3], refs[-3:]
    rows = halo_back.shape[0]
    chip, _, plane, _ = position(rows)
    for b in range(4):
        slot = b ^ chip
        for s in range(4):

            @pl.when(slot == s)
            def _():
                cols[0, :, b * rows : (b + 1) * rows] = parts[s][0]
                cols[1, :, b * rows : (b + 1) * rows] = other_parts[s]

    for side, pieces in enumerate(((halo_back, line, halo_ahead), (other_back, other_line, other_ahead))):
        whole[side, :rows] = pieces[0][...]
        whole[side, rows : 5 * rows] = pieces[1][...]
        whole[side, 5 * rows :] = pieces[2][...]
    own_cols = sums.shape[2]
    for k in range(3):
        span = slice(k * rows, (k + 4) * rows)
        value = dot(cols[0], whole[0, span]) + dot(cols[1], whole[1, span])
        for z in range(planes):
            sums[k, z] = value[z * own_cols : (z + 1) * own_cols]
    if len(outs) == 1:
        outs[0][...] = sums[...]
    else:
        for k in range(3):
            outs[0][k] = sums[k, plane]
            for s in range(1, 4):
                outs[s][k] = sums[k, plane ^ s].astype(BF16)


def second_forward(far, *refs):
    *others, acts, output_first, taps, output = refs
    first = position(acts.shape[0])[3]
    conv = dot(acts[...], taps[1])
    if others:
        conv = conv + dot(others[0][...], taps[2]) + dot(far[...], taps[0])
    else:
        conv = conv + dot(far[...], taps[2 * first])
    output[...] = (output_first[...].astype(F32) + conv).astype(BF16)


def first_backward(middle, behind, ahead, slope, taps, output):
    back = dot_t(middle[...], taps[1]) + dot_t(ahead[...], taps[0]) + dot_t(behind[...], taps[2])
    output[...] = (middle[...].astype(F32) + slope[...] * back).astype(BF16)


def far_pieces(values):
    size = lax.axis_size("seq")
    steps = DILATION_TWO // values.shape[0]
    if 2 * steps == size:
        return [moved(values, lambda i: i ^ steps)]
    return [moved(values, lambda i: i + steps), moved(values, lambda i: i - steps)]


def local(features, first_taps, second_taps, upstream):
    size = lax.axis_size("seq")
    planes = size // PLANE
    rows, width = features.shape
    own_cols = width // size
    group = own_cols * planes
    block = ((rows, width), BF16)
    wide = ((rows, width), F32)
    far_up = far_pieces(upstream)
    acts = gelu_pair(features)[0].astype(BF16)
    edge = moved(acts, lambda i: {0: i - 2, 3: i + 2}.get((i // 2) % 4))
    flip, turn, cross = (moved(acts, lambda i, s=s: i ^ (2 * s)) for s in (1, 3, 2))

    conv, back, slope = call(
        center_body, "center", [wide, wide, wide],
        features, acts, upstream, first_taps, second_taps,
    )
    flip, turn, cross, edge, conv, back, *far_up = lax.optimization_barrier(
        (flip, turn, cross, edge, conv, back, *far_up)
    )
    line, line_first, line_last = call(
        line_body, "line", [((4 * rows, width), BF16), block, block],
        acts, flip, turn, cross,
    )
    other_line = moved(line, lambda i: i ^ 1)
    halo_back = moved(line_last, lambda i: i + PLANE)
    halo_ahead = moved(line_first, lambda i: i - PLANE)

    part = ((2, group, rows), BF16)
    output_first, acts_second, middle, *parts = call(
        functools.partial(middle_body, planes=planes), "middle",
        [block, block, block, part, part, part, part],
        *far_up, line, edge, conv, upstream, back, first_taps, second_taps,
        scratch=[pltpu.VMEM((PLANE, group, rows), F32), pltpu.VMEM((2, rows, width), BF16)],
    )
    parts = [parts[0]] + [moved(parts[s], lambda i, s=s: i ^ (2 * s)) for s in (1, 2, 3)]
    gathered = jnp.stack([p[1] for p in parts])
    other_parts = moved(gathered, lambda i: i ^ 1)

    other_back, other_ahead = (moved(h, lambda i: i ^ 1) for h in (halo_back, halo_ahead))
    far_second = far_pieces(acts_second)

    piece = ((3, own_cols, width), BF16)
    outs = [((3, own_cols, width), F32), piece, piece, piece]
    if planes != 4:
        outs = [((3, planes, own_cols, width), F32)]
    terms = call(
        functools.partial(terms_body, planes=planes), "terms", outs,
        *parts, other_parts, line, other_line, halo_back, halo_ahead, other_back, other_ahead,
        scratch=[
            pltpu.VMEM((2, group, 4 * rows), BF16),
            pltpu.VMEM((2, 6 * rows, width), BF16),
            pltpu.VMEM((3, planes, own_cols, width), F32),
        ],
    )
    terms, far_second = lax.optimization_barrier((terms, far_second))
    if planes == 4:
        got = [moved(terms[s], lambda i, s=s: i ^ (PLANE * s)) for s in (1, 2, 3)]
        total = terms[0] + sum(g.astype(F32) for g in got)
    else:
        lines = [list(range(r, size, PLANE)) for r in range(PLANE)]
        total = lax.psum_scatter(terms[0], "seq", scatter_dimension=1, axis_index_groups=lines)
    first_taps_gradient = jnp.swapaxes(total, 1, 2)

    middle, acts_second = lax.optimization_barrier((middle, acts_second, terms[0]))[:2]
    behind = moved(middle, lambda i: i + 2)
    ahead = moved(middle, lambda i: i - 2)
    (second_layer_output,) = call(
        second_forward, "second_forward", [block],
        *far_second, acts_second, output_first, second_taps,
    )
    (input_gradient,) = call(
        first_backward, "first_backward", [block],
        middle, behind, ahead, slope, first_taps,
    )
    return second_layer_output, input_gradient, first_taps_gradient


def solution(mesh):
    placed = (P(("groups", "seq"), None), P(), P(), P(("groups", "seq"), None))
    return jax.shard_map(
        local,
        mesh=mesh,
        in_specs=placed,
        out_specs=(
            P(("groups", "seq"), None),
            P(("groups", "seq"), None),
            P(None, "groups", "seq"),
        ),
        check_vma=False,
    )
```

time: 81.5 us -> 66.7 us (0.82)
  the two profiles are of different devices: /device:TPU:0 before, /device:TPU:20 now
where the time goes in v2:
time: 66.7 us; the launch traced here: 66.4 us
  starting transfers between devices  31 us (46%)
  waiting for transfers between devices  20.5 us (31%)
  Pallas kernels  6.28 us (9%)
  local copies, waits for them, and re-layouts  5.87 us (9%)
  other arithmetic  1.86 us (3%)
  between operations  0.79 us (1%)
    ppermute x20, starting transfers between devices, moved(): return lax.ppermute(array, 'seq', pairs)  31 us
    ppermute x20, waiting for transfers between devices, moved(): return lax.ppermute(array, 'seq', pairs)  20.5 us
    pallas_call x6, Pallas kernels, call(): pl.pallas_call(body, name=name, out_shape=[jax.ShapeDtypeStruct(shape, ki...  6.28 us
    unnamed x12, local copies, waits for them, and re-layouts  5.86 us
  transfers between devices with their start and end apart: 20, of which 8 were waited for; matrix products, arithmetic and copies ran while one was open for 1% of the time, Pallas kernels for 6%

profile of v2, /device:TPU:20, one launch (start us, length us, event | category | flops | bytes accessed | tf_op | source)
XLA Modules:
  0.0 66.4 jit_solution(14728035514283479067)
XLA Ops:
  0.6 1.1 %fusion.5.acts = bf16[128,768]{1,0:T(8,128)(2,1)S(1)} fusion(bf16[128,768]{1,0:T(8,128)(2,1)} %features.1), kind=kLoop, calls=%fused_computation.9 | loop fusion | flops 983040 | bytes 393216 | tf_op jit(solution)/shard_map/convert_element_type | solution.py:189
  1.8 1.6 %collective-permute-start = (bf16[128,768]{1,0:T(8,128)(2,1)S(1)}, bf16[128,768]{1,0:T(8,128)(2,1)S(1)}, u32[]{:S(2)}, u32[]{:S(2)}) collective-permute-start(bf16[128,768]{1,0:T(8,128)(2,1)S(1)} %fusion.5.acts), channel_id=1, source_target_pairs={{0,2},{1,3},{2,0},{3,1},{4,6},{5,7},{6,4},{7,5},{8,10},{9,11},{10,... | collective-permute-start | bytes 589832 | tf_op jit(solution)/shard_map/ppermute | solution.py:22
  3.3 0.5 collective-permute-start.1
  3.8 1.5 %collective-permute-start.2 = (bf16[128,768]{1,0:T(8,128)(2,1)S(1)}, bf16[128,768]{1,0:T(8,128)(2,1)S(1)}, u32[]{:S(2)}, u32[]{:S(2)}) collective-permute-start(bf16[128,768]{1,0:T(8,128)(2,1)S(1)} %fusion.5.acts), channel_id=1, source_target_pairs={{0,4},{1,5},{2,6},{3,7},{4,0},{5,1},{6,2},{7,3},{8,12},{9,13},{10,... | collective-permute-start | bytes 589832 | tf_op jit(solution)/shard_map/ppermute | solution.py:22
  5.3 0.7 collective-permute-start.3
  6.4 2.0 %copy-done = bf16[3,768,768]{2,1,0:T(8,128)(2,1)S(1)} copy-done((bf16[3,768,768]{2,1,0:T(8,128)(2,1)S(1)}, bf16[3,768,768]{2,1,0:T(8,128)(2,1)}, u32[]{:S(2)}) %copy-start) | copy-done | bytes 3538968
  8.4 2.0 %copy-done.2 = bf16[3,768,768]{2,1,0:T(8,128)(2,1)S(1)} copy-done((bf16[3,768,768]{2,1,0:T(8,128)(2,1)S(1)}, bf16[3,768,768]{2,1,0:T(8,128)(2,1)}, u32[]{:S(2)}) %copy-start.2) | copy-done | bytes 3538968
  10.4 0.9 %copy-done.3 = bf16[128,768]{1,0:T(8,128)(2,1)S(1)} copy-done((bf16[128,768]{1,0:T(8,128)(2,1)S(1)}, bf16[128,768]{1,0:T(8,128)(2,1)}, u32[]{:S(2)}) %copy-start.3) | copy-done | bytes 196632
  11.3 0.9 %copy-done.4 = bf16[128,768]{1,0:T(8,128)(2,1)S(1)} copy-done((bf16[128,768]{1,0:T(8,128)(2,1)S(1)}, bf16[128,768]{1,0:T(8,128)(2,1)}, u32[]{:S(2)}) %copy-start.4) | copy-done | bytes 196632
  12.2 1.0 %center.1 = (f32[128,768]{1,0:T(8,128)S(1)}, f32[128,768]{1,0:T(8,128)S(1)}, f32[128,768]{1,0:T(8,128)S(1)}) custom-call(bf16[128,768]{1,0:T(8,128)(2,1)S(1)} %copy-done.3, bf16[128,768]{1,0:T(8,128)(2,1)S(1)} %fusion.5.acts, bf16[128,768]{1,0:T(8,128)(2,1)S(1)} %copy-done.4, bf16[3,768,768]{2,1,0:T(8,128)(2,1)S(1)} %copy-done, ...), custom_call_target="tpu_custom_call" | custom-call | tf_op jit(solution)/shard_map/center/pallas_call | solution.py:44
  13.3 3.0 %collective-permute-done.2.cross = bf16[128,768]{1,0:T(8,128)(2,1)S(1)} collective-permute-done((bf16[128,768]{1,0:T(8,128)(2,1)S(1)}, bf16[128,768]{1,0:T(8,128)(2,1)S(1)}, u32[]{:S(2)}, u32[]{:S(2)}) %collective-permute-start.2) | collective-permute-done | bytes 196640 | tf_op jit(solution)/shard_map/ppermute | solution.py:22
  16.5 4.5 %collective-permute-start.10 = (bf16[128,768]{1,0:T(8,128)(2,1)S(1)}, bf16[128,768]{1,0:T(8,128)(2,1)S(1)}, u32[]{:S(2)}, u32[]{:S(2)}) collective-permute-start(bf16[128,768]{1,0:T(8,128)(2,1)S(1)} %get-tuple-element.48), channel_id=1, source_target_pairs={{0,8},{1,9},{2,10},{3,11},{4,12},{5,13},{6,14},{7,15},{8,16},{9,17... | collective-permute-start | bytes 589832 | tf_op jit(solution)/shard_map/ppermute | solution.py:22
  21.0 1.9 %collective-permute-start.11 = (bf16[128,768]{1,0:T(8,128)(2,1)S(1)}, bf16[128,768]{1,0:T(8,128)(2,1)S(1)}, u32[]{:S(2)}, u32[]{:S(2)}) collective-permute-start(bf16[128,768]{1,0:T(8,128)(2,1)S(1)} %get-tuple-element.49), channel_id=1, source_target_pairs={{8,0},{9,1},{10,2},{11,3},{12,4},{13,5},{14,6},{15,7},{16,8},{17,9... | collective-permute-start | bytes 589832 | tf_op jit(solution)/shard_map/ppermute | solution.py:22
  23.0 1.0 %middle.1 = (bf16[128,768]{1,0:T(8,128)(2,1)S(1)}, bf16[128,768]{1,0:T(8,128)(2,1)S(1)}, bf16[128,768]{1,0:T(8,128)(2,1)S(1)}, bf16[2,96,128]{2,1,0:T(8,128)(2,1...) custom-call(bf16[128,768]{1,0:T(8,128)(2,1)S(1)} %collective-permute-done.4, ...), custom_call_target="tpu_custom_call" | custom-call | tf_op jit(solution)/shard_map/middle/pallas_call | solution.py:44
  24.0 5.5 %collective-permute-start.5 = (bf16[2,96,128]{2,1,0:T(8,128)(2,1)S(1)}, bf16[2,96,128]{2,1,0:T(8,128)(2,1)S(1)}, u32[]{:S(2)}, u32[]{:S(2)}) collective-permute-start(bf16[2,96,128]{2,1,0:T(8,128)(2,1)S(1)} %get-tuple-element.45), channel_id=1, source_target_pairs={{0,2},{1,3},{2,0},{3,1},{4,6},{5,7},{6,4},{7,5},{8,10},{9,11},{10,... | collective-permute-start | bytes 147464 | tf_op jit(solution)/shard_map/ppermute | solution.py:22
  29.5 2.1 %collective-permute-done.5.refs_1_ = bf16[2,96,128]{2,1,0:T(8,128)(2,1)S(1)} collective-permute-done((bf16[2,96,128]{2,1,0:T(8,128)(2,1)S(1)}, bf16[2,96,128]{2,1,0:T(8,128)(2,1)S(1)}, u32[]{:S(2)}, u32[]{:S(2)}) %collective-permute-start.5) | collective-permute-done | bytes 49184 | tf_op jit(solution)/shard_map/ppermute | solution.py:22
  31.6 1.0 %collective-permute-start.7 = (bf16[2,96,128]{2,1,0:T(8,128)(2,1)S(1)}, bf16[2,96,128]{2,1,0:T(8,128)(2,1)S(1)}, u32[]{:S(2)}, u32[]{:S(2)}) collective-permute-start(bf16[2,96,128]{2,1,0:T(8,128)(2,1)S(1)} %get-tuple-element.47), channel_id=1, source_target_pairs={{0,6},{1,7},{2,4},{3,5},{4,2},{5,3},{6,0},{7,1},{8,14},{9,15},{10,... | collective-permute-start | bytes 147464 | tf_op jit(solution)/shard_map/ppermute | solution.py:22
  32.6 1.0 %collective-permute-done.6.refs_2_ = bf16[2,96,128]{2,1,0:T(8,128)(2,1)S(1)} collective-permute-done((bf16[2,96,128]{2,1,0:T(8,128)(2,1)S(1)}, bf16[2,96,128]{2,1,0:T(8,128)(2,1)S(1)}, u32[]{:S(2)}, u32[]{:S(2)}) %collective-permute-start.6) | collective-permute-done | bytes 49184 | tf_op jit(solution)/shard_map/ppermute | solution.py:22
  33.6 3.0 %collective-permute-done.7.refs_3_ = bf16[2,96,128]{2,1,0:T(8,128)(2,1)S(1)} collective-permute-done((bf16[2,96,128]{2,1,0:T(8,128)(2,1)S(1)}, bf16[2,96,128]{2,1,0:T(8,128)(2,1)S(1)}, u32[]{:S(2)}, u32[]{:S(2)}) %collective-permute-start.7) | collective-permute-done | bytes 49184 | tf_op jit(solution)/shard_map/ppermute | solution.py:22
  36.6 0.5 collective-permute-start.13
  37.3 1.2 %collective-permute-done.8.refs_4_ = bf16[4,96,128]{2,1,0:T(8,128)(2,1)S(1)} collective-permute-done((bf16[4,96,128]{2,1,0:T(8,128)(2,1)S(1)}, bf16[4,96,128]{2,1,0:T(8,128)(2,1)S(1)}, u32[]{:S(2)}, u32[]{:S(2)}) %collective-permute-start.8) | collective-permute-done | bytes 98336 | tf_op jit(solution)/shard_map/ppermute | solution.py:22
  38.5 1.0 %terms.1 = (f32[3,24,768]{2,1,0:T(8,128)S(1)}, bf16[3,24,768]{2,1,0:T(8,128)(2,1)S(1)}, bf16[3,24,768]{2,1,0:T(8,128)(2,1)S(1)}, bf16[3,24,768]{2,1,0:T(8,128)(2,1)S(1)}) custom-call(bf16[2,96,128]{2,1,0:T(8,128)(2,1)S(1)} %get-tuple-element.44.refs_0_, bf16[2,96,128]{2,1,0:T(8,128)(2,1)S(1)} %collective-permute-done.5.refs_1_, ...), custom_call_target="tpu_custom_call" | custom-call | tf_op jit(solution)/shard_map/terms/pallas_call | solution.py:44
  39.6 1.6 %collective-permute-done.14.far = bf16[128,768]{1,0:T(8,128)(2,1)S(1)} collective-permute-done((bf16[128,768]{1,0:T(8,128)(2,1)S(1)}, bf16[128,768]{1,0:T(8,128)(2,1)S(1)}, u32[]{:S(2)}, u32[]{:S(2)}) %collective-permute-start.14) | collective-permute-done | bytes 196640 | tf_op jit(solution)/shard_map/ppermute | solution.py:22
  41.2 4.6 %collective-permute-start.17 = (bf16[3,24,768]{2,1,0:T(8,128)(2,1)S(1)}, bf16[3,24,768]{2,1,0:T(8,128)(2,1)S(1)}, u32[]{:S(2)}, u32[]{:S(2)}) collective-permute-start(bf16[3,24,768]{2,1,0:T(8,128)(2,1)S(1)} %get-tuple-element.62), channel_id=1, source_target_pairs={{0,8},{1,9},{2,10},{3,11},{4,12},{5,13},{6,14},{7,15},{8,0},{9,1},... | collective-permute-start | bytes 331784 | tf_op jit(solution)/shard_map/ppermute | solution.py:22
  45.8 1.5 %collective-permute-start.19 = (bf16[3,24,768]{2,1,0:T(8,128)(2,1)S(1)}, bf16[3,24,768]{2,1,0:T(8,128)(2,1)S(1)}, u32[]{:S(2)}, u32[]{:S(2)}) collective-permute-start(bf16[3,24,768]{2,1,0:T(8,128)(2,1)S(1)} %get-tuple-element.64), channel_id=1, source_target_pairs={{0,24},{1,25},{2,26},{3,27},{4,28},{5,29},{6,30},{7,31},{8,16},{9,... | collective-permute-start | bytes 331784 | tf_op jit(solution)/shard_map/ppermute | solution.py:22
  47.2 2.5 %collective-permute-start.15 = (bf16[128,768]{1,0:T(8,128)(2,1)S(1)}, bf16[128,768]{1,0:T(8,128)(2,1)S(1)}, u32[]{:S(2)}, u32[]{:S(2)}) collective-permute-start(bf16[128,768]{1,0:T(8,128)(2,1)S(1)} %get-tuple-element.60.middle), channel_id=1, source_target_pairs={{0,2},{1,3},{2,4},{3,5},{4,6},{5,7},{6,8},{7,9},{8,10},{9,11},{10,... | collective-permute-start | bytes 589832 | tf_op jit(solution)/shard_map/ppermute | solution.py:22
  49.8 4.2 %collective-permute-start.16 = (bf16[128,768]{1,0:T(8,128)(2,1)S(1)}, bf16[128,768]{1,0:T(8,128)(2,1)S(1)}, u32[]{:S(2)}, u32[]{:S(2)}) collective-permute-start(bf16[128,768]{1,0:T(8,128)(2,1)S(1)} %get-tuple-element.60.middle), channel_id=1, source_target_pairs={{2,0},{3,1},{4,2},{5,3},{6,4},{7,5},{8,6},{9,7},{10,8},{11,9},{12,... | collective-permute-start | bytes 589832 | tf_op jit(solution)/shard_map/ppermute | solution.py:22
  54.0 1.2 %second_forward.1 = bf16[128,768]{1,0:T(8,128)(2,1)} custom-call(bf16[128,768]{1,0:T(8,128)(2,1)S(1)} %collective-permute-done.14.far, bf16[128,768]{1,0:T(8,128)(2,1)S(1)} %get-tuple-element.58.refs_0_, bf16[128,768]{1,0:T(8,128)(2,1)S(1)} %get-tuple-element.59.refs_1_, bf16[3,768,768]{2,1,0:T(8,128)(2,1)S(1)} %copy-done.2), custom_call_target="tpu_custom_call" | custom-call | tf_op jit(solution)/shard_map/second_forward/pallas_call | solution.py:44
  55.2 2.2 %collective-permute-done.19 = bf16[3,24,768]{2,1,0:T(8,128)(2,1)S(1)} collective-permute-done((bf16[3,24,768]{2,1,0:T(8,128)(2,1)S(1)}, bf16[3,24,768]{2,1,0:T(8,128)(2,1)S(1)}, u32[]{:S(2)}, u32[]{:S(2)}) %collective-permute-start.19) | collective-permute-done | bytes 110624 | tf_op jit(solution)/shard_map/ppermute | solution.py:22
  57.3 0.7 %add_bitcast_fusion = f32[3,768,24]{1,2,0:T(8,128)} fusion(f32[3,24,768]{2,1,0:T(8,128)S(1)} %get-tuple-element.57, bf16[3,24,768]{2,1,0:T(8,128)(2,1)S(1)} %collective-permute-done.19, bf16[3,24,768]{2,1,0:T(8,128)(2,1)S(1)} %collective-permute-done.18, bf16[3,24,768]{2,1,0:T(8,128)(2,1)S(1)} %collective-permute-done.17), kind=kLoop, calls=%fused_computation.10 | loop fusion | flops 331776 | bytes 774144 | tf_op jit(solution)/shard_map/transpose | solution.py:242
  58.1 6.3 %collective-permute-done.16.ahead = bf16[128,768]{1,0:T(8,128)(2,1)S(1)} collective-permute-done((bf16[128,768]{1,0:T(8,128)(2,1)S(1)}, bf16[128,768]{1,0:T(8,128)(2,1)S(1)}, u32[]{:S(2)}, u32[]{:S(2)}) %collective-permute-start.16) | collective-permute-done | bytes 196640 | tf_op jit(solution)/shard_map/ppermute | solution.py:22
  64.4 2.0 %first_backward.1 = bf16[128,768]{1,0:T(8,128)(2,1)} custom-call(bf16[128,768]{1,0:T(8,128)(2,1)S(1)} %get-tuple-element.60.middle, bf16[128,768]{1,0:T(8,128)(2,1)S(1)} %collective-permute-done.15.behind, bf16[128,768]{1,0:T(8,128)(2,1)S(1)} %collective-permute-done.16.ahead, f32[128,768]{1,0:T(8,128)S(1)} %get-tuple-element.61.slope, ...), custom_call_target="tpu_custom_call" | custom-call | tf_op jit(solution)/shard_map/first_backward/pallas_call | solution.py:44
  (33 shorter events, 0.8 us)
Async XLA Ops:
  0.6 22.3 %copy-start.5 = (bf16[128,768]{1,0:T(8,128)(2,1)S(1)}, bf16[128,768]{1,0:T(8,128)(2,1)}, u32[]{:S(2)}) copy-start(bf16[128,768]{1,0:T(8,128)(2,1)} %refs_3_.1) | copy-start | bytes 589828
  1.8 11.5 %collective-permute-start = (bf16[128,768]{1,0:T(8,128)(2,1)S(1)}, bf16[128,768]{1,0:T(8,128)(2,1)S(1)}, u32[]{:S(2)}, u32[]{:S(2)}) collective-permute-start(bf16[128,768]{1,0:T(8,128)(2,1)S(1)} %fusion.5.acts), channel_id=1, source_target_pairs={{0,2},{1,3},{2,0},{3,1},{4,6},{5,7},{6,4},{7,5},{8,10},{9,11},{10,... | collective-permute-start | bytes 589832 | tf_op jit(solution)/shard_map/ppermute | solution.py:22
  3.3 9.9 %collective-permute-start.1 = (bf16[128,768]{1,0:T(8,128)(2,1)S(1)}, bf16[128,768]{1,0:T(8,128)(2,1)S(1)}, u32[]{:S(2)}, u32[]{:S(2)}) collective-permute-start(bf16[128,768]{1,0:T(8,128)(2,1)S(1)} %fusion.5.acts), channel_id=1, source_target_pairs={{0,6},{1,7},{2,4},{3,5},{4,2},{5,3},{6,0},{7,1},{8,14},{9,15},{10,... | collective-permute-start | bytes 589832 | tf_op jit(solution)/shard_map/ppermute | solution.py:22
  3.8 12.5 %collective-permute-start.2 = (bf16[128,768]{1,0:T(8,128)(2,1)S(1)}, bf16[128,768]{1,0:T(8,128)(2,1)S(1)}, u32[]{:S(2)}, u32[]{:S(2)}) collective-permute-start(bf16[128,768]{1,0:T(8,128)(2,1)S(1)} %fusion.5.acts), channel_id=1, source_target_pairs={{0,4},{1,5},{2,6},{3,7},{4,0},{5,1},{6,2},{7,3},{8,12},{9,13},{10,... | collective-permute-start | bytes 589832 | tf_op jit(solution)/shard_map/ppermute | solution.py:22
  5.3 11.0 %collective-permute-start.3 = (bf16[128,768]{1,0:T(8,128)(2,1)S(1)}, bf16[128,768]{1,0:T(8,128)(2,1)S(1)}, u32[]{:S(2)}, u32[]{:S(2)}) collective-permute-start(bf16[128,768]{1,0:T(8,128)(2,1)S(1)} %fusion.5.acts), channel_id=1, source_target_pairs={{6,8},{7,9},{8,6},{9,7},{14,16},{15,17},{16,14},{17,15},{22,24},{2... | collective-permute-start | bytes 589832 | tf_op jit(solution)/shard_map/ppermute | solution.py:22
  6.0 10.3 %collective-permute-start.4 = (bf16[128,768]{1,0:T(8,128)(2,1)}, bf16[128,768]{1,0:T(8,128)(2,1)S(1)}, u32[]{:S(2)}, u32[]{:S(2)}) collective-permute-start(bf16[128,768]{1,0:T(8,128)(2,1)} %refs_3_.1), channel_id=1, source_target_pairs={{0,16},{1,17},{2,18},{3,19},{4,20},{5,21},{6,22},{7,23},{8,24},{9,... | collective-permute-start | bytes 589832 | tf_op jit(solution)/shard_map/ppermute | solution.py:22
  6.4 2.0 %copy-start = (bf16[3,768,768]{2,1,0:T(8,128)(2,1)S(1)}, bf16[3,768,768]{2,1,0:T(8,128)(2,1)}, u32[]{:S(2)}) copy-start(bf16[3,768,768]{2,1,0:T(8,128)(2,1)} %taps.3) | copy-start | bytes 10616836
  8.4 2.0 %copy-start.2 = (bf16[3,768,768]{2,1,0:T(8,128)(2,1)S(1)}, bf16[3,768,768]{2,1,0:T(8,128)(2,1)}, u32[]{:S(2)}) copy-start(bf16[3,768,768]{2,1,0:T(8,128)(2,1)} %refs_2_.1) | copy-start | bytes 10616836
  10.4 0.9 %copy-start.3 = (bf16[128,768]{1,0:T(8,128)(2,1)S(1)}, bf16[128,768]{1,0:T(8,128)(2,1)}, u32[]{:S(2)}) copy-start(bf16[128,768]{1,0:T(8,128)(2,1)} %features.1) | copy-start | bytes 589828
  11.3 0.9 %copy-start.4 = (bf16[128,768]{1,0:T(8,128)(2,1)S(1)}, bf16[128,768]{1,0:T(8,128)(2,1)}, u32[]{:S(2)}) copy-start(bf16[128,768]{1,0:T(8,128)(2,1)} %refs_3_.1) | copy-start | bytes 589828
  12.2 10.7 %copy-start.1 = (bf16[3,768,768]{2,1,0:T(8,128)(2,1)S(1)}, bf16[3,768,768]{2,1,0:T(8,128)(2,1)}, u32[]{:S(2)}) copy-start(bf16[3,768,768]{2,1,0:T(8,128)(2,1)} %taps.3) | copy-start | bytes 10616836
  16.4 22.1 %collective-permute-start.9 = (bf16[512,768]{1,0:T(8,128)(2,1)S(1)}, bf16[512,768]{1,0:T(8,128)(2,1)S(1)}, u32[]{:S(2)}, u32[]{:S(2)}) collective-permute-start(bf16[512,768]{1,0:T(8,128)(2,1)S(1)} %get-tuple-element.40.refs_0_.refs_5_), channel_id=1, source_target_pairs={{0,1},{1,0},{2,3},{3,2},{4,5},{5,4},{6,7},{7,6},{8,9},{9,8},{10,11... | collective-permute-start | bytes 2359304 | tf_op jit(solution)/shard_map/ppermute | solution.py:22
  16.5 20.1 %collective-permute-start.10 = (bf16[128,768]{1,0:T(8,128)(2,1)S(1)}, bf16[128,768]{1,0:T(8,128)(2,1)S(1)}, u32[]{:S(2)}, u32[]{:S(2)}) collective-permute-start(bf16[128,768]{1,0:T(8,128)(2,1)S(1)} %get-tuple-element.48), channel_id=1, source_target_pairs={{0,8},{1,9},{2,10},{3,11},{4,12},{5,13},{6,14},{7,15},{8,16},{9,17... | collective-permute-start | bytes 589832 | tf_op jit(solution)/shard_map/ppermute | solution.py:22
  21.0 15.6 %collective-permute-start.11 = (bf16[128,768]{1,0:T(8,128)(2,1)S(1)}, bf16[128,768]{1,0:T(8,128)(2,1)S(1)}, u32[]{:S(2)}, u32[]{:S(2)}) collective-permute-start(bf16[128,768]{1,0:T(8,128)(2,1)S(1)} %get-tuple-element.49), channel_id=1, source_target_pairs={{8,0},{9,1},{10,2},{11,3},{12,4},{13,5},{14,6},{15,7},{16,8},{17,9... | collective-permute-start | bytes 589832 | tf_op jit(solution)/shard_map/ppermute | solution.py:22
  24.0 7.6 %collective-permute-start.5 = (bf16[2,96,128]{2,1,0:T(8,128)(2,1)S(1)}, bf16[2,96,128]{2,1,0:T(8,128)(2,1)S(1)}, u32[]{:S(2)}, u32[]{:S(2)}) collective-permute-start(bf16[2,96,128]{2,1,0:T(8,128)(2,1)S(1)} %get-tuple-element.45), channel_id=1, source_target_pairs={{0,2},{1,3},{2,0},{3,1},{4,6},{5,7},{6,4},{7,5},{8,10},{9,11},{10,... | collective-permute-start | bytes 147464 | tf_op jit(solution)/shard_map/ppermute | solution.py:22
  29.5 4.1 %collective-permute-start.6 = (bf16[2,96,128]{2,1,0:T(8,128)(2,1)S(1)}, bf16[2,96,128]{2,1,0:T(8,128)(2,1)S(1)}, u32[]{:S(2)}, u32[]{:S(2)}) collective-permute-start(bf16[2,96,128]{2,1,0:T(8,128)(2,1)S(1)} %get-tuple-element.46), channel_id=1, source_target_pairs={{0,4},{1,5},{2,6},{3,7},{4,0},{5,1},{6,2},{7,3},{8,12},{9,13},{10,... | collective-permute-start | bytes 147464 | tf_op jit(solution)/shard_map/ppermute | solution.py:22
  31.6 5.0 %collective-permute-start.7 = (bf16[2,96,128]{2,1,0:T(8,128)(2,1)S(1)}, bf16[2,96,128]{2,1,0:T(8,128)(2,1)S(1)}, u32[]{:S(2)}, u32[]{:S(2)}) collective-permute-start(bf16[2,96,128]{2,1,0:T(8,128)(2,1)S(1)} %get-tuple-element.47), channel_id=1, source_target_pairs={{0,6},{1,7},{2,4},{3,5},{4,2},{5,3},{6,0},{7,1},{8,14},{9,15},{10,... | collective-permute-start | bytes 147464 | tf_op jit(solution)/shard_map/ppermute | solution.py:22
  33.6 7.6 %collective-permute-start.14 = (bf16[128,768]{1,0:T(8,128)(2,1)S(1)}, bf16[128,768]{1,0:T(8,128)(2,1)S(1)}, u32[]{:S(2)}, u32[]{:S(2)}) collective-permute-start(bf16[128,768]{1,0:T(8,128)(2,1)S(1)} %get-tuple-element.58.refs_0_), channel_id=1, source_target_pairs={{0,16},{1,17},{2,18},{3,19},{4,20},{5,21},{6,22},{7,23},{8,24},{9,... | collective-permute-start | bytes 589832 | tf_op jit(solution)/shard_map/ppermute | solution.py:22
  36.6 1.9 %collective-permute-start.12 = (bf16[128,768]{1,0:T(8,128)(2,1)S(1)}, bf16[128,768]{1,0:T(8,128)(2,1)S(1)}, u32[]{:S(2)}, u32[]{:S(2)}) collective-permute-start(bf16[128,768]{1,0:T(8,128)(2,1)S(1)} %collective-permute-done.10.refs_7_), channel_id=1, source_target_pairs={{0,1},{1,0},{2,3},{3,2},{4,5},{5,4},{6,7},{7,6},{8,9},{9,8},{10,11... | collective-permute-start | bytes 589832 | tf_op jit(solution)/shard_map/ppermute | solution.py:22
  36.6 1.9 %collective-permute-start.13 = (bf16[128,768]{1,0:T(8,128)(2,1)S(1)}, bf16[128,768]{1,0:T(8,128)(2,1)S(1)}, u32[]{:S(2)}, u32[]{:S(2)}) collective-permute-start(bf16[128,768]{1,0:T(8,128)(2,1)S(1)} %collective-permute-done.11.refs_8_), channel_id=1, source_target_pairs={{0,1},{1,0},{2,3},{3,2},{4,5},{5,4},{6,7},{7,6},{8,9},{9,8},{10,11... | collective-permute-start | bytes 589832 | tf_op jit(solution)/shard_map/ppermute | solution.py:22
  37.2 1.4 %collective-permute-start.8 = (bf16[4,96,128]{2,1,0:T(8,128)(2,1)S(1)}, bf16[4,96,128]{2,1,0:T(8,128)(2,1)S(1)}, u32[]{:S(2)}, u32[]{:S(2)}) collective-permute-start(bf16[4,96,128]{2,1,0:T(8,128)(2,1)S(1)} %pad_maximum_fusion), channel_id=1, source_target_pairs={{0,1},{1,0},{2,3},{3,2},{4,5},{5,4},{6,7},{7,6},{8,9},{9,8},{10,11... | collective-permute-start | bytes 294920 | tf_op jit(solution)/shard_map/ppermute | solution.py:22
  41.2 13.9 %collective-permute-start.17 = (bf16[3,24,768]{2,1,0:T(8,128)(2,1)S(1)}, bf16[3,24,768]{2,1,0:T(8,128)(2,1)S(1)}, u32[]{:S(2)}, u32[]{:S(2)}) collective-permute-start(bf16[3,24,768]{2,1,0:T(8,128)(2,1)S(1)} %get-tuple-element.62), channel_id=1, source_target_pairs={{0,8},{1,9},{2,10},{3,11},{4,12},{5,13},{6,14},{7,15},{8,0},{9,1},... | collective-permute-start | bytes 331784 | tf_op jit(solution)/shard_map/ppermute | solution.py:22
  45.8 9.4 %collective-permute-start.18 = (bf16[3,24,768]{2,1,0:T(8,128)(2,1)S(1)}, bf16[3,24,768]{2,1,0:T(8,128)(2,1)S(1)}, u32[]{:S(2)}, u32[]{:S(2)}) collective-permute-start(bf16[3,24,768]{2,1,0:T(8,128)(2,1)S(1)} %get-tuple-element.63), channel_id=1, source_target_pairs={{0,16},{1,17},{2,18},{3,19},{4,20},{5,21},{6,22},{7,23},{8,24},{9,... | collective-permute-start | bytes 331784 | tf_op jit(solution)/shard_map/ppermute | solution.py:22
  45.8 11.6 %collective-permute-start.19 = (bf16[3,24,768]{2,1,0:T(8,128)(2,1)S(1)}, bf16[3,24,768]{2,1,0:T(8,128)(2,1)S(1)}, u32[]{:S(2)}, u32[]{:S(2)}) collective-permute-start(bf16[3,24,768]{2,1,0:T(8,128)(2,1)S(1)} %get-tuple-element.64), channel_id=1, source_target_pairs={{0,24},{1,25},{2,26},{3,27},{4,28},{5,29},{6,30},{7,31},{8,16},{9,... | collective-permute-start | bytes 331784 | tf_op jit(solution)/shard_map/ppermute | solution.py:22
  47.2 10.8 %collective-permute-start.15 = (bf16[128,768]{1,0:T(8,128)(2,1)S(1)}, bf16[128,768]{1,0:T(8,128)(2,1)S(1)}, u32[]{:S(2)}, u32[]{:S(2)}) collective-permute-start(bf16[128,768]{1,0:T(8,128)(2,1)S(1)} %get-tuple-element.60.middle), channel_id=1, source_target_pairs={{0,2},{1,3},{2,4},{3,5},{4,6},{5,7},{6,8},{7,9},{8,10},{9,11},{10,... | collective-permute-start | bytes 589832 | tf_op jit(solution)/shard_map/ppermute | solution.py:22
  49.8 14.6 %collective-permute-start.16 = (bf16[128,768]{1,0:T(8,128)(2,1)S(1)}, bf16[128,768]{1,0:T(8,128)(2,1)S(1)}, u32[]{:S(2)}, u32[]{:S(2)}) collective-permute-start(bf16[128,768]{1,0:T(8,128)(2,1)S(1)} %get-tuple-element.60.middle), channel_id=1, source_target_pairs={{2,0},{3,1},{4,2},{5,3},{6,4},{7,5},{8,6},{9,7},{10,8},{11,9},{12,... | collective-permute-start | bytes 589832 | tf_op jit(solution)/shard_map/ppermute | solution.py:22

commit v3 on v1

v3 whole, which is shorter than its diff:
```python
import functools

import jax
import jax.numpy as jnp
from jax import lax
from jax.experimental import pallas as pl
from jax.experimental.pallas import tpu as pltpu
from jax.sharding import PartitionSpec as P

DILATION_ONE = 256
DILATION_TWO = 2048
PLANE = 8
LIMIT = 8 * 2**20
F32 = jnp.float32
BF16 = jnp.bfloat16


def moved(array, target):
    size = lax.axis_size("seq")
    pairs = [(i, target(i)) for i in range(size)]
    pairs = [(i, t) for i, t in pairs if t is not None and 0 <= t < size]
    return lax.ppermute(array, "seq", pairs)


def flipped(array):
    return moved(array, lambda i: i ^ 2)


def stepped(array):
    return moved(array, lambda i: i + 2 if (i // 2) % 2 else i - 2)


def far_pieces(values):
    size = lax.axis_size("seq")
    steps = DILATION_TWO // values.shape[0]
    if 2 * steps == size:
        return [moved(values, lambda i: i ^ steps)]
    return [moved(values, lambda i: i + steps), moved(values, lambda i: i - steps)]


def gelu_pair(values):
    wide = values.astype(F32)
    return jax.jvp(jax.nn.gelu, (wide,), (jnp.ones_like(wide),))


def dot(a, b):
    return jnp.dot(a, b, preferred_element_type=F32)


def dot_t(a, b):
    return lax.dot_general(a, b, (((1,), (1,)), ((), ())), preferred_element_type=F32)


def call(body, name, outs, *arrays, held=(), scratch=()):
    vmem = pl.BlockSpec(memory_space=pltpu.VMEM)
    held = [pltpu.with_memory_space_constraint(a, pltpu.HBM) for a in held]
    return pl.pallas_call(
        body,
        name=name,
        out_shape=[jax.ShapeDtypeStruct(shape, kind) for shape, kind in outs],
        in_specs=[pl.BlockSpec(memory_space=pltpu.HBM)] * len(held) + [vmem] * len(arrays),
        out_specs=[vmem] * len(outs),
        scratch_shapes=list(scratch),
        compiler_params=pltpu.CompilerParams(vmem_limit_bytes=LIMIT),
    )(*held, *arrays)


def position(rows):
    index = lax.axis_index("seq")
    lower = (index < DILATION_TWO // rows).astype(jnp.int32)
    return (index >> 1) & 3, index & 1, index >> 3, lower


def load_body(features, up, taps, second_taps, acts, conv, back, *refs):
    held, second_held, values, cotangent, sems = refs
    pairs = [(features, values), (taps.at[1], held.at[1])]
    pairs += [(up, cotangent), (second_taps.at[1], second_held.at[1])]
    for k in (0, 2):
        pairs += [(taps.at[k], held.at[k]), (second_taps.at[k], second_held.at[k])]
    copies = [pltpu.make_async_copy(a, b, sems.at[n]) for n, (a, b) in enumerate(pairs)]
    for copy in copies:
        copy.start()
    copies[0].wait()
    copies[1].wait()
    conv[...] = values[...].astype(F32) + dot(acts[...], held[1])
    copies[2].wait()
    copies[3].wait()
    back[...] = dot_t(cotangent[...], second_held[1])
    for copy in copies[4:]:
        copy.wait()


def forward_body(flip, step, conv, taps, output, acts_second, slope):
    odd = position(flip.shape[0])[0] & 1
    result = conv[...] + dot(step[...], taps[2 * odd]) + dot(flip[...], taps[2 - 2 * odd])
    result = result.astype(BF16)
    output[...] = result
    activated, steep = gelu_pair(result)
    acts_second[...] = activated.astype(BF16)
    slope[...] = steep


def middle_body(*refs, planes):
    *far, slope, up, back, taps, middle, own, one, two, three, turned = refs
    chip, core, _, lower = position(up.shape[0])
    total = back[...]
    if len(far) == 2:
        total = total + dot_t(far[0][...], taps[2]) + dot_t(far[1][...], taps[0])
    else:
        total = total + dot_t(far[0][...], taps[2 - 2 * lower])
    value = (up[...].astype(F32) + slope[...] * total).astype(BF16)
    middle[...] = value
    flat = value.astype(F32).T
    cols = turned.shape[1] // planes
    for plane in range(planes):
        for owner in range(PLANE):
            start = (plane * PLANE + owner) * cols
            turned[owner, plane * cols : (plane + 1) * cols] = flat[start : start + cols]
    for slot, out in enumerate((own, one, two, three)):
        for other in range(2):
            out[other] = turned[2 * (chip ^ slot) + (core ^ other)].astype(BF16)


def line_body(acts, flip, step, cross, turn, line):
    rows = acts.shape[0]
    chip = position(rows)[0]
    for slot, piece in enumerate((acts, flip, cross)):
        line[pl.ds((chip ^ slot) * rows, rows)] = piece[...]
    inner = (chip == 1) | (chip == 2)

    @pl.when(inner)
    def _():
        line[pl.ds((chip ^ 3) * rows, rows)] = step[...]

    @pl.when(jnp.logical_not(inner))
    def _():
        line[pl.ds((chip ^ 3) * rows, rows)] = turn[...]


def regroup_body(*refs):
    parts, (other_parts, cols, first, last) = refs[:4], refs[4:]
    rows = first.shape[2]
    chip = position(rows)[0]
    for slot, part in enumerate(parts):
        for side, piece in enumerate((part[0], other_parts[slot])):
            for b in range(4):

                @pl.when(chip == (slot ^ b))
                def _():
                    cols[side, :, b * rows : (b + 1) * rows] = piece

            @pl.when(chip == slot)
            def _():
                first[side] = piece

            @pl.when(chip == (slot ^ 3))
            def _():
                last[side] = piece


def terms_body(cols, behind, ahead, line, other_line, *refs, planes):
    outs, (stacked, sums) = refs[:-2], refs[-2:]
    group, rows = behind.shape[1:]
    plane = position(rows)[2]
    own_cols = group // planes
    total = None
    for side, acts in enumerate((line, other_line)):
        stacked[:group, : 3 * rows] = cols[side, :, rows:]
        stacked[:group, 3 * rows :] = ahead[side]
        stacked[group : 2 * group] = cols[side]
        stacked[2 * group :, :rows] = behind[side]
        stacked[2 * group :, rows:] = cols[side, :, : 3 * rows]
        value = dot(stacked[...], acts[...])
        total = value if total is None else total + value
    for k in range(3):
        for z in range(planes):
            start = k * group + z * own_cols
            sums[k, z] = total[start : start + own_cols]
    if len(outs) == 1:
        outs[0][...] = sums[...]
    else:
        for k in range(3):
            outs[0][k] = sums[k, plane]
            for s in range(1, 4):
                outs[s][k] = sums[k, plane ^ s].astype(BF16)


def second_forward(*refs):
    *far, acts, output_first, taps, output = refs
    lower = position(acts.shape[0])[3]
    conv = dot(acts[...], taps[1])
    if len(far) == 2:
        conv = conv + dot(far[0][...], taps[0]) + dot(far[1][...], taps[2])
    else:
        conv = conv + dot(far[0][...], taps[2 * lower])
    output[...] = (output_first[...].astype(F32) + conv).astype(BF16)


def first_backward(middle, flip, step, features, taps, output):
    odd = position(middle.shape[0])[0] & 1
    back = dot_t(middle[...], taps[1])
    back = back + dot_t(step[...], taps[2 - 2 * odd]) + dot_t(flip[...], taps[2 * odd])
    slope = gelu_pair(features[...])[1]
    output[...] = (middle[...].astype(F32) + slope * back).astype(BF16)


def local(features, first_taps, second_taps, upstream):
    size = lax.axis_size("seq")
    planes = size // PLANE
    rows, width = features.shape
    own_cols = width // size
    group = own_cols * planes
    block, wide = ((rows, width), BF16), ((rows, width), F32)
    all_taps = ((3, width, width), BF16)
    part = ((2, group, rows), BF16)
    together = lax.optimization_barrier

    acts = gelu_pair(features)[0].astype(BF16)
    far_up = far_pieces(upstream)
    conv, back, first_taps, second_taps, features, upstream = call(
        load_body, "load", [wide, wide, all_taps, all_taps, block, block],
        acts, held=(features, upstream, first_taps, second_taps),
        scratch=[pltpu.SemaphoreType.DMA((8,))],
    )
    flip, step = flipped(acts), stepped(acts)
    cross = moved(acts, lambda i: i ^ 4)
    turn = moved(acts, lambda i: i ^ 6 if (i // 2) % 4 in (0, 3) else None)
    step, flip, conv = together((step, flip, conv))
    output_first, acts_second, slope = call(
        forward_body, "forward", [block, block, wide], flip, step, conv, first_taps
    )
    middle, *parts = call(
        functools.partial(middle_body, planes=planes), "middle",
        [block, part, part, part, part],
        *far_up, slope, upstream, back, second_taps,
        scratch=[pltpu.VMEM((PLANE, group, rows), F32)],
    )

    cross, turn, *parts = together((cross, turn, *parts))
    parts = [parts[0]] + [moved(parts[s], lambda i, s=s: i ^ (2 * s)) for s in (1, 2, 3)]
    far_second = far_pieces(acts_second)
    other_parts = moved(jnp.stack([p[1] for p in parts]), lambda i: i ^ 1)
    cols, col_first, col_last = call(
        regroup_body, "regroup", [((2, group, 4 * rows), BF16), part, part], *parts, other_parts
    )
    (line,) = call(
        line_body, "line", [((4 * rows, width), BF16)], acts, flip, step, cross, turn
    )
    other_line = moved(line, lambda i: i ^ 1)
    cols_behind = moved(col_last, lambda i: i + PLANE)
    cols_ahead = moved(col_first, lambda i: i - PLANE)
    other_line, far_second = together((other_line, far_second))

    piece = ((3, own_cols, width), BF16)
    outs = [((3, own_cols, width), F32), piece, piece, piece]
    if planes != 4:
        outs = [((3, planes, own_cols, width), F32)]
    terms = call(
        functools.partial(terms_body, planes=planes), "terms", outs,
        cols, cols_behind, cols_ahead, line, other_line,
        scratch=[
            pltpu.VMEM((3 * group, 4 * rows), BF16),
            pltpu.VMEM((3, planes, own_cols, width), F32),
        ],
    )
    late, _ = together((middle, terms[0]))
    middle_flip, middle_step = flipped(late), stepped(late)
    if planes == 4:
        got = [moved(terms[s], lambda i, s=s: i ^ (PLANE * s)) for s in (1, 2, 3)]
        total = terms[0] + sum(g.astype(F32) for g in got)
    else:
        lines = [list(range(r, size, PLANE)) for r in range(PLANE)]
        total = lax.psum_scatter(terms[0], "seq", scatter_dimension=1, axis_index_groups=lines)
    first_taps_gradient = jnp.swapaxes(total, 1, 2)

    (second_layer_output,) = call(
        second_forward, "second_forward", [block],
        *far_second, acts_second, output_first, second_taps,
    )
    (input_gradient,) = call(
        first_backward, "first_backward", [block],
        middle, middle_flip, middle_step, features, first_taps,
    )
    return second_layer_output, input_gradient, first_taps_gradient


def solution(mesh):
    placed = (P(("groups", "seq"), None), P(), P(), P(("groups", "seq"), None))
    return jax.shard_map(
        local,
        mesh=mesh,
        in_specs=placed,
        out_specs=(
            P(("groups", "seq"), None),
            P(("groups", "seq"), None),
            P(None, "groups", "seq"),
        ),
        check_vma=False,
    )
```

time: 81.5 us -> 57.1 us (0.70)
  the two profiles are of different devices: /device:TPU:0 before, /device:TPU:16 now
where the time goes in v3:
time: 57.1 us; the launch traced here: 56.9 us
  starting transfers between devices  30.4 us (53%)
  waiting for transfers between devices  15.1 us (26%)
  Pallas kernels  8.71 us (15%)
  other arithmetic  1.83 us (3%)
  between operations  0.79 us (1%)
    ppermute x18, starting transfers between devices, moved(): return lax.ppermute(array, 'seq', pairs)  30.4 us
    ppermute x18, waiting for transfers between devices, moved(): return lax.ppermute(array, 'seq', pairs)  15.1 us
    pallas_call x8, Pallas kernels, call(): pl.pallas_call(body, name=name, out_shape=[jax.ShapeDtypeStruct(shape, ki...  8.71 us
  transfers between devices with their start and end apart: 18, of which 9 were waited for; matrix products, arithmetic and copies ran while one was open for 1% of the time, Pallas kernels for 10%

profile of v3, /device:TPU:16, one launch (start us, length us, event | category | flops | bytes accessed | tf_op | source)
XLA Modules:
  0.0 56.9 jit_solution(9424735624989287436)
XLA Ops:
  0.6 1.1 %fusion.5.acts = bf16[128,768]{1,0:T(8,128)(2,1)S(1)} fusion(bf16[128,768]{1,0:T(8,128)(2,1)} %features.1), kind=kLoop, calls=%fused_computation.9 | loop fusion | flops 983040 | bytes 393216 | tf_op jit(solution)/shard_map/convert_element_type | solution.py:218
  1.7 4.2 %collective-permute-start = (bf16[128,768]{1,0:T(8,128)(2,1)S(1)}, bf16[128,768]{1,0:T(8,128)(2,1)S(1)}, u32[]{:S(2)}, u32[]{:S(2)}) collective-permute-start(bf16[128,768]{1,0:T(8,128)(2,1)S(1)} %fusion.5.acts), channel_id=1, source_target_pairs={{2,4},{3,5},{4,2},{5,3},{6,8},{7,9},{8,6},{9,7},{10,12},{11,13},{1... | collective-permute-start | bytes 589832 | tf_op jit(solution)/shard_map/ppermute | solution.py:22
  6.0 0.7 %collective-permute-start.1 = (bf16[128,768]{1,0:T(8,128)(2,1)S(1)}, bf16[128,768]{1,0:T(8,128)(2,1)S(1)}, u32[]{:S(2)}, u32[]{:S(2)}) collective-permute-start(bf16[128,768]{1,0:T(8,128)(2,1)S(1)} %fusion.5.acts), channel_id=1, source_target_pairs={{0,2},{1,3},{2,0},{3,1},{4,6},{5,7},{6,4},{7,5},{8,10},{9,11},{10,... | collective-permute-start | bytes 589832 | tf_op jit(solution)/shard_map/ppermute | solution.py:22
  6.7 0.3 collective-permute-start.4
  7.0 1.5 %collective-permute-start.2 = (bf16[128,768]{1,0:T(8,128)(2,1)S(1)}, bf16[128,768]{1,0:T(8,128)(2,1)S(1)}, u32[]{:S(2)}, u32[]{:S(2)}) collective-permute-start(bf16[128,768]{1,0:T(8,128)(2,1)S(1)} %fusion.5.acts), channel_id=1, source_target_pairs={{0,4},{1,5},{2,6},{3,7},{4,0},{5,1},{6,2},{7,3},{8,12},{9,13},{10,... | collective-permute-start | bytes 589832 | tf_op jit(solution)/shard_map/ppermute | solution.py:22
  8.5 2.9 %collective-permute-start.3 = (bf16[128,768]{1,0:T(8,128)(2,1)S(1)}, bf16[128,768]{1,0:T(8,128)(2,1)S(1)}, u32[]{:S(2)}, u32[]{:S(2)}) collective-permute-start(bf16[128,768]{1,0:T(8,128)(2,1)S(1)} %fusion.5.acts), channel_id=1, source_target_pairs={{0,6},{1,7},{6,0},{7,1},{8,14},{9,15},{14,8},{15,9},{16,22},{17,23... | collective-permute-start | bytes 589832 | tf_op jit(solution)/shard_map/ppermute | solution.py:22
  11.4 3.3 %load.1 = (f32[128,768]{1,0:T(8,128)S(1)}, f32[128,768]{1,0:T(8,128)S(1)}, bf16[3,768,768]{2,1,0:T(8,128)(2,1)S(1)}, bf16[3,768,768]{2,1,0:T(8,128)(2,1)S(1)}, b...) custom-call(bf16[128,768]{1,0:T(8,128)(2,1)} %features.1, bf16[128,768]{1,0:T(8,128)(2,1)} %up.1, ...), custom_call_target="tpu_custom_call" | custom-call | tf_op jit(solution)/shard_map/load/pallas_call | solution.py:57
  14.7 2.8 %collective-permute-done.step = bf16[128,768]{1,0:T(8,128)(2,1)S(1)} collective-permute-done((bf16[128,768]{1,0:T(8,128)(2,1)S(1)}, bf16[128,768]{1,0:T(8,128)(2,1)S(1)}, u32[]{:S(2)}, u32[]{:S(2)}) %collective-permute-start) | collective-permute-done | bytes 196640 | tf_op jit(solution)/shard_map/ppermute | solution.py:22
  17.5 0.6 %forward.1 = (bf16[128,768]{1,0:T(8,128)(2,1)S(1)}, bf16[128,768]{1,0:T(8,128)(2,1)S(1)}, f32[128,768]{1,0:T(8,128)S(1)}) custom-call(bf16[128,768]{1,0:T(8,128)(2,1)S(1)} %collective-permute-done.1.flip, bf16[128,768]{1,0:T(8,128)(2,1)S(1)} %collective-permute-done.step, f32[128,768]{1,0:T(8,128)S(1)} %get-tuple-element.39.conv, ...), custom_call_target="tpu_custom_call" | custom-call | tf_op jit(solution)/shard_map/forward/pallas_call | solution.py:57
  18.1 0.5 collective-permute-done.4.refs_0_
  18.7 0.7 %middle.1 = (bf16[128,768]{1,0:T(8,128)(2,1)S(1)}, bf16[2,96,128]{2,1,0:T(8,128)(2,1)S(1)}, bf16[2,96,128]{2,1,0:T(8,128)(2,1)S(1)}, bf16[2,96,128]{2,1,0:T(8,128)(2,1)S(1)}, bf16[2,96,128]{2,1,0:T(8,128)(2,1)S(1)}) custom-call(bf16[128,768]{1,0:T(8,128)(2,1)S(1)} %collective-permute-done.4.refs_0_, f32[128,768]{1,0:T(8,128)S(1)} %get-tuple-element.41.refs_1_, ...), custom_call_target="tpu_custom_call" | custom-call | tf_op jit(solution)/shard_map/middle/pallas_call | solution.py:57
  19.3 1.2 %collective-permute-done.3.turn = bf16[128,768]{1,0:T(8,128)(2,1)S(1)} collective-permute-done((bf16[128,768]{1,0:T(8,128)(2,1)S(1)}, bf16[128,768]{1,0:T(8,128)(2,1)S(1)}, u32[]{:S(2)}, u32[]{:S(2)}) %collective-permute-start.3) | collective-permute-done | bytes 196640 | tf_op jit(solution)/shard_map/ppermute | solution.py:22
  20.6 2.2 %collective-permute-start.9 = (bf16[2,96,128]{2,1,0:T(8,128)(2,1)S(1)}, bf16[2,96,128]{2,1,0:T(8,128)(2,1)S(1)}, u32[]{:S(2)}, u32[]{:S(2)}) collective-permute-start(bf16[2,96,128]{2,1,0:T(8,128)(2,1)S(1)} %get-tuple-element.58), channel_id=1, source_target_pairs={{0,6},{1,7},{2,4},{3,5},{4,2},{5,3},{6,0},{7,1},{8,14},{9,15},{10,... | collective-permute-start | bytes 147464 | tf_op jit(solution)/shard_map/ppermute | solution.py:22
  22.9 1.3 %collective-permute-start.7 = (bf16[2,96,128]{2,1,0:T(8,128)(2,1)S(1)}, bf16[2,96,128]{2,1,0:T(8,128)(2,1)S(1)}, u32[]{:S(2)}, u32[]{:S(2)}) collective-permute-start(bf16[2,96,128]{2,1,0:T(8,128)(2,1)S(1)} %get-tuple-element.56), channel_id=1, source_target_pairs={{0,2},{1,3},{2,0},{3,1},{4,6},{5,7},{6,4},{7,5},{8,10},{9,11},{10,... | collective-permute-start | bytes 147464 | tf_op jit(solution)/shard_map/ppermute | solution.py:22
  24.2 2.1 %collective-permute-start.6 = (bf16[128,768]{1,0:T(8,128)(2,1)S(1)}, bf16[128,768]{1,0:T(8,128)(2,1)S(1)}, u32[]{:S(2)}, u32[]{:S(2)}) collective-permute-start(bf16[128,768]{1,0:T(8,128)(2,1)S(1)} %get-tuple-element.51.refs_1_), channel_id=1, source_target_pairs={{0,16},{1,17},{2,18},{3,19},{4,20},{5,21},{6,22},{7,23},{8,24},{9,... | collective-permute-start | bytes 589832 | tf_op jit(solution)/shard_map/ppermute | solution.py:22
  26.4 0.6 %collective-permute-done.8.refs_2_ = bf16[2,96,128]{2,1,0:T(8,128)(2,1)S(1)} collective-permute-done((bf16[2,96,128]{2,1,0:T(8,128)(2,1)S(1)}, bf16[2,96,128]{2,1,0:T(8,128)(2,1)S(1)}, u32[]{:S(2)}, u32[]{:S(2)}) %collective-permute-start.8) | collective-permute-done | bytes 49184 | tf_op jit(solution)/shard_map/ppermute | solution.py:22
  27.1 1.3 %collective-permute-done.10.refs_4_ = bf16[4,96,128]{2,1,0:T(8,128)(2,1)S(1)} collective-permute-done((bf16[4,96,128]{2,1,0:T(8,128)(2,1)S(1)}, bf16[4,96,128]{2,1,0:T(8,128)(2,1)S(1)}, u32[]{:S(2)}, u32[]{:S(2)}) %collective-permute-start.10) | collective-permute-done | bytes 98336 | tf_op jit(solution)/shard_map/ppermute | solution.py:22
  28.6 3.2 %collective-permute-start.11 = (bf16[2,96,128]{2,1,0:T(8,128)(2,1)S(1)}, bf16[2,96,128]{2,1,0:T(8,128)(2,1)S(1)}, u32[]{:S(2)}, u32[]{:S(2)}) collective-permute-start(bf16[2,96,128]{2,1,0:T(8,128)(2,1)S(1)} %get-tuple-element.60), channel_id=1, source_target_pairs={{0,8},{1,9},{2,10},{3,11},{4,12},{5,13},{6,14},{7,15},{8,16},{9,17... | collective-permute-start | bytes 147464 | tf_op jit(solution)/shard_map/ppermute | solution.py:22
  31.8 2.6 %collective-permute-start.12 = (bf16[2,96,128]{2,1,0:T(8,128)(2,1)S(1)}, bf16[2,96,128]{2,1,0:T(8,128)(2,1)S(1)}, u32[]{:S(2)}, u32[]{:S(2)}) collective-permute-start(bf16[2,96,128]{2,1,0:T(8,128)(2,1)S(1)} %get-tuple-element.61), channel_id=1, source_target_pairs={{8,0},{9,1},{10,2},{11,3},{12,4},{13,5},{14,6},{15,7},{16,8},{17,9... | collective-permute-start | bytes 147464 | tf_op jit(solution)/shard_map/ppermute | solution.py:22
  34.5 2.4 %collective-permute-done.11.behind = bf16[2,96,128]{2,1,0:T(8,128)(2,1)S(1)} collective-permute-done((bf16[2,96,128]{2,1,0:T(8,128)(2,1)S(1)}, bf16[2,96,128]{2,1,0:T(8,128)(2,1)S(1)}, u32[]{:S(2)}, u32[]{:S(2)}) %collective-permute-start.11) | collective-permute-done | bytes 49184 | tf_op jit(solution)/shard_map/ppermute | solution.py:22
  36.8 1.0 %collective-permute-done.12.ahead = bf16[2,96,128]{2,1,0:T(8,128)(2,1)S(1)} collective-permute-done((bf16[2,96,128]{2,1,0:T(8,128)(2,1)S(1)}, bf16[2,96,128]{2,1,0:T(8,128)(2,1)S(1)}, u32[]{:S(2)}, u32[]{:S(2)}) %collective-permute-start.12) | collective-permute-done | bytes 49184 | tf_op jit(solution)/shard_map/ppermute | solution.py:22
  37.8 0.7 %terms.1 = (f32[3,24,768]{2,1,0:T(8,128)S(1)}, bf16[3,24,768]{2,1,0:T(8,128)(2,1)S(1)}, bf16[3,24,768]{2,1,0:T(8,128)(2,1)S(1)}, bf16[3,24,768]{2,1,0:T(8,128)(2,1)S(1)}) custom-call(bf16[2,96,512]{2,1,0:T(8,128)(2,1)S(1)} %get-tuple-element.59.cols, bf16[2,96,128]{2,1,0:T(8,128)(2,1)S(1)} %collective-permute-done.11.behind, ...), custom_call_target="tpu_custom_call" | custom-call | tf_op jit(solution)/shard_map/terms/pallas_call | solution.py:57
  38.5 0.8 %collective-permute-start.17 = (bf16[3,24,768]{2,1,0:T(8,128)(2,1)S(1)}, bf16[3,24,768]{2,1,0:T(8,128)(2,1)S(1)}, u32[]{:S(2)}, u32[]{:S(2)}) collective-permute-start(bf16[3,24,768]{2,1,0:T(8,128)(2,1)S(1)} %get-tuple-element.68), channel_id=1, source_target_pairs={{0,24},{1,25},{2,26},{3,27},{4,28},{5,29},{6,30},{7,31},{8,16},{9,... | collective-permute-start | bytes 331784 | tf_op jit(solution)/shard_map/ppermute | solution.py:22
  39.3 2.1 %collective-permute-start.16 = (bf16[3,24,768]{2,1,0:T(8,128)(2,1)S(1)}, bf16[3,24,768]{2,1,0:T(8,128)(2,1)S(1)}, u32[]{:S(2)}, u32[]{:S(2)}) collective-permute-start(bf16[3,24,768]{2,1,0:T(8,128)(2,1)S(1)} %get-tuple-element.67), channel_id=1, source_target_pairs={{0,16},{1,17},{2,18},{3,19},{4,20},{5,21},{6,22},{7,23},{8,24},{9,... | collective-permute-start | bytes 331784 | tf_op jit(solution)/shard_map/ppermute | solution.py:22
  41.4 0.7 %collective-permute-start.15 = (bf16[3,24,768]{2,1,0:T(8,128)(2,1)S(1)}, bf16[3,24,768]{2,1,0:T(8,128)(2,1)S(1)}, u32[]{:S(2)}, u32[]{:S(2)}) collective-permute-start(bf16[3,24,768]{2,1,0:T(8,128)(2,1)S(1)} %get-tuple-element.66), channel_id=1, source_target_pairs={{0,8},{1,9},{2,10},{3,11},{4,12},{5,13},{6,14},{7,15},{8,0},{9,1},... | collective-permute-start | bytes 331784 | tf_op jit(solution)/shard_map/ppermute | solution.py:22
  42.1 1.5 %collective-permute-start.13 = (bf16[128,768]{1,0:T(8,128)(2,1)S(1)}, bf16[128,768]{1,0:T(8,128)(2,1)S(1)}, u32[]{:S(2)}, u32[]{:S(2)}) collective-permute-start(bf16[128,768]{1,0:T(8,128)(2,1)S(1)} %get-tuple-element.64.middle), channel_id=1, source_target_pairs={{0,2},{1,3},{2,0},{3,1},{4,6},{5,7},{6,4},{7,5},{8,10},{9,11},{10,... | collective-permute-start | bytes 589832 | tf_op jit(solution)/shard_map/ppermute | solution.py:22
  43.6 3.9 %collective-permute-start.14 = (bf16[128,768]{1,0:T(8,128)(2,1)S(1)}, bf16[128,768]{1,0:T(8,128)(2,1)S(1)}, u32[]{:S(2)}, u32[]{:S(2)}) collective-permute-start(bf16[128,768]{1,0:T(8,128)(2,1)S(1)} %get-tuple-element.64.middle), channel_id=1, source_target_pairs={{2,4},{3,5},{4,2},{5,3},{6,8},{7,9},{8,6},{9,7},{10,12},{11,13},{1... | collective-permute-start | bytes 589832 | tf_op jit(solution)/shard_map/ppermute | solution.py:22
  47.6 1.2 %second_forward.1 = bf16[128,768]{1,0:T(8,128)(2,1)} custom-call(bf16[128,768]{1,0:T(8,128)(2,1)S(1)} %collective-permute-done.6.refs_0_, bf16[128,768]{1,0:T(8,128)(2,1)S(1)} %get-tuple-element.51.refs_1_, bf16[128,768]{1,0:T(8,128)(2,1)S(1)} %get-tuple-element.53.refs_2_, bf16[3,768,768]{2,1,0:T(8,128)(2,1)S(1)} %get-tuple-element.44.refs_4_.refs_3_), custom_call_target="tpu_custom_call" | custom-call | tf_op jit(solution)/shard_map/second_forward/pallas_call | solution.py:57
  48.7 0.7 %add_bitcast_fusion = f32[3,768,24]{1,2,0:T(8,128)} fusion(f32[3,24,768]{2,1,0:T(8,128)S(1)} %get-tuple-element.63, bf16[3,24,768]{2,1,0:T(8,128)(2,1)S(1)} %collective-permute-done.17, bf16[3,24,768]{2,1,0:T(8,128)(2,1)S(1)} %collective-permute-done.16, bf16[3,24,768]{2,1,0:T(8,128)(2,1)S(1)} %collective-permute-done.15), kind=kLoop, calls=%fused_computation.10 | loop fusion | flops 331776 | bytes 774144 | tf_op jit(solution)/shard_map/transpose | solution.py:274
  49.5 1.6 %collective-permute-done.13.flip = bf16[128,768]{1,0:T(8,128)(2,1)S(1)} collective-permute-done((bf16[128,768]{1,0:T(8,128)(2,1)S(1)}, bf16[128,768]{1,0:T(8,128)(2,1)S(1)}, u32[]{:S(2)}, u32[]{:S(2)}) %collective-permute-start.13) | collective-permute-done | bytes 196640 | tf_op jit(solution)/shard_map/ppermute | solution.py:22
  51.0 3.8 %collective-permute-done.14.step = bf16[128,768]{1,0:T(8,128)(2,1)S(1)} collective-permute-done((bf16[128,768]{1,0:T(8,128)(2,1)S(1)}, bf16[128,768]{1,0:T(8,128)(2,1)S(1)}, u32[]{:S(2)}, u32[]{:S(2)}) %collective-permute-start.14) | collective-permute-done | bytes 196640 | tf_op jit(solution)/shard_map/ppermute | solution.py:22
  54.8 2.0 %first_backward.1 = bf16[128,768]{1,0:T(8,128)(2,1)} custom-call(bf16[128,768]{1,0:T(8,128)(2,1)S(1)} %get-tuple-element.64.middle, bf16[128,768]{1,0:T(8,128)(2,1)S(1)} %collective-permute-done.13.flip, bf16[128,768]{1,0:T(8,128)(2,1)S(1)} %collective-permute-done.14.step, bf16[128,768]{1,0:T(8,128)(2,1)S(1)} %get-tuple-element.65.features, ...), custom_call_target="tpu_custom_call" | custom-call | tf_op jit(solution)/shard_map/first_backward/pallas_call | solution.py:57
  (19 shorter events, 0.5 us)
Async XLA Ops:
  1.7 15.8 %collective-permute-start = (bf16[128,768]{1,0:T(8,128)(2,1)S(1)}, bf16[128,768]{1,0:T(8,128)(2,1)S(1)}, u32[]{:S(2)}, u32[]{:S(2)}) collective-permute-start(bf16[128,768]{1,0:T(8,128)(2,1)S(1)} %fusion.5.acts), channel_id=1, source_target_pairs={{2,4},{3,5},{4,2},{5,3},{6,8},{7,9},{8,6},{9,7},{10,12},{11,13},{1... | collective-permute-start | bytes 589832 | tf_op jit(solution)/shard_map/ppermute | solution.py:22
  6.0 11.5 %collective-permute-start.1 = (bf16[128,768]{1,0:T(8,128)(2,1)S(1)}, bf16[128,768]{1,0:T(8,128)(2,1)S(1)}, u32[]{:S(2)}, u32[]{:S(2)}) collective-permute-start(bf16[128,768]{1,0:T(8,128)(2,1)S(1)} %fusion.5.acts), channel_id=1, source_target_pairs={{0,2},{1,3},{2,0},{3,1},{4,6},{5,7},{6,4},{7,5},{8,10},{9,11},{10,... | collective-permute-start | bytes 589832 | tf_op jit(solution)/shard_map/ppermute | solution.py:22
  6.7 12.0 %collective-permute-start.4 = (bf16[128,768]{1,0:T(8,128)(2,1)}, bf16[128,768]{1,0:T(8,128)(2,1)S(1)}, u32[]{:S(2)}, u32[]{:S(2)}) collective-permute-start(bf16[128,768]{1,0:T(8,128)(2,1)} %up.1), channel_id=1, source_target_pairs={{0,16},{1,17},{2,18},{3,19},{4,20},{5,21},{6,22},{7,23},{8,24},{9,... | collective-permute-start | bytes 589832 | tf_op jit(solution)/shard_map/ppermute | solution.py:22
  7.0 12.3 %collective-permute-start.2 = (bf16[128,768]{1,0:T(8,128)(2,1)S(1)}, bf16[128,768]{1,0:T(8,128)(2,1)S(1)}, u32[]{:S(2)}, u32[]{:S(2)}) collective-permute-start(bf16[128,768]{1,0:T(8,128)(2,1)S(1)} %fusion.5.acts), channel_id=1, source_target_pairs={{0,4},{1,5},{2,6},{3,7},{4,0},{5,1},{6,2},{7,3},{8,12},{9,13},{10,... | collective-permute-start | bytes 589832 | tf_op jit(solution)/shard_map/ppermute | solution.py:22
  8.5 12.0 %collective-permute-start.3 = (bf16[128,768]{1,0:T(8,128)(2,1)S(1)}, bf16[128,768]{1,0:T(8,128)(2,1)S(1)}, u32[]{:S(2)}, u32[]{:S(2)}) collective-permute-start(bf16[128,768]{1,0:T(8,128)(2,1)S(1)} %fusion.5.acts), channel_id=1, source_target_pairs={{0,6},{1,7},{6,0},{7,1},{8,14},{9,15},{14,8},{15,9},{16,22},{17,23... | collective-permute-start | bytes 589832 | tf_op jit(solution)/shard_map/ppermute | solution.py:22
  20.6 13.9 %collective-permute-start.5 = (bf16[512,768]{1,0:T(8,128)(2,1)S(1)}, bf16[512,768]{1,0:T(8,128)(2,1)S(1)}, u32[]{:S(2)}, u32[]{:S(2)}) collective-permute-start(bf16[512,768]{1,0:T(8,128)(2,1)S(1)} %line.1), channel_id=1, source_target_pairs={{0,1},{1,0},{2,3},{3,2},{4,5},{5,4},{6,7},{7,6},{8,9},{9,8},{10,11... | collective-permute-start | bytes 2359304 | tf_op jit(solution)/shard_map/ppermute | solution.py:22
  20.6 5.7 %collective-permute-start.9 = (bf16[2,96,128]{2,1,0:T(8,128)(2,1)S(1)}, bf16[2,96,128]{2,1,0:T(8,128)(2,1)S(1)}, u32[]{:S(2)}, u32[]{:S(2)}) collective-permute-start(bf16[2,96,128]{2,1,0:T(8,128)(2,1)S(1)} %get-tuple-element.58), channel_id=1, source_target_pairs={{0,6},{1,7},{2,4},{3,5},{4,2},{5,3},{6,0},{7,1},{8,14},{9,15},{10,... | collective-permute-start | bytes 147464 | tf_op jit(solution)/shard_map/ppermute | solution.py:22
  22.9 4.1 %collective-permute-start.8 = (bf16[2,96,128]{2,1,0:T(8,128)(2,1)S(1)}, bf16[2,96,128]{2,1,0:T(8,128)(2,1)S(1)}, u32[]{:S(2)}, u32[]{:S(2)}) collective-permute-start(bf16[2,96,128]{2,1,0:T(8,128)(2,1)S(1)} %get-tuple-element.57), channel_id=1, source_target_pairs={{0,4},{1,5},{2,6},{3,7},{4,0},{5,1},{6,2},{7,3},{8,12},{9,13},{10,... | collective-permute-start | bytes 147464 | tf_op jit(solution)/shard_map/ppermute | solution.py:22
  22.9 4.1 %collective-permute-start.7 = (bf16[2,96,128]{2,1,0:T(8,128)(2,1)S(1)}, bf16[2,96,128]{2,1,0:T(8,128)(2,1)S(1)}, u32[]{:S(2)}, u32[]{:S(2)}) collective-permute-start(bf16[2,96,128]{2,1,0:T(8,128)(2,1)S(1)} %get-tuple-element.56), channel_id=1, source_target_pairs={{0,2},{1,3},{2,0},{3,1},{4,6},{5,7},{6,4},{7,5},{8,10},{9,11},{10,... | collective-permute-start | bytes 147464 | tf_op jit(solution)/shard_map/ppermute | solution.py:22
  24.2 10.2 %collective-permute-start.6 = (bf16[128,768]{1,0:T(8,128)(2,1)S(1)}, bf16[128,768]{1,0:T(8,128)(2,1)S(1)}, u32[]{:S(2)}, u32[]{:S(2)}) collective-permute-start(bf16[128,768]{1,0:T(8,128)(2,1)S(1)} %get-tuple-element.51.refs_1_), channel_id=1, source_target_pairs={{0,16},{1,17},{2,18},{3,19},{4,20},{5,21},{6,22},{7,23},{8,24},{9,... | collective-permute-start | bytes 589832 | tf_op jit(solution)/shard_map/ppermute | solution.py:22
  27.0 1.4 %collective-permute-start.10 = (bf16[4,96,128]{2,1,0:T(8,128)(2,1)S(1)}, bf16[4,96,128]{2,1,0:T(8,128)(2,1)S(1)}, u32[]{:S(2)}, u32[]{:S(2)}) collective-permute-start(bf16[4,96,128]{2,1,0:T(8,128)(2,1)S(1)} %pad_maximum_fusion), channel_id=1, source_target_pairs={{0,1},{1,0},{2,3},{3,2},{4,5},{5,4},{6,7},{7,6},{8,9},{9,8},{10,11... | collective-permute-start | bytes 294920 | tf_op jit(solution)/shard_map/ppermute | solution.py:22
  28.6 8.2 %collective-permute-start.11 = (bf16[2,96,128]{2,1,0:T(8,128)(2,1)S(1)}, bf16[2,96,128]{2,1,0:T(8,128)(2,1)S(1)}, u32[]{:S(2)}, u32[]{:S(2)}) collective-permute-start(bf16[2,96,128]{2,1,0:T(8,128)(2,1)S(1)} %get-tuple-element.60), channel_id=1, source_target_pairs={{0,8},{1,9},{2,10},{3,11},{4,12},{5,13},{6,14},{7,15},{8,16},{9,17... | collective-permute-start | bytes 147464 | tf_op jit(solution)/shard_map/ppermute | solution.py:22
  31.8 6.0 %collective-permute-start.12 = (bf16[2,96,128]{2,1,0:T(8,128)(2,1)S(1)}, bf16[2,96,128]{2,1,0:T(8,128)(2,1)S(1)}, u32[]{:S(2)}, u32[]{:S(2)}) collective-permute-start(bf16[2,96,128]{2,1,0:T(8,128)(2,1)S(1)} %get-tuple-element.61), channel_id=1, source_target_pairs={{8,0},{9,1},{10,2},{11,3},{12,4},{13,5},{14,6},{15,7},{16,8},{17,9... | collective-permute-start | bytes 147464 | tf_op jit(solution)/shard_map/ppermute | solution.py:22
  38.5 10.2 %collective-permute-start.17 = (bf16[3,24,768]{2,1,0:T(8,128)(2,1)S(1)}, bf16[3,24,768]{2,1,0:T(8,128)(2,1)S(1)}, u32[]{:S(2)}, u32[]{:S(2)}) collective-permute-start(bf16[3,24,768]{2,1,0:T(8,128)(2,1)S(1)} %get-tuple-element.68), channel_id=1, source_target_pairs={{0,24},{1,25},{2,26},{3,27},{4,28},{5,29},{6,30},{7,31},{8,16},{9,... | collective-permute-start | bytes 331784 | tf_op jit(solution)/shard_map/ppermute | solution.py:22
  39.3 9.5 %collective-permute-start.16 = (bf16[3,24,768]{2,1,0:T(8,128)(2,1)S(1)}, bf16[3,24,768]{2,1,0:T(8,128)(2,1)S(1)}, u32[]{:S(2)}, u32[]{:S(2)}) collective-permute-start(bf16[3,24,768]{2,1,0:T(8,128)(2,1)S(1)} %get-tuple-element.67), channel_id=1, source_target_pairs={{0,16},{1,17},{2,18},{3,19},{4,20},{5,21},{6,22},{7,23},{8,24},{9,... | collective-permute-start | bytes 331784 | tf_op jit(solution)/shard_map/ppermute | solution.py:22
  41.4 7.4 %collective-permute-start.15 = (bf16[3,24,768]{2,1,0:T(8,128)(2,1)S(1)}, bf16[3,24,768]{2,1,0:T(8,128)(2,1)S(1)}, u32[]{:S(2)}, u32[]{:S(2)}) collective-permute-start(bf16[3,24,768]{2,1,0:T(8,128)(2,1)S(1)} %get-tuple-element.66), channel_id=1, source_target_pairs={{0,8},{1,9},{2,10},{3,11},{4,12},{5,13},{6,14},{7,15},{8,0},{9,1},... | collective-permute-start | bytes 331784 | tf_op jit(solution)/shard_map/ppermute | solution.py:22
  42.1 9.0 %collective-permute-start.13 = (bf16[128,768]{1,0:T(8,128)(2,1)S(1)}, bf16[128,768]{1,0:T(8,128)(2,1)S(1)}, u32[]{:S(2)}, u32[]{:S(2)}) collective-permute-start(bf16[128,768]{1,0:T(8,128)(2,1)S(1)} %get-tuple-element.64.middle), channel_id=1, source_target_pairs={{0,2},{1,3},{2,0},{3,1},{4,6},{5,7},{6,4},{7,5},{8,10},{9,11},{10,... | collective-permute-start | bytes 589832 | tf_op jit(solution)/shard_map/ppermute | solution.py:22
  43.6 11.2 %collective-permute-start.14 = (bf16[128,768]{1,0:T(8,128)(2,1)S(1)}, bf16[128,768]{1,0:T(8,128)(2,1)S(1)}, u32[]{:S(2)}, u32[]{:S(2)}) collective-permute-start(bf16[128,768]{1,0:T(8,128)(2,1)S(1)} %get-tuple-element.64.middle), channel_id=1, source_target_pairs={{2,4},{3,5},{4,2},{5,3},{6,8},{7,9},{8,6},{9,7},{10,12},{11,13},{1... | collective-permute-start | bytes 589832 | tf_op jit(solution)/shard_map/ppermute | solution.py:22

commit v4 on v3

--- a/solution.py
+++ b/solution.py
@@ -41,6 +41,10 @@
 def gelu_pair(values):
     wide = values.astype(F32)
     return jax.jvp(jax.nn.gelu, (wide,), (jnp.ones_like(wide),))
+
+
+def gelu(ref):
+    return jax.nn.gelu(ref[...].astype(F32)).astype(BF16)
 
 
 def dot(a, b):
@@ -81,6 +85,7 @@
     for copy in copies:
         copy.start()
     copies[0].wait()
+    acts[...] = gelu(values)
     copies[1].wait()
     conv[...] = values[...].astype(F32) + dot(acts[...], held[1])
     copies[2].wait()
@@ -90,9 +95,12 @@
         copy.wait()
 
 
-def forward_body(flip, step, conv, taps, output, acts_second, slope):
+def forward_body(flip, step, conv, taps, output, acts_second, slope, flip_acts, step_acts):
     odd = position(flip.shape[0])[0] & 1
-    result = conv[...] + dot(step[...], taps[2 * odd]) + dot(flip[...], taps[2 - 2 * odd])
+    flip_acts[...] = gelu(flip)
+    step_acts[...] = gelu(step)
+    result = conv[...] + dot(step_acts[...], taps[2 * odd])
+    result = result + dot(flip_acts[...], taps[2 - 2 * odd])
     result = result.astype(BF16)
     output[...] = result
     activated, steep = gelu_pair(result)
@@ -124,8 +132,9 @@
 def line_body(acts, flip, step, cross, turn, line):
     rows = acts.shape[0]
     chip = position(rows)[0]
-    for slot, piece in enumerate((acts, flip, cross)):
+    for slot, piece in enumerate((acts, flip)):
         line[pl.ds((chip ^ slot) * rows, rows)] = piece[...]
+    line[pl.ds((chip ^ 2) * rows, rows)] = gelu(cross)
     inner = (chip == 1) | (chip == 2)
 
     @pl.when(inner)
@@ -134,7 +143,7 @@
 
     @pl.when(jnp.logical_not(inner))
     def _():
-        line[pl.ds((chip ^ 3) * rows, rows)] = turn[...]
+        line[pl.ds((chip ^ 3) * rows, rows)] = gelu(turn)
 
 
 def regroup_body(*refs):
@@ -196,12 +205,15 @@
     output[...] = (output_first[...].astype(F32) + conv).astype(BF16)
 
 
-def first_backward(middle, flip, step, features, taps, output):
+def early_backward(middle, features, taps, partial, slope):
+    slope[...] = gelu_pair(features[...])[1]
+    partial[...] = dot_t(middle[...], taps[1])
+
+
+def first_backward(middle, flip, step, partial, slope, taps, output):
     odd = position(middle.shape[0])[0] & 1
-    back = dot_t(middle[...], taps[1])
-    back = back + dot_t(step[...], taps[2 - 2 * odd]) + dot_t(flip[...], taps[2 * odd])
-    slope = gelu_pair(features[...])[1]
-    output[...] = (middle[...].astype(F32) + slope * back).astype(BF16)
+    back = partial[...] + dot_t(step[...], taps[2 - 2 * odd]) + dot_t(flip[...], taps[2 * odd])
+    output[...] = (middle[...].astype(F32) + slope[...] * back).astype(BF16)
 
 
 def local(features, first_taps, second_taps, upstream):
@@ -215,19 +227,18 @@
     part = ((2, group, rows), BF16)
     together = lax.optimization_barrier
 
-    acts = gelu_pair(features)[0].astype(BF16)
     far_up = far_pieces(upstream)
-    conv, back, first_taps, second_taps, features, upstream = call(
-        load_body, "load", [wide, wide, all_taps, all_taps, block, block],
-        acts, held=(features, upstream, first_taps, second_taps),
+    flip, step = flipped(features), stepped(features)
+    cross = moved(features, lambda i: i ^ 4)
+    turn = moved(features, lambda i: i ^ 6 if (i // 2) % 4 in (0, 3) else None)
+    acts, conv, back, first_taps, second_taps, features, upstream = call(
+        load_body, "load", [block, wide, wide, all_taps, all_taps, block, block],
+        held=(features, upstream, first_taps, second_taps),
         scratch=[pltpu.SemaphoreType.DMA((8,))],
     )
-    flip, step = flipped(acts), stepped(acts)
-    cross = moved(acts, lambda i: i ^ 4)
-    turn = moved(acts, lambda i: i ^ 6 if (i // 2) % 4 in (0, 3) else None)
     step, flip, conv = together((step, flip, conv))
-    output_first, acts_second, slope = call(
-        forward_body, "forward", [block, block, wide], flip, step, conv, first_taps
+    output_first, acts_second, slope, flip, step = call(
+        forward_body, "forward", [block, block, wide, block, block], flip, step, conv, first_taps
     )
     middle, *parts = call(
         functools.partial(middle_body, planes=planes), "middle",
@@ -273,13 +284,16 @@
         total = lax.psum_scatter(terms[0], "seq", scatter_dimension=1, axis_index_groups=lines)
     first_taps_gradient = jnp.swapaxes(total, 1, 2)
 
+    partial, slope_first = call(
+        early_backward, "early_backward", [wide, wide], late, features, first_taps
+    )
     (second_layer_output,) = call(
         second_forward, "second_forward", [block],
         *far_second, acts_second, output_first, second_taps,
     )
     (input_gradient,) = call(
         first_backward, "first_backward", [block],
-        middle, middle_flip, middle_step, features, first_taps,
+        middle, middle_flip, middle_step, partial, slope_first, first_taps,
     )
     return second_layer_output, input_gradient, first_taps_gradient
 

time: 57.1 us -> 56 us (0.981)
  other arithmetic: 1.83 us -> 0.76 us
  Pallas kernels: 8.71 us -> 9.34 us
  waiting for transfers between devices: 15.1 us -> 14.5 us
    convert_element_type x1 -> x0, other arithmetic: 1.07 us -> none  [local(): acts = gelu_pair(features)[0].astype(BF16)]
    pallas_call x8 -> x9, Pallas kernels: 8.71 us -> 9.34 us  [call(): pl.pallas_call(body, name=name, out_shape=[jax.ShapeDtypeStruct(shape, ki...]
    ppermute x18, waiting for transfers between devices: 15.1 us -> 14.5 us  [moved(): return lax.ppermute(array, 'seq', pairs)]
  transfers between devices with their start and end apart: 18 -> 18, of which waited for: 9 -> 9; matrix products, arithmetic and copies ran while one was open for 1% -> 1% of each run, Pallas kernels for 10% -> 12%
where the time goes in v4:
time: 56 us; the launch traced here: 55.8 us
  starting transfers between devices  30.4 us (54%)
  waiting for transfers between devices  14.5 us (26%)
  Pallas kernels  9.34 us (17%)
  between operations  0.79 us (1%)
  other arithmetic  0.76 us (1%)
    ppermute x18, starting transfers between devices, moved(): return lax.ppermute(array, 'seq', pairs)  30.4 us
    ppermute x18, waiting for transfers between devices, moved(): return lax.ppermute(array, 'seq', pairs)  14.5 us
    pallas_call x9, Pallas kernels, call(): pl.pallas_call(body, name=name, out_shape=[jax.ShapeDtypeStruct(shape, ki...  9.34 us
  transfers between devices with their start and end apart: 18, of which 9 were waited for; matrix products, arithmetic and copies ran while one was open for 1% of the time, Pallas kernels for 12%

profile of v4, /device:TPU:16, one launch (start us, length us, event | category | flops | bytes accessed | tf_op | source)
XLA Modules:
  0.0 55.8 jit_solution(13812595079373854906)
XLA Ops:
  0.6 4.2 %collective-permute-start = (bf16[128,768]{1,0:T(8,128)(2,1)}, bf16[128,768]{1,0:T(8,128)(2,1)S(1)}, u32[]{:S(2)}, u32[]{:S(2)}) collective-permute-start(bf16[128,768]{1,0:T(8,128)(2,1)} %features.1), channel_id=1, source_target_pairs={{2,4},{3,5},{4,2},{5,3},{6,8},{7,9},{8,6},{9,7},{10,12},{11,13},{1... | collective-permute-start | bytes 589832 | tf_op jit(solution)/shard_map/ppermute | solution.py:22
  4.9 0.7 %collective-permute-start.1 = (bf16[128,768]{1,0:T(8,128)(2,1)}, bf16[128,768]{1,0:T(8,128)(2,1)S(1)}, u32[]{:S(2)}, u32[]{:S(2)}) collective-permute-start(bf16[128,768]{1,0:T(8,128)(2,1)} %features.1), channel_id=1, source_target_pairs={{0,2},{1,3},{2,0},{3,1},{4,6},{5,7},{6,4},{7,5},{8,10},{9,11},{10,... | collective-permute-start | bytes 589832 | tf_op jit(solution)/shard_map/ppermute | solution.py:22
  5.6 0.3 collective-permute-start.4
  5.9 1.5 %collective-permute-start.2 = (bf16[128,768]{1,0:T(8,128)(2,1)}, bf16[128,768]{1,0:T(8,128)(2,1)S(1)}, u32[]{:S(2)}, u32[]{:S(2)}) collective-permute-start(bf16[128,768]{1,0:T(8,128)(2,1)} %features.1), channel_id=1, source_target_pairs={{0,4},{1,5},{2,6},{3,7},{4,0},{5,1},{6,2},{7,3},{8,12},{9,13},{10,... | collective-permute-start | bytes 589832 | tf_op jit(solution)/shard_map/ppermute | solution.py:22
  7.5 2.9 %collective-permute-start.3 = (bf16[128,768]{1,0:T(8,128)(2,1)}, bf16[128,768]{1,0:T(8,128)(2,1)S(1)}, u32[]{:S(2)}, u32[]{:S(2)}) collective-permute-start(bf16[128,768]{1,0:T(8,128)(2,1)} %features.1), channel_id=1, source_target_pairs={{0,6},{1,7},{6,0},{7,1},{8,14},{9,15},{14,8},{15,9},{16,22},{17,23... | collective-permute-start | bytes 589832 | tf_op jit(solution)/shard_map/ppermute | solution.py:22
  10.3 3.3 %load.1 = (bf16[128,768]{1,0:T(8,128)(2,1)S(1)}, f32[128,768]{1,0:T(8,128)S(1)}, f32[128,768]{1,0:T(8,128)S(1)}, bf16[3,768,768]{2,1,0:T(8,128)(2,1)S(1)}, bf16[...) custom-call(bf16[128,768]{1,0:T(8,128)(2,1)} %features.1, ...), custom_call_target="tpu_custom_call" | custom-call | tf_op jit(solution)/shard_map/load/pallas_call | solution.py:61
  13.6 3.0 %collective-permute-done.step = bf16[128,768]{1,0:T(8,128)(2,1)S(1)} collective-permute-done((bf16[128,768]{1,0:T(8,128)(2,1)}, bf16[128,768]{1,0:T(8,128)(2,1)S(1)}, u32[]{:S(2)}, u32[]{:S(2)}) %collective-permute-start) | collective-permute-done | bytes 196640 | tf_op jit(solution)/shard_map/ppermute | solution.py:22
  16.6 0.7 %forward.1 = (bf16[128,768]{1,0:T(8,128)(2,1)S(1)}, bf16[128,768]{1,0:T(8,128)(2,1)S(1)}, f32[128,768]{1,0:T(8,128)S(1)}, bf16[128,768]{1,0:T(8,128)(2,1)S(1)}, bf16[128,768]{1,0:T(8,128)(2,1)S(1)}) custom-call(bf16[128,768]{1,0:T(8,128)(2,1)S(1)} %collective-permute-done.1.flip, bf16[128,768]{1,0:T(8,128)(2,1)S(1)} %collective-permute-done.step, ...), custom_call_target="tpu_custom_call" | custom-call | tf_op jit(solution)/shard_map/forward/pallas_call | solution.py:61
  17.3 0.5 collective-permute-done.4.refs_0_
  17.8 0.7 %middle.1 = (bf16[128,768]{1,0:T(8,128)(2,1)S(1)}, bf16[2,96,128]{2,1,0:T(8,128)(2,1)S(1)}, bf16[2,96,128]{2,1,0:T(8,128)(2,1)S(1)}, bf16[2,96,128]{2,1,0:T(8,128)(2,1)S(1)}, bf16[2,96,128]{2,1,0:T(8,128)(2,1)S(1)}) custom-call(bf16[128,768]{1,0:T(8,128)(2,1)S(1)} %collective-permute-done.4.refs_0_, f32[128,768]{1,0:T(8,128)S(1)} %get-tuple-element.49.refs_1_, ...), custom_call_target="tpu_custom_call" | custom-call | tf_op jit(solution)/shard_map/middle/pallas_call | solution.py:61
  18.5 1.2 %collective-permute-done.3.turn = bf16[128,768]{1,0:T(8,128)(2,1)S(1)} collective-permute-done((bf16[128,768]{1,0:T(8,128)(2,1)}, bf16[128,768]{1,0:T(8,128)(2,1)S(1)}, u32[]{:S(2)}, u32[]{:S(2)}) %collective-permute-start.3) | collective-permute-done | bytes 196640 | tf_op jit(solution)/shard_map/ppermute | solution.py:22
  20.0 2.2 %collective-permute-start.9 = (bf16[2,96,128]{2,1,0:T(8,128)(2,1)S(1)}, bf16[2,96,128]{2,1,0:T(8,128)(2,1)S(1)}, u32[]{:S(2)}, u32[]{:S(2)}) collective-permute-start(bf16[2,96,128]{2,1,0:T(8,128)(2,1)S(1)} %get-tuple-element.66), channel_id=1, source_target_pairs={{0,6},{1,7},{2,4},{3,5},{4,2},{5,3},{6,0},{7,1},{8,14},{9,15},{10,... | collective-permute-start | bytes 147464 | tf_op jit(solution)/shard_map/ppermute | solution.py:22
  22.3 1.3 %collective-permute-start.7 = (bf16[2,96,128]{2,1,0:T(8,128)(2,1)S(1)}, bf16[2,96,128]{2,1,0:T(8,128)(2,1)S(1)}, u32[]{:S(2)}, u32[]{:S(2)}) collective-permute-start(bf16[2,96,128]{2,1,0:T(8,128)(2,1)S(1)} %get-tuple-element.64), channel_id=1, source_target_pairs={{0,2},{1,3},{2,0},{3,1},{4,6},{5,7},{6,4},{7,5},{8,10},{9,11},{10,... | collective-permute-start | bytes 147464 | tf_op jit(solution)/shard_map/ppermute | solution.py:22
  23.6 2.1 %collective-permute-start.6 = (bf16[128,768]{1,0:T(8,128)(2,1)S(1)}, bf16[128,768]{1,0:T(8,128)(2,1)S(1)}, u32[]{:S(2)}, u32[]{:S(2)}) collective-permute-start(bf16[128,768]{1,0:T(8,128)(2,1)S(1)} %get-tuple-element.59.refs_1_), channel_id=1, source_target_pairs={{0,16},{1,17},{2,18},{3,19},{4,20},{5,21},{6,22},{7,23},{8,24},{9,... | collective-permute-start | bytes 589832 | tf_op jit(solution)/shard_map/ppermute | solution.py:22
  25.7 0.6 %collective-permute-done.8.refs_2_ = bf16[2,96,128]{2,1,0:T(8,128)(2,1)S(1)} collective-permute-done((bf16[2,96,128]{2,1,0:T(8,128)(2,1)S(1)}, bf16[2,96,128]{2,1,0:T(8,128)(2,1)S(1)}, u32[]{:S(2)}, u32[]{:S(2)}) %collective-permute-start.8) | collective-permute-done | bytes 49184 | tf_op jit(solution)/shard_map/ppermute | solution.py:22
  26.5 1.3 %collective-permute-done.10.refs_4_ = bf16[4,96,128]{2,1,0:T(8,128)(2,1)S(1)} collective-permute-done((bf16[4,96,128]{2,1,0:T(8,128)(2,1)S(1)}, bf16[4,96,128]{2,1,0:T(8,128)(2,1)S(1)}, u32[]{:S(2)}, u32[]{:S(2)}) %collective-permute-start.10) | collective-permute-done | bytes 98336 | tf_op jit(solution)/shard_map/ppermute | solution.py:22
  28.0 3.2 %collective-permute-start.11 = (bf16[2,96,128]{2,1,0:T(8,128)(2,1)S(1)}, bf16[2,96,128]{2,1,0:T(8,128)(2,1)S(1)}, u32[]{:S(2)}, u32[]{:S(2)}) collective-permute-start(bf16[2,96,128]{2,1,0:T(8,128)(2,1)S(1)} %get-tuple-element.68), channel_id=1, source_target_pairs={{0,8},{1,9},{2,10},{3,11},{4,12},{5,13},{6,14},{7,15},{8,16},{9,17... | collective-permute-start | bytes 147464 | tf_op jit(solution)/shard_map/ppermute | solution.py:22
  31.2 2.6 %collective-permute-start.12 = (bf16[2,96,128]{2,1,0:T(8,128)(2,1)S(1)}, bf16[2,96,128]{2,1,0:T(8,128)(2,1)S(1)}, u32[]{:S(2)}, u32[]{:S(2)}) collective-permute-start(bf16[2,96,128]{2,1,0:T(8,128)(2,1)S(1)} %get-tuple-element.69), channel_id=1, source_target_pairs={{8,0},{9,1},{10,2},{11,3},{12,4},{13,5},{14,6},{15,7},{16,8},{17,9... | collective-permute-start | bytes 147464 | tf_op jit(solution)/shard_map/ppermute | solution.py:22
  33.8 2.4 %collective-permute-done.11.behind = bf16[2,96,128]{2,1,0:T(8,128)(2,1)S(1)} collective-permute-done((bf16[2,96,128]{2,1,0:T(8,128)(2,1)S(1)}, bf16[2,96,128]{2,1,0:T(8,128)(2,1)S(1)}, u32[]{:S(2)}, u32[]{:S(2)}) %collective-permute-start.11) | collective-permute-done | bytes 49184 | tf_op jit(solution)/shard_map/ppermute | solution.py:22
  36.2 1.0 %collective-permute-done.12.ahead = bf16[2,96,128]{2,1,0:T(8,128)(2,1)S(1)} collective-permute-done((bf16[2,96,128]{2,1,0:T(8,128)(2,1)S(1)}, bf16[2,96,128]{2,1,0:T(8,128)(2,1)S(1)}, u32[]{:S(2)}, u32[]{:S(2)}) %collective-permute-start.12) | collective-permute-done | bytes 49184 | tf_op jit(solution)/shard_map/ppermute | solution.py:22
  37.2 0.7 %terms.1 = (f32[3,24,768]{2,1,0:T(8,128)S(1)}, bf16[3,24,768]{2,1,0:T(8,128)(2,1)S(1)}, bf16[3,24,768]{2,1,0:T(8,128)(2,1)S(1)}, bf16[3,24,768]{2,1,0:T(8,128)(2,1)S(1)}) custom-call(bf16[2,96,512]{2,1,0:T(8,128)(2,1)S(1)} %get-tuple-element.67.cols, bf16[2,96,128]{2,1,0:T(8,128)(2,1)S(1)} %collective-permute-done.11.behind, ...), custom_call_target="tpu_custom_call" | custom-call | tf_op jit(solution)/shard_map/terms/pallas_call | solution.py:61
  37.9 0.8 %collective-permute-start.17 = (bf16[3,24,768]{2,1,0:T(8,128)(2,1)S(1)}, bf16[3,24,768]{2,1,0:T(8,128)(2,1)S(1)}, u32[]{:S(2)}, u32[]{:S(2)}) collective-permute-start(bf16[3,24,768]{2,1,0:T(8,128)(2,1)S(1)} %get-tuple-element.78), channel_id=1, source_target_pairs={{0,24},{1,25},{2,26},{3,27},{4,28},{5,29},{6,30},{7,31},{8,16},{9,... | collective-permute-start | bytes 331784 | tf_op jit(solution)/shard_map/ppermute | solution.py:22
  38.6 2.1 %collective-permute-start.16 = (bf16[3,24,768]{2,1,0:T(8,128)(2,1)S(1)}, bf16[3,24,768]{2,1,0:T(8,128)(2,1)S(1)}, u32[]{:S(2)}, u32[]{:S(2)}) collective-permute-start(bf16[3,24,768]{2,1,0:T(8,128)(2,1)S(1)} %get-tuple-element.77), channel_id=1, source_target_pairs={{0,16},{1,17},{2,18},{3,19},{4,20},{5,21},{6,22},{7,23},{8,24},{9,... | collective-permute-start | bytes 331784 | tf_op jit(solution)/shard_map/ppermute | solution.py:22
  40.8 0.7 %collective-permute-start.15 = (bf16[3,24,768]{2,1,0:T(8,128)(2,1)S(1)}, bf16[3,24,768]{2,1,0:T(8,128)(2,1)S(1)}, u32[]{:S(2)}, u32[]{:S(2)}) collective-permute-start(bf16[3,24,768]{2,1,0:T(8,128)(2,1)S(1)} %get-tuple-element.76), channel_id=1, source_target_pairs={{0,8},{1,9},{2,10},{3,11},{4,12},{5,13},{6,14},{7,15},{8,0},{9,1},... | collective-permute-start | bytes 331784 | tf_op jit(solution)/shard_map/ppermute | solution.py:22
  41.4 1.5 %collective-permute-start.13 = (bf16[128,768]{1,0:T(8,128)(2,1)S(1)}, bf16[128,768]{1,0:T(8,128)(2,1)S(1)}, u32[]{:S(2)}, u32[]{:S(2)}) collective-permute-start(bf16[128,768]{1,0:T(8,128)(2,1)S(1)} %get-tuple-element.72.middle), channel_id=1, source_target_pairs={{0,2},{1,3},{2,0},{3,1},{4,6},{5,7},{6,4},{7,5},{8,10},{9,11},{10,... | collective-permute-start | bytes 589832 | tf_op jit(solution)/shard_map/ppermute | solution.py:22
  43.0 3.9 %collective-permute-start.14 = (bf16[128,768]{1,0:T(8,128)(2,1)S(1)}, bf16[128,768]{1,0:T(8,128)(2,1)S(1)}, u32[]{:S(2)}, u32[]{:S(2)}) collective-permute-start(bf16[128,768]{1,0:T(8,128)(2,1)S(1)} %get-tuple-element.72.middle), channel_id=1, source_target_pairs={{2,4},{3,5},{4,2},{5,3},{6,8},{7,9},{8,6},{9,7},{10,12},{11,13},{1... | collective-permute-start | bytes 589832 | tf_op jit(solution)/shard_map/ppermute | solution.py:22
  46.9 0.8 %early_backward.1 = (f32[128,768]{1,0:T(8,128)S(1)}, f32[128,768]{1,0:T(8,128)S(1)}) custom-call(bf16[128,768]{1,0:T(8,128)(2,1)S(1)} %get-tuple-element.72.middle, bf16[128,768]{1,0:T(8,128)(2,1)S(1)} %get-tuple-element.73.features, bf16[3,768,768]{2,1,0:T(8,128)(2,1)S(1)} %get-tuple-element.46.taps), custom_call_target="tpu_custom_call" | custom-call | tf_op jit(solution)/shard_map/early_backward/pallas_call | solution.py:61
  47.7 1.2 %second_forward.1 = bf16[128,768]{1,0:T(8,128)(2,1)} custom-call(bf16[128,768]{1,0:T(8,128)(2,1)S(1)} %collective-permute-done.6.refs_0_, bf16[128,768]{1,0:T(8,128)(2,1)S(1)} %get-tuple-element.59.refs_1_, bf16[128,768]{1,0:T(8,128)(2,1)S(1)} %get-tuple-element.61.refs_2_, bf16[3,768,768]{2,1,0:T(8,128)(2,1)S(1)} %get-tuple-element.52.refs_4_.refs_3_), custom_call_target="tpu_custom_call" | custom-call | tf_op jit(solution)/shard_map/second_forward/pallas_call | solution.py:61
  48.9 0.7 %add_bitcast_fusion = f32[3,768,24]{1,2,0:T(8,128)} fusion(f32[3,24,768]{2,1,0:T(8,128)S(1)} %get-tuple-element.71, bf16[3,24,768]{2,1,0:T(8,128)(2,1)S(1)} %collective-permute-done.17, bf16[3,24,768]{2,1,0:T(8,128)(2,1)S(1)} %collective-permute-done.16, bf16[3,24,768]{2,1,0:T(8,128)(2,1)S(1)} %collective-permute-done.15), kind=kLoop, calls=%fused_computation | loop fusion | flops 331776 | bytes 774144 | tf_op jit(solution)/shard_map/transpose | solution.py:285
  49.6 0.8 %collective-permute-done.13.flip = bf16[128,768]{1,0:T(8,128)(2,1)S(1)} collective-permute-done((bf16[128,768]{1,0:T(8,128)(2,1)S(1)}, bf16[128,768]{1,0:T(8,128)(2,1)S(1)}, u32[]{:S(2)}, u32[]{:S(2)}) %collective-permute-start.13) | collective-permute-done | bytes 196640 | tf_op jit(solution)/shard_map/ppermute | solution.py:22
  50.4 3.8 %collective-permute-done.14.step = bf16[128,768]{1,0:T(8,128)(2,1)S(1)} collective-permute-done((bf16[128,768]{1,0:T(8,128)(2,1)S(1)}, bf16[128,768]{1,0:T(8,128)(2,1)S(1)}, u32[]{:S(2)}, u32[]{:S(2)}) %collective-permute-start.14) | collective-permute-done | bytes 196640 | tf_op jit(solution)/shard_map/ppermute | solution.py:22
  54.2 1.6 %first_backward.1 = bf16[128,768]{1,0:T(8,128)(2,1)} custom-call(bf16[128,768]{1,0:T(8,128)(2,1)S(1)} %get-tuple-element.72.middle, bf16[128,768]{1,0:T(8,128)(2,1)S(1)} %collective-permute-done.13.flip, bf16[128,768]{1,0:T(8,128)(2,1)S(1)} %collective-permute-done.14.step, f32[128,768]{1,0:T(8,128)S(1)} %get-tuple-element.74.partial, ...), custom_call_target="tpu_custom_call" | custom-call | tf_op jit(solution)/shard_map/first_backward/pallas_call | solution.py:61
  (19 shorter events, 0.7 us)
Async XLA Ops:
  0.6 16.0 %collective-permute-start = (bf16[128,768]{1,0:T(8,128)(2,1)}, bf16[128,768]{1,0:T(8,128)(2,1)S(1)}, u32[]{:S(2)}, u32[]{:S(2)}) collective-permute-start(bf16[128,768]{1,0:T(8,128)(2,1)} %features.1), channel_id=1, source_target_pairs={{2,4},{3,5},{4,2},{5,3},{6,8},{7,9},{8,6},{9,7},{10,12},{11,13},{1... | collective-permute-start | bytes 589832 | tf_op jit(solution)/shard_map/ppermute | solution.py:22
  4.9 11.7 %collective-permute-start.1 = (bf16[128,768]{1,0:T(8,128)(2,1)}, bf16[128,768]{1,0:T(8,128)(2,1)S(1)}, u32[]{:S(2)}, u32[]{:S(2)}) collective-permute-start(bf16[128,768]{1,0:T(8,128)(2,1)} %features.1), channel_id=1, source_target_pairs={{0,2},{1,3},{2,0},{3,1},{4,6},{5,7},{6,4},{7,5},{8,10},{9,11},{10,... | collective-permute-start | bytes 589832 | tf_op jit(solution)/shard_map/ppermute | solution.py:22
  5.6 12.2 %collective-permute-start.4 = (bf16[128,768]{1,0:T(8,128)(2,1)}, bf16[128,768]{1,0:T(8,128)(2,1)S(1)}, u32[]{:S(2)}, u32[]{:S(2)}) collective-permute-start(bf16[128,768]{1,0:T(8,128)(2,1)} %up.1), channel_id=1, source_target_pairs={{0,16},{1,17},{2,18},{3,19},{4,20},{5,21},{6,22},{7,23},{8,24},{9,... | collective-permute-start | bytes 589832 | tf_op jit(solution)/shard_map/ppermute | solution.py:22
  5.9 12.5 %collective-permute-start.2 = (bf16[128,768]{1,0:T(8,128)(2,1)}, bf16[128,768]{1,0:T(8,128)(2,1)S(1)}, u32[]{:S(2)}, u32[]{:S(2)}) collective-permute-start(bf16[128,768]{1,0:T(8,128)(2,1)} %features.1), channel_id=1, source_target_pairs={{0,4},{1,5},{2,6},{3,7},{4,0},{5,1},{6,2},{7,3},{8,12},{9,13},{10,... | collective-permute-start | bytes 589832 | tf_op jit(solution)/shard_map/ppermute | solution.py:22
  7.5 12.2 %collective-permute-start.3 = (bf16[128,768]{1,0:T(8,128)(2,1)}, bf16[128,768]{1,0:T(8,128)(2,1)S(1)}, u32[]{:S(2)}, u32[]{:S(2)}) collective-permute-start(bf16[128,768]{1,0:T(8,128)(2,1)} %features.1), channel_id=1, source_target_pairs={{0,6},{1,7},{6,0},{7,1},{8,14},{9,15},{14,8},{15,9},{16,22},{17,23... | collective-permute-start | bytes 589832 | tf_op jit(solution)/shard_map/ppermute | solution.py:22
  19.9 13.9 %collective-permute-start.5 = (bf16[512,768]{1,0:T(8,128)(2,1)S(1)}, bf16[512,768]{1,0:T(8,128)(2,1)S(1)}, u32[]{:S(2)}, u32[]{:S(2)}) collective-permute-start(bf16[512,768]{1,0:T(8,128)(2,1)S(1)} %line.1), channel_id=1, source_target_pairs={{0,1},{1,0},{2,3},{3,2},{4,5},{5,4},{6,7},{7,6},{8,9},{9,8},{10,11... | collective-permute-start | bytes 2359304 | tf_op jit(solution)/shard_map/ppermute | solution.py:22
  20.0 5.7 %collective-permute-start.9 = (bf16[2,96,128]{2,1,0:T(8,128)(2,1)S(1)}, bf16[2,96,128]{2,1,0:T(8,128)(2,1)S(1)}, u32[]{:S(2)}, u32[]{:S(2)}) collective-permute-start(bf16[2,96,128]{2,1,0:T(8,128)(2,1)S(1)} %get-tuple-element.66), channel_id=1, source_target_pairs={{0,6},{1,7},{2,4},{3,5},{4,2},{5,3},{6,0},{7,1},{8,14},{9,15},{10,... | collective-permute-start | bytes 147464 | tf_op jit(solution)/shard_map/ppermute | solution.py:22
  22.3 4.1 %collective-permute-start.8 = (bf16[2,96,128]{2,1,0:T(8,128)(2,1)S(1)}, bf16[2,96,128]{2,1,0:T(8,128)(2,1)S(1)}, u32[]{:S(2)}, u32[]{:S(2)}) collective-permute-start(bf16[2,96,128]{2,1,0:T(8,128)(2,1)S(1)} %get-tuple-element.65), channel_id=1, source_target_pairs={{0,4},{1,5},{2,6},{3,7},{4,0},{5,1},{6,2},{7,3},{8,12},{9,13},{10,... | collective-permute-start | bytes 147464 | tf_op jit(solution)/shard_map/ppermute | solution.py:22
  22.3 4.1 %collective-permute-start.7 = (bf16[2,96,128]{2,1,0:T(8,128)(2,1)S(1)}, bf16[2,96,128]{2,1,0:T(8,128)(2,1)S(1)}, u32[]{:S(2)}, u32[]{:S(2)}) collective-permute-start(bf16[2,96,128]{2,1,0:T(8,128)(2,1)S(1)} %get-tuple-element.64), channel_id=1, source_target_pairs={{0,2},{1,3},{2,0},{3,1},{4,6},{5,7},{6,4},{7,5},{8,10},{9,11},{10,... | collective-permute-start | bytes 147464 | tf_op jit(solution)/shard_map/ppermute | solution.py:22
  23.6 10.2 %collective-permute-start.6 = (bf16[128,768]{1,0:T(8,128)(2,1)S(1)}, bf16[128,768]{1,0:T(8,128)(2,1)S(1)}, u32[]{:S(2)}, u32[]{:S(2)}) collective-permute-start(bf16[128,768]{1,0:T(8,128)(2,1)S(1)} %get-tuple-element.59.refs_1_), channel_id=1, source_target_pairs={{0,16},{1,17},{2,18},{3,19},{4,20},{5,21},{6,22},{7,23},{8,24},{9,... | collective-permute-start | bytes 589832 | tf_op jit(solution)/shard_map/ppermute | solution.py:22
  26.4 1.4 %collective-permute-start.10 = (bf16[4,96,128]{2,1,0:T(8,128)(2,1)S(1)}, bf16[4,96,128]{2,1,0:T(8,128)(2,1)S(1)}, u32[]{:S(2)}, u32[]{:S(2)}) collective-permute-start(bf16[4,96,128]{2,1,0:T(8,128)(2,1)S(1)} %pad_maximum_fusion), channel_id=1, source_target_pairs={{0,1},{1,0},{2,3},{3,2},{4,5},{5,4},{6,7},{7,6},{8,9},{9,8},{10,11... | collective-permute-start | bytes 294920 | tf_op jit(solution)/shard_map/ppermute | solution.py:22
  28.0 8.2 %collective-permute-start.11 = (bf16[2,96,128]{2,1,0:T(8,128)(2,1)S(1)}, bf16[2,96,128]{2,1,0:T(8,128)(2,1)S(1)}, u32[]{:S(2)}, u32[]{:S(2)}) collective-permute-start(bf16[2,96,128]{2,1,0:T(8,128)(2,1)S(1)} %get-tuple-element.68), channel_id=1, source_target_pairs={{0,8},{1,9},{2,10},{3,11},{4,12},{5,13},{6,14},{7,15},{8,16},{9,17... | collective-permute-start | bytes 147464 | tf_op jit(solution)/shard_map/ppermute | solution.py:22
  31.2 6.0 %collective-permute-start.12 = (bf16[2,96,128]{2,1,0:T(8,128)(2,1)S(1)}, bf16[2,96,128]{2,1,0:T(8,128)(2,1)S(1)}, u32[]{:S(2)}, u32[]{:S(2)}) collective-permute-start(bf16[2,96,128]{2,1,0:T(8,128)(2,1)S(1)} %get-tuple-element.69), channel_id=1, source_target_pairs={{8,0},{9,1},{10,2},{11,3},{12,4},{13,5},{14,6},{15,7},{16,8},{17,9... | collective-permute-start | bytes 147464 | tf_op jit(solution)/shard_map/ppermute | solution.py:22
  37.9 11.0 %collective-permute-start.17 = (bf16[3,24,768]{2,1,0:T(8,128)(2,1)S(1)}, bf16[3,24,768]{2,1,0:T(8,128)(2,1)S(1)}, u32[]{:S(2)}, u32[]{:S(2)}) collective-permute-start(bf16[3,24,768]{2,1,0:T(8,128)(2,1)S(1)} %get-tuple-element.78), channel_id=1, source_target_pairs={{0,24},{1,25},{2,26},{3,27},{4,28},{5,29},{6,30},{7,31},{8,16},{9,... | collective-permute-start | bytes 331784 | tf_op jit(solution)/shard_map/ppermute | solution.py:22
  38.6 10.3 %collective-permute-start.16 = (bf16[3,24,768]{2,1,0:T(8,128)(2,1)S(1)}, bf16[3,24,768]{2,1,0:T(8,128)(2,1)S(1)}, u32[]{:S(2)}, u32[]{:S(2)}) collective-permute-start(bf16[3,24,768]{2,1,0:T(8,128)(2,1)S(1)} %get-tuple-element.77), channel_id=1, source_target_pairs={{0,16},{1,17},{2,18},{3,19},{4,20},{5,21},{6,22},{7,23},{8,24},{9,... | collective-permute-start | bytes 331784 | tf_op jit(solution)/shard_map/ppermute | solution.py:22
  40.8 8.1 %collective-permute-start.15 = (bf16[3,24,768]{2,1,0:T(8,128)(2,1)S(1)}, bf16[3,24,768]{2,1,0:T(8,128)(2,1)S(1)}, u32[]{:S(2)}, u32[]{:S(2)}) collective-permute-start(bf16[3,24,768]{2,1,0:T(8,128)(2,1)S(1)} %get-tuple-element.76), channel_id=1, source_target_pairs={{0,8},{1,9},{2,10},{3,11},{4,12},{5,13},{6,14},{7,15},{8,0},{9,1},... | collective-permute-start | bytes 331784 | tf_op jit(solution)/shard_map/ppermute | solution.py:22
  41.4 9.0 %collective-permute-start.13 = (bf16[128,768]{1,0:T(8,128)(2,1)S(1)}, bf16[128,768]{1,0:T(8,128)(2,1)S(1)}, u32[]{:S(2)}, u32[]{:S(2)}) collective-permute-start(bf16[128,768]{1,0:T(8,128)(2,1)S(1)} %get-tuple-element.72.middle), channel_id=1, source_target_pairs={{0,2},{1,3},{2,0},{3,1},{4,6},{5,7},{6,4},{7,5},{8,10},{9,11},{10,... | collective-permute-start | bytes 589832 | tf_op jit(solution)/shard_map/ppermute | solution.py:22
  43.0 11.2 %collective-permute-start.14 = (bf16[128,768]{1,0:T(8,128)(2,1)S(1)}, bf16[128,768]{1,0:T(8,128)(2,1)S(1)}, u32[]{:S(2)}, u32[]{:S(2)}) collective-permute-start(bf16[128,768]{1,0:T(8,128)(2,1)S(1)} %get-tuple-element.72.middle), channel_id=1, source_target_pairs={{2,4},{3,5},{4,2},{5,3},{6,8},{7,9},{8,6},{9,7},{10,12},{11,13},{1... | collective-permute-start | bytes 589832 | tf_op jit(solution)/shard_map/ppermute | solution.py:22

commit v5 on v4

--- a/solution.py
+++ b/solution.py
@@ -205,14 +205,16 @@
     output[...] = (output_first[...].astype(F32) + conv).astype(BF16)
 
 
-def early_backward(middle, features, taps, partial, slope):
+def early_backward(middle, features, taps, partial, slope, step_tap, flip_tap):
+    odd = position(middle.shape[0])[0] & 1
+    step_tap[...] = taps[2 - 2 * odd].T
+    flip_tap[...] = taps[2 * odd].T
     slope[...] = gelu_pair(features[...])[1]
     partial[...] = dot_t(middle[...], taps[1])
 
 
-def first_backward(middle, flip, step, partial, slope, taps, output):
-    odd = position(middle.shape[0])[0] & 1
-    back = partial[...] + dot_t(step[...], taps[2 - 2 * odd]) + dot_t(flip[...], taps[2 * odd])
+def first_backward(middle, flip, step, partial, slope, step_tap, flip_tap, output):
+    back = partial[...] + dot(step[...], step_tap[...]) + dot(flip[...], flip_tap[...])
     output[...] = (middle[...].astype(F32) + slope[...] * back).astype(BF16)
 
 
@@ -275,7 +277,8 @@
         ],
     )
     late, _ = together((middle, terms[0]))
-    middle_flip, middle_step = flipped(late), stepped(late)
+    middle_flip = flipped(late)
+    middle_step = stepped(together((middle, other_line))[0])
     if planes == 4:
         got = [moved(terms[s], lambda i, s=s: i ^ (PLANE * s)) for s in (1, 2, 3)]
         total = terms[0] + sum(g.astype(F32) for g in got)
@@ -284,8 +287,9 @@
         total = lax.psum_scatter(terms[0], "seq", scatter_dimension=1, axis_index_groups=lines)
     first_taps_gradient = jnp.swapaxes(total, 1, 2)
 
-    partial, slope_first = call(
-        early_backward, "early_backward", [wide, wide], late, features, first_taps
+    tap = ((width, width), BF16)
+    partial, slope_first, *turned = call(
+        early_backward, "early_backward", [wide, wide, tap, tap], late, features, first_taps
     )
     (second_layer_output,) = call(
         second_forward, "second_forward", [block],
@@ -293,7 +297,7 @@
     )
     (input_gradient,) = call(
         first_backward, "first_backward", [block],
-        middle, middle_flip, middle_step, partial, slope_first, first_taps,
+        middle, middle_flip, middle_step, partial, slope_first, *turned,
     )
     return second_layer_output, input_gradient, first_taps_gradient
 

time: 56 us -> 55.6 us (level)
  transfers between devices with their start and end apart: 18 -> 18, of which waited for: 9 -> 9; matrix products, arithmetic and copies ran while one was open for 1% -> 1% of each run, Pallas kernels for 12% -> 13%
where the time goes in v5:
time: 55.6 us; the launch traced here: 55.4 us
  starting transfers between devices  30.4 us (55%)
  waiting for transfers between devices  14.2 us (26%)
  Pallas kernels  9.21 us (17%)
  between operations  0.79 us (1%)
  other arithmetic  0.76 us (1%)
    ppermute x18, starting transfers between devices, moved(): return lax.ppermute(array, 'seq', pairs)  30.4 us
    ppermute x18, waiting for transfers between devices, moved(): return lax.ppermute(array, 'seq', pairs)  14.2 us
    pallas_call x9, Pallas kernels, call(): pl.pallas_call(body, name=name, out_shape=[jax.ShapeDtypeStruct(shape, ki...  9.21 us
  transfers between devices with their start and end apart: 18, of which 9 were waited for; matrix products, arithmetic and copies ran while one was open for 1% of the time, Pallas kernels for 13%

profile of v5, /device:TPU:16, one launch (start us, length us, event | category | flops | bytes accessed | tf_op | source)
XLA Modules:
  0.0 55.4 jit_solution(3099760890435297562)
XLA Ops:
  0.6 4.2 %collective-permute-start = (bf16[128,768]{1,0:T(8,128)(2,1)}, bf16[128,768]{1,0:T(8,128)(2,1)S(1)}, u32[]{:S(2)}, u32[]{:S(2)}) collective-permute-start(bf16[128,768]{1,0:T(8,128)(2,1)} %features.1), channel_id=1, source_target_pairs={{2,4},{3,5},{4,2},{5,3},{6,8},{7,9},{8,6},{9,7},{10,12},{11,13},{1... | collective-permute-start | bytes 589832 | tf_op jit(solution)/shard_map/ppermute | solution.py:22
  4.9 0.7 %collective-permute-start.1 = (bf16[128,768]{1,0:T(8,128)(2,1)}, bf16[128,768]{1,0:T(8,128)(2,1)S(1)}, u32[]{:S(2)}, u32[]{:S(2)}) collective-permute-start(bf16[128,768]{1,0:T(8,128)(2,1)} %features.1), channel_id=1, source_target_pairs={{0,2},{1,3},{2,0},{3,1},{4,6},{5,7},{6,4},{7,5},{8,10},{9,11},{10,... | collective-permute-start | bytes 589832 | tf_op jit(solution)/shard_map/ppermute | solution.py:22
  5.6 0.3 collective-permute-start.4
  5.9 1.5 %collective-permute-start.2 = (bf16[128,768]{1,0:T(8,128)(2,1)}, bf16[128,768]{1,0:T(8,128)(2,1)S(1)}, u32[]{:S(2)}, u32[]{:S(2)}) collective-permute-start(bf16[128,768]{1,0:T(8,128)(2,1)} %features.1), channel_id=1, source_target_pairs={{0,4},{1,5},{2,6},{3,7},{4,0},{5,1},{6,2},{7,3},{8,12},{9,13},{10,... | collective-permute-start | bytes 589832 | tf_op jit(solution)/shard_map/ppermute | solution.py:22
  7.5 2.9 %collective-permute-start.3 = (bf16[128,768]{1,0:T(8,128)(2,1)}, bf16[128,768]{1,0:T(8,128)(2,1)S(1)}, u32[]{:S(2)}, u32[]{:S(2)}) collective-permute-start(bf16[128,768]{1,0:T(8,128)(2,1)} %features.1), channel_id=1, source_target_pairs={{0,6},{1,7},{6,0},{7,1},{8,14},{9,15},{14,8},{15,9},{16,22},{17,23... | collective-permute-start | bytes 589832 | tf_op jit(solution)/shard_map/ppermute | solution.py:22
  10.3 3.3 %load.1 = (bf16[128,768]{1,0:T(8,128)(2,1)S(1)}, f32[128,768]{1,0:T(8,128)S(1)}, f32[128,768]{1,0:T(8,128)S(1)}, bf16[3,768,768]{2,1,0:T(8,128)(2,1)S(1)}, bf16[...) custom-call(bf16[128,768]{1,0:T(8,128)(2,1)} %features.1, ...), custom_call_target="tpu_custom_call" | custom-call | tf_op jit(solution)/shard_map/load/pallas_call | solution.py:61
  13.6 3.0 %collective-permute-done.step = bf16[128,768]{1,0:T(8,128)(2,1)S(1)} collective-permute-done((bf16[128,768]{1,0:T(8,128)(2,1)}, bf16[128,768]{1,0:T(8,128)(2,1)S(1)}, u32[]{:S(2)}, u32[]{:S(2)}) %collective-permute-start) | collective-permute-done | bytes 196640 | tf_op jit(solution)/shard_map/ppermute | solution.py:22
  16.6 0.7 %forward.1 = (bf16[128,768]{1,0:T(8,128)(2,1)S(1)}, bf16[128,768]{1,0:T(8,128)(2,1)S(1)}, f32[128,768]{1,0:T(8,128)S(1)}, bf16[128,768]{1,0:T(8,128)(2,1)S(1)}, bf16[128,768]{1,0:T(8,128)(2,1)S(1)}) custom-call(bf16[128,768]{1,0:T(8,128)(2,1)S(1)} %collective-permute-done.1.flip, bf16[128,768]{1,0:T(8,128)(2,1)S(1)} %collective-permute-done.step, ...), custom_call_target="tpu_custom_call" | custom-call | tf_op jit(solution)/shard_map/forward/pallas_call | solution.py:61
  17.3 0.5 collective-permute-done.4.refs_0_
  17.8 0.7 %middle.1 = (bf16[128,768]{1,0:T(8,128)(2,1)S(1)}, bf16[2,96,128]{2,1,0:T(8,128)(2,1)S(1)}, bf16[2,96,128]{2,1,0:T(8,128)(2,1)S(1)}, bf16[2,96,128]{2,1,0:T(8,128)(2,1)S(1)}, bf16[2,96,128]{2,1,0:T(8,128)(2,1)S(1)}) custom-call(bf16[128,768]{1,0:T(8,128)(2,1)S(1)} %collective-permute-done.4.refs_0_, f32[128,768]{1,0:T(8,128)S(1)} %get-tuple-element.52.refs_1_, ...), custom_call_target="tpu_custom_call" | custom-call | tf_op jit(solution)/shard_map/middle/pallas_call | solution.py:61
  18.5 1.2 %collective-permute-done.3.turn = bf16[128,768]{1,0:T(8,128)(2,1)S(1)} collective-permute-done((bf16[128,768]{1,0:T(8,128)(2,1)}, bf16[128,768]{1,0:T(8,128)(2,1)S(1)}, u32[]{:S(2)}, u32[]{:S(2)}) %collective-permute-start.3) | collective-permute-done | bytes 196640 | tf_op jit(solution)/shard_map/ppermute | solution.py:22
  20.0 2.2 %collective-permute-start.9 = (bf16[2,96,128]{2,1,0:T(8,128)(2,1)S(1)}, bf16[2,96,128]{2,1,0:T(8,128)(2,1)S(1)}, u32[]{:S(2)}, u32[]{:S(2)}) collective-permute-start(bf16[2,96,128]{2,1,0:T(8,128)(2,1)S(1)} %get-tuple-element.69), channel_id=1, source_target_pairs={{0,6},{1,7},{2,4},{3,5},{4,2},{5,3},{6,0},{7,1},{8,14},{9,15},{10,... | collective-permute-start | bytes 147464 | tf_op jit(solution)/shard_map/ppermute | solution.py:22
  22.3 1.3 %collective-permute-start.7 = (bf16[2,96,128]{2,1,0:T(8,128)(2,1)S(1)}, bf16[2,96,128]{2,1,0:T(8,128)(2,1)S(1)}, u32[]{:S(2)}, u32[]{:S(2)}) collective-permute-start(bf16[2,96,128]{2,1,0:T(8,128)(2,1)S(1)} %get-tuple-element.67), channel_id=1, source_target_pairs={{0,2},{1,3},{2,0},{3,1},{4,6},{5,7},{6,4},{7,5},{8,10},{9,11},{10,... | collective-permute-start | bytes 147464 | tf_op jit(solution)/shard_map/ppermute | solution.py:22
  23.6 2.1 %collective-permute-start.6 = (bf16[128,768]{1,0:T(8,128)(2,1)S(1)}, bf16[128,768]{1,0:T(8,128)(2,1)S(1)}, u32[]{:S(2)}, u32[]{:S(2)}) collective-permute-start(bf16[128,768]{1,0:T(8,128)(2,1)S(1)} %get-tuple-element.62.refs_1_), channel_id=1, source_target_pairs={{0,16},{1,17},{2,18},{3,19},{4,20},{5,21},{6,22},{7,23},{8,24},{9,... | collective-permute-start | bytes 589832 | tf_op jit(solution)/shard_map/ppermute | solution.py:22
  25.7 0.6 %collective-permute-done.8.refs_2_ = bf16[2,96,128]{2,1,0:T(8,128)(2,1)S(1)} collective-permute-done((bf16[2,96,128]{2,1,0:T(8,128)(2,1)S(1)}, bf16[2,96,128]{2,1,0:T(8,128)(2,1)S(1)}, u32[]{:S(2)}, u32[]{:S(2)}) %collective-permute-start.8) | collective-permute-done | bytes 49184 | tf_op jit(solution)/shard_map/ppermute | solution.py:22
  26.5 1.3 %collective-permute-done.10.refs_4_ = bf16[4,96,128]{2,1,0:T(8,128)(2,1)S(1)} collective-permute-done((bf16[4,96,128]{2,1,0:T(8,128)(2,1)S(1)}, bf16[4,96,128]{2,1,0:T(8,128)(2,1)S(1)}, u32[]{:S(2)}, u32[]{:S(2)}) %collective-permute-start.10) | collective-permute-done | bytes 98336 | tf_op jit(solution)/shard_map/ppermute | solution.py:22
  28.0 3.2 %collective-permute-start.11 = (bf16[2,96,128]{2,1,0:T(8,128)(2,1)S(1)}, bf16[2,96,128]{2,1,0:T(8,128)(2,1)S(1)}, u32[]{:S(2)}, u32[]{:S(2)}) collective-permute-start(bf16[2,96,128]{2,1,0:T(8,128)(2,1)S(1)} %get-tuple-element.71), channel_id=1, source_target_pairs={{0,8},{1,9},{2,10},{3,11},{4,12},{5,13},{6,14},{7,15},{8,16},{9,17... | collective-permute-start | bytes 147464 | tf_op jit(solution)/shard_map/ppermute | solution.py:22
  31.2 2.6 %collective-permute-start.12 = (bf16[2,96,128]{2,1,0:T(8,128)(2,1)S(1)}, bf16[2,96,128]{2,1,0:T(8,128)(2,1)S(1)}, u32[]{:S(2)}, u32[]{:S(2)}) collective-permute-start(bf16[2,96,128]{2,1,0:T(8,128)(2,1)S(1)} %get-tuple-element.72), channel_id=1, source_target_pairs={{8,0},{9,1},{10,2},{11,3},{12,4},{13,5},{14,6},{15,7},{16,8},{17,9... | collective-permute-start | bytes 147464 | tf_op jit(solution)/shard_map/ppermute | solution.py:22
  33.8 2.4 %collective-permute-done.11.behind = bf16[2,96,128]{2,1,0:T(8,128)(2,1)S(1)} collective-permute-done((bf16[2,96,128]{2,1,0:T(8,128)(2,1)S(1)}, bf16[2,96,128]{2,1,0:T(8,128)(2,1)S(1)}, u32[]{:S(2)}, u32[]{:S(2)}) %collective-permute-start.11) | collective-permute-done | bytes 49184 | tf_op jit(solution)/shard_map/ppermute | solution.py:22
  36.2 1.0 %collective-permute-done.12.ahead = bf16[2,96,128]{2,1,0:T(8,128)(2,1)S(1)} collective-permute-done((bf16[2,96,128]{2,1,0:T(8,128)(2,1)S(1)}, bf16[2,96,128]{2,1,0:T(8,128)(2,1)S(1)}, u32[]{:S(2)}, u32[]{:S(2)}) %collective-permute-start.12) | collective-permute-done | bytes 49184 | tf_op jit(solution)/shard_map/ppermute | solution.py:22
  37.2 0.7 %terms.1 = (f32[3,24,768]{2,1,0:T(8,128)S(1)}, bf16[3,24,768]{2,1,0:T(8,128)(2,1)S(1)}, bf16[3,24,768]{2,1,0:T(8,128)(2,1)S(1)}, bf16[3,24,768]{2,1,0:T(8,128)(2,1)S(1)}) custom-call(bf16[2,96,512]{2,1,0:T(8,128)(2,1)S(1)} %get-tuple-element.70.cols, bf16[2,96,128]{2,1,0:T(8,128)(2,1)S(1)} %collective-permute-done.11.behind, ...), custom_call_target="tpu_custom_call" | custom-call | tf_op jit(solution)/shard_map/terms/pallas_call | solution.py:61
  37.9 0.8 %collective-permute-start.17 = (bf16[3,24,768]{2,1,0:T(8,128)(2,1)S(1)}, bf16[3,24,768]{2,1,0:T(8,128)(2,1)S(1)}, u32[]{:S(2)}, u32[]{:S(2)}) collective-permute-start(bf16[3,24,768]{2,1,0:T(8,128)(2,1)S(1)} %get-tuple-element.84), channel_id=1, source_target_pairs={{0,24},{1,25},{2,26},{3,27},{4,28},{5,29},{6,30},{7,31},{8,16},{9,... | collective-permute-start | bytes 331784 | tf_op jit(solution)/shard_map/ppermute | solution.py:22
  38.6 2.1 %collective-permute-start.16 = (bf16[3,24,768]{2,1,0:T(8,128)(2,1)S(1)}, bf16[3,24,768]{2,1,0:T(8,128)(2,1)S(1)}, u32[]{:S(2)}, u32[]{:S(2)}) collective-permute-start(bf16[3,24,768]{2,1,0:T(8,128)(2,1)S(1)} %get-tuple-element.83), channel_id=1, source_target_pairs={{0,16},{1,17},{2,18},{3,19},{4,20},{5,21},{6,22},{7,23},{8,24},{9,... | collective-permute-start | bytes 331784 | tf_op jit(solution)/shard_map/ppermute | solution.py:22
  40.8 0.7 %collective-permute-start.15 = (bf16[3,24,768]{2,1,0:T(8,128)(2,1)S(1)}, bf16[3,24,768]{2,1,0:T(8,128)(2,1)S(1)}, u32[]{:S(2)}, u32[]{:S(2)}) collective-permute-start(bf16[3,24,768]{2,1,0:T(8,128)(2,1)S(1)} %get-tuple-element.82), channel_id=1, source_target_pairs={{0,8},{1,9},{2,10},{3,11},{4,12},{5,13},{6,14},{7,15},{8,0},{9,1},... | collective-permute-start | bytes 331784 | tf_op jit(solution)/shard_map/ppermute | solution.py:22
  41.4 1.5 %collective-permute-start.13 = (bf16[128,768]{1,0:T(8,128)(2,1)S(1)}, bf16[128,768]{1,0:T(8,128)(2,1)S(1)}, u32[]{:S(2)}, u32[]{:S(2)}) collective-permute-start(bf16[128,768]{1,0:T(8,128)(2,1)S(1)} %get-tuple-element.76.middle), channel_id=1, source_target_pairs={{0,2},{1,3},{2,0},{3,1},{4,6},{5,7},{6,4},{7,5},{8,10},{9,11},{10,... | collective-permute-start | bytes 589832 | tf_op jit(solution)/shard_map/ppermute | solution.py:22
  43.0 3.9 %collective-permute-start.14 = (bf16[128,768]{1,0:T(8,128)(2,1)S(1)}, bf16[128,768]{1,0:T(8,128)(2,1)S(1)}, u32[]{:S(2)}, u32[]{:S(2)}) collective-permute-start(bf16[128,768]{1,0:T(8,128)(2,1)S(1)} %get-tuple-element.76.middle), channel_id=1, source_target_pairs={{2,4},{3,5},{4,2},{5,3},{6,8},{7,9},{8,6},{9,7},{10,12},{11,13},{1... | collective-permute-start | bytes 589832 | tf_op jit(solution)/shard_map/ppermute | solution.py:22
  46.9 1.1 %early_backward.1 = (f32[128,768]{1,0:T(8,128)S(1)}, f32[128,768]{1,0:T(8,128)S(1)}, bf16[768,768]{1,0:T(8,128)(2,1)S(1)}, bf16[768,768]{1,0:T(8,128)(2,1)S(1)}) custom-call(bf16[128,768]{1,0:T(8,128)(2,1)S(1)} %get-tuple-element.76.middle, bf16[128,768]{1,0:T(8,128)(2,1)S(1)} %get-tuple-element.77.features, bf16[3,768,768]{2,1,0:T(8,128)(2,1)S(1)} %get-tuple-element.49.taps), custom_call_target="tpu_custom_call" | custom-call | tf_op jit(solution)/shard_map/early_backward/pallas_call | solution.py:61
  48.0 1.2 %second_forward.1 = bf16[128,768]{1,0:T(8,128)(2,1)} custom-call(bf16[128,768]{1,0:T(8,128)(2,1)S(1)} %collective-permute-done.6.refs_0_, bf16[128,768]{1,0:T(8,128)(2,1)S(1)} %get-tuple-element.62.refs_1_, bf16[128,768]{1,0:T(8,128)(2,1)S(1)} %get-tuple-element.64.refs_2_, bf16[3,768,768]{2,1,0:T(8,128)(2,1)S(1)} %get-tuple-element.55.refs_4_.refs_3_), custom_call_target="tpu_custom_call" | custom-call | tf_op jit(solution)/shard_map/second_forward/pallas_call | solution.py:61
  49.2 0.7 %add_bitcast_fusion = f32[3,768,24]{1,2,0:T(8,128)} fusion(f32[3,24,768]{2,1,0:T(8,128)S(1)} %get-tuple-element.74, bf16[3,24,768]{2,1,0:T(8,128)(2,1)S(1)} %collective-permute-done.17, bf16[3,24,768]{2,1,0:T(8,128)(2,1)S(1)} %collective-permute-done.16, bf16[3,24,768]{2,1,0:T(8,128)(2,1)S(1)} %collective-permute-done.15), kind=kLoop, calls=%fused_computation | loop fusion | flops 331776 | bytes 774144 | tf_op jit(solution)/shard_map/transpose | solution.py:288
  49.9 0.5 collective-permute-done.13.flip
  50.4 3.8 %collective-permute-done.14.step = bf16[128,768]{1,0:T(8,128)(2,1)S(1)} collective-permute-done((bf16[128,768]{1,0:T(8,128)(2,1)S(1)}, bf16[128,768]{1,0:T(8,128)(2,1)S(1)}, u32[]{:S(2)}, u32[]{:S(2)}) %collective-permute-start.14) | collective-permute-done | bytes 196640 | tf_op jit(solution)/shard_map/ppermute | solution.py:22
  54.2 1.2 %first_backward.1 = bf16[128,768]{1,0:T(8,128)(2,1)} custom-call(bf16[128,768]{1,0:T(8,128)(2,1)S(1)} %get-tuple-element.76.middle, bf16[128,768]{1,0:T(8,128)(2,1)S(1)} %collective-permute-done.13.flip, bf16[128,768]{1,0:T(8,128)(2,1)S(1)} %collective-permute-done.14.step, f32[128,768]{1,0:T(8,128)S(1)} %get-tuple-element.78.partial, ...), custom_call_target="tpu_custom_call" | custom-call | tf_op jit(solution)/shard_map/first_backward/pallas_call | solution.py:61
  (19 shorter events, 0.7 us)
Async XLA Ops:
  0.6 16.0 %collective-permute-start = (bf16[128,768]{1,0:T(8,128)(2,1)}, bf16[128,768]{1,0:T(8,128)(2,1)S(1)}, u32[]{:S(2)}, u32[]{:S(2)}) collective-permute-start(bf16[128,768]{1,0:T(8,128)(2,1)} %features.1), channel_id=1, source_target_pairs={{2,4},{3,5},{4,2},{5,3},{6,8},{7,9},{8,6},{9,7},{10,12},{11,13},{1... | collective-permute-start | bytes 589832 | tf_op jit(solution)/shard_map/ppermute | solution.py:22
  4.9 11.7 %collective-permute-start.1 = (bf16[128,768]{1,0:T(8,128)(2,1)}, bf16[128,768]{1,0:T(8,128)(2,1)S(1)}, u32[]{:S(2)}, u32[]{:S(2)}) collective-permute-start(bf16[128,768]{1,0:T(8,128)(2,1)} %features.1), channel_id=1, source_target_pairs={{0,2},{1,3},{2,0},{3,1},{4,6},{5,7},{6,4},{7,5},{8,10},{9,11},{10,... | collective-permute-start | bytes 589832 | tf_op jit(solution)/shard_map/ppermute | solution.py:22
  5.6 12.2 %collective-permute-start.4 = (bf16[128,768]{1,0:T(8,128)(2,1)}, bf16[128,768]{1,0:T(8,128)(2,1)S(1)}, u32[]{:S(2)}, u32[]{:S(2)}) collective-permute-start(bf16[128,768]{1,0:T(8,128)(2,1)} %up.1), channel_id=1, source_target_pairs={{0,16},{1,17},{2,18},{3,19},{4,20},{5,21},{6,22},{7,23},{8,24},{9,... | collective-permute-start | bytes 589832 | tf_op jit(solution)/shard_map/ppermute | solution.py:22
  5.9 12.5 %collective-permute-start.2 = (bf16[128,768]{1,0:T(8,128)(2,1)}, bf16[128,768]{1,0:T(8,128)(2,1)S(1)}, u32[]{:S(2)}, u32[]{:S(2)}) collective-permute-start(bf16[128,768]{1,0:T(8,128)(2,1)} %features.1), channel_id=1, source_target_pairs={{0,4},{1,5},{2,6},{3,7},{4,0},{5,1},{6,2},{7,3},{8,12},{9,13},{10,... | collective-permute-start | bytes 589832 | tf_op jit(solution)/shard_map/ppermute | solution.py:22
  7.5 12.2 %collective-permute-start.3 = (bf16[128,768]{1,0:T(8,128)(2,1)}, bf16[128,768]{1,0:T(8,128)(2,1)S(1)}, u32[]{:S(2)}, u32[]{:S(2)}) collective-permute-start(bf16[128,768]{1,0:T(8,128)(2,1)} %features.1), channel_id=1, source_target_pairs={{0,6},{1,7},{6,0},{7,1},{8,14},{9,15},{14,8},{15,9},{16,22},{17,23... | collective-permute-start | bytes 589832 | tf_op jit(solution)/shard_map/ppermute | solution.py:22
  19.9 13.9 %collective-permute-start.5 = (bf16[512,768]{1,0:T(8,128)(2,1)S(1)}, bf16[512,768]{1,0:T(8,128)(2,1)S(1)}, u32[]{:S(2)}, u32[]{:S(2)}) collective-permute-start(bf16[512,768]{1,0:T(8,128)(2,1)S(1)} %line.1), channel_id=1, source_target_pairs={{0,1},{1,0},{2,3},{3,2},{4,5},{5,4},{6,7},{7,6},{8,9},{9,8},{10,11... | collective-permute-start | bytes 2359304 | tf_op jit(solution)/shard_map/ppermute | solution.py:22
  20.0 5.7 %collective-permute-start.9 = (bf16[2,96,128]{2,1,0:T(8,128)(2,1)S(1)}, bf16[2,96,128]{2,1,0:T(8,128)(2,1)S(1)}, u32[]{:S(2)}, u32[]{:S(2)}) collective-permute-start(bf16[2,96,128]{2,1,0:T(8,128)(2,1)S(1)} %get-tuple-element.69), channel_id=1, source_target_pairs={{0,6},{1,7},{2,4},{3,5},{4,2},{5,3},{6,0},{7,1},{8,14},{9,15},{10,... | collective-permute-start | bytes 147464 | tf_op jit(solution)/shard_map/ppermute | solution.py:22
  22.3 4.1 %collective-permute-start.8 = (bf16[2,96,128]{2,1,0:T(8,128)(2,1)S(1)}, bf16[2,96,128]{2,1,0:T(8,128)(2,1)S(1)}, u32[]{:S(2)}, u32[]{:S(2)}) collective-permute-start(bf16[2,96,128]{2,1,0:T(8,128)(2,1)S(1)} %get-tuple-element.68), channel_id=1, source_target_pairs={{0,4},{1,5},{2,6},{3,7},{4,0},{5,1},{6,2},{7,3},{8,12},{9,13},{10,... | collective-permute-start | bytes 147464 | tf_op jit(solution)/shard_map/ppermute | solution.py:22
  22.3 4.1 %collective-permute-start.7 = (bf16[2,96,128]{2,1,0:T(8,128)(2,1)S(1)}, bf16[2,96,128]{2,1,0:T(8,128)(2,1)S(1)}, u32[]{:S(2)}, u32[]{:S(2)}) collective-permute-start(bf16[2,96,128]{2,1,0:T(8,128)(2,1)S(1)} %get-tuple-element.67), channel_id=1, source_target_pairs={{0,2},{1,3},{2,0},{3,1},{4,6},{5,7},{6,4},{7,5},{8,10},{9,11},{10,... | collective-permute-start | bytes 147464 | tf_op jit(solution)/shard_map/ppermute | solution.py:22
  23.6 10.2 %collective-permute-start.6 = (bf16[128,768]{1,0:T(8,128)(2,1)S(1)}, bf16[128,768]{1,0:T(8,128)(2,1)S(1)}, u32[]{:S(2)}, u32[]{:S(2)}) collective-permute-start(bf16[128,768]{1,0:T(8,128)(2,1)S(1)} %get-tuple-element.62.refs_1_), channel_id=1, source_target_pairs={{0,16},{1,17},{2,18},{3,19},{4,20},{5,21},{6,22},{7,23},{8,24},{9,... | collective-permute-start | bytes 589832 | tf_op jit(solution)/shard_map/ppermute | solution.py:22
  26.4 1.4 %collective-permute-start.10 = (bf16[4,96,128]{2,1,0:T(8,128)(2,1)S(1)}, bf16[4,96,128]{2,1,0:T(8,128)(2,1)S(1)}, u32[]{:S(2)}, u32[]{:S(2)}) collective-permute-start(bf16[4,96,128]{2,1,0:T(8,128)(2,1)S(1)} %pad_maximum_fusion), channel_id=1, source_target_pairs={{0,1},{1,0},{2,3},{3,2},{4,5},{5,4},{6,7},{7,6},{8,9},{9,8},{10,11... | collective-permute-start | bytes 294920 | tf_op jit(solution)/shard_map/ppermute | solution.py:22
  28.0 8.2 %collective-permute-start.11 = (bf16[2,96,128]{2,1,0:T(8,128)(2,1)S(1)}, bf16[2,96,128]{2,1,0:T(8,128)(2,1)S(1)}, u32[]{:S(2)}, u32[]{:S(2)}) collective-permute-start(bf16[2,96,128]{2,1,0:T(8,128)(2,1)S(1)} %get-tuple-element.71), channel_id=1, source_target_pairs={{0,8},{1,9},{2,10},{3,11},{4,12},{5,13},{6,14},{7,15},{8,16},{9,17... | collective-permute-start | bytes 147464 | tf_op jit(solution)/shard_map/ppermute | solution.py:22
  31.2 6.0 %collective-permute-start.12 = (bf16[2,96,128]{2,1,0:T(8,128)(2,1)S(1)}, bf16[2,96,128]{2,1,0:T(8,128)(2,1)S(1)}, u32[]{:S(2)}, u32[]{:S(2)}) collective-permute-start(bf16[2,96,128]{2,1,0:T(8,128)(2,1)S(1)} %get-tuple-element.72), channel_id=1, source_target_pairs={{8,0},{9,1},{10,2},{11,3},{12,4},{13,5},{14,6},{15,7},{16,8},{17,9... | collective-permute-start | bytes 147464 | tf_op jit(solution)/shard_map/ppermute | solution.py:22
  37.9 11.3 %collective-permute-start.17 = (bf16[3,24,768]{2,1,0:T(8,128)(2,1)S(1)}, bf16[3,24,768]{2,1,0:T(8,128)(2,1)S(1)}, u32[]{:S(2)}, u32[]{:S(2)}) collective-permute-start(bf16[3,24,768]{2,1,0:T(8,128)(2,1)S(1)} %get-tuple-element.84), channel_id=1, source_target_pairs={{0,24},{1,25},{2,26},{3,27},{4,28},{5,29},{6,30},{7,31},{8,16},{9,... | collective-permute-start | bytes 331784 | tf_op jit(solution)/shard_map/ppermute | solution.py:22
  38.6 10.5 %collective-permute-start.16 = (bf16[3,24,768]{2,1,0:T(8,128)(2,1)S(1)}, bf16[3,24,768]{2,1,0:T(8,128)(2,1)S(1)}, u32[]{:S(2)}, u32[]{:S(2)}) collective-permute-start(bf16[3,24,768]{2,1,0:T(8,128)(2,1)S(1)} %get-tuple-element.83), channel_id=1, source_target_pairs={{0,16},{1,17},{2,18},{3,19},{4,20},{5,21},{6,22},{7,23},{8,24},{9,... | collective-permute-start | bytes 331784 | tf_op jit(solution)/shard_map/ppermute | solution.py:22
  40.8 8.4 %collective-permute-start.15 = (bf16[3,24,768]{2,1,0:T(8,128)(2,1)S(1)}, bf16[3,24,768]{2,1,0:T(8,128)(2,1)S(1)}, u32[]{:S(2)}, u32[]{:S(2)}) collective-permute-start(bf16[3,24,768]{2,1,0:T(8,128)(2,1)S(1)} %get-tuple-element.82), channel_id=1, source_target_pairs={{0,8},{1,9},{2,10},{3,11},{4,12},{5,13},{6,14},{7,15},{8,0},{9,1},... | collective-permute-start | bytes 331784 | tf_op jit(solution)/shard_map/ppermute | solution.py:22
  41.4 9.0 %collective-permute-start.13 = (bf16[128,768]{1,0:T(8,128)(2,1)S(1)}, bf16[128,768]{1,0:T(8,128)(2,1)S(1)}, u32[]{:S(2)}, u32[]{:S(2)}) collective-permute-start(bf16[128,768]{1,0:T(8,128)(2,1)S(1)} %get-tuple-element.76.middle), channel_id=1, source_target_pairs={{0,2},{1,3},{2,0},{3,1},{4,6},{5,7},{6,4},{7,5},{8,10},{9,11},{10,... | collective-permute-start | bytes 589832 | tf_op jit(solution)/shard_map/ppermute | solution.py:22
  43.0 11.2 %collective-permute-start.14 = (bf16[128,768]{1,0:T(8,128)(2,1)S(1)}, bf16[128,768]{1,0:T(8,128)(2,1)S(1)}, u32[]{:S(2)}, u32[]{:S(2)}) collective-permute-start(bf16[128,768]{1,0:T(8,128)(2,1)S(1)} %get-tuple-element.76.middle), channel_id=1, source_target_pairs={{2,4},{3,5},{4,2},{5,3},{6,8},{7,9},{8,6},{9,7},{10,12},{11,13},{1... | collective-permute-start | bytes 589832 | tf_op jit(solution)/shard_map/ppermute | solution.py:22

commit v6 on v5

--- a/solution.py
+++ b/solution.py
@@ -167,7 +167,7 @@
                 last[side] = piece
 
 
-def terms_body(cols, behind, ahead, line, other_line, *refs, planes):
+def terms_body(cols, ahead, behind, line, other_line, *refs, planes):
     outs, (stacked, sums) = refs[:-2], refs[-2:]
     group, rows = behind.shape[1:]
     plane = position(rows)[2]
@@ -249,7 +249,7 @@
         scratch=[pltpu.VMEM((PLANE, group, rows), F32)],
     )
 
-    cross, turn, *parts = together((cross, turn, *parts))
+    cross, turn, parts[3] = together((cross, turn, parts[3]))
     parts = [parts[0]] + [moved(parts[s], lambda i, s=s: i ^ (2 * s)) for s in (1, 2, 3)]
     far_second = far_pieces(acts_second)
     other_parts = moved(jnp.stack([p[1] for p in parts]), lambda i: i ^ 1)
@@ -260,8 +260,8 @@
         line_body, "line", [((4 * rows, width), BF16)], acts, flip, step, cross, turn
     )
     other_line = moved(line, lambda i: i ^ 1)
+    cols_ahead = moved(col_first, lambda i: i - PLANE)
     cols_behind = moved(col_last, lambda i: i + PLANE)
-    cols_ahead = moved(col_first, lambda i: i - PLANE)
     other_line, far_second = together((other_line, far_second))
 
     piece = ((3, own_cols, width), BF16)
@@ -270,15 +270,15 @@
         outs = [((3, planes, own_cols, width), F32)]
     terms = call(
         functools.partial(terms_body, planes=planes), "terms", outs,
-        cols, cols_behind, cols_ahead, line, other_line,
+        cols, cols_ahead, cols_behind, line, other_line,
         scratch=[
             pltpu.VMEM((3 * group, 4 * rows), BF16),
             pltpu.VMEM((3, planes, own_cols, width), F32),
         ],
     )
     late, _ = together((middle, terms[0]))
-    middle_flip = flipped(late)
-    middle_step = stepped(together((middle, other_line))[0])
+    middle_flip = flipped(together((middle, other_line))[0])
+    middle_step = stepped(late)
     if planes == 4:
         got = [moved(terms[s], lambda i, s=s: i ^ (PLANE * s)) for s in (1, 2, 3)]
         total = terms[0] + sum(g.astype(F32) for g in got)

time: 55.6 us -> 55.5 us (level)
  no operation moved by 1% of the time
where the time goes in v6:
time: 55.5 us; the launch traced here: 55 us
  starting transfers between devices  30.4 us (55%)
  waiting for transfers between devices  13.8 us (25%)
  Pallas kernels  9.22 us (17%)
  between operations  0.79 us (1%)
  other arithmetic  0.76 us (1%)
    ppermute x18, starting transfers between devices, moved(): return lax.ppermute(array, 'seq', pairs)  30.4 us
    ppermute x18, waiting for transfers between devices, moved(): return lax.ppermute(array, 'seq', pairs)  13.8 us
    pallas_call x9, Pallas kernels, call(): pl.pallas_call(body, name=name, out_shape=[jax.ShapeDtypeStruct(shape, ki...  9.22 us
  transfers between devices with their start and end apart: 18, of which 9 were waited for; matrix products, arithmetic and copies ran while one was open for 1% of the time, Pallas kernels for 13%

profile of v6, /device:TPU:16, one launch (start us, length us, event | category | flops | bytes accessed | tf_op | source)
XLA Modules:
  0.0 55.0 jit_solution(15455365294426356036)
XLA Ops:
  0.6 4.2 %collective-permute-start = (bf16[128,768]{1,0:T(8,128)(2,1)}, bf16[128,768]{1,0:T(8,128)(2,1)S(1)}, u32[]{:S(2)}, u32[]{:S(2)}) collective-permute-start(bf16[128,768]{1,0:T(8,128)(2,1)} %features.1), channel_id=1, source_target_pairs={{2,4},{3,5},{4,2},{5,3},{6,8},{7,9},{8,6},{9,7},{10,12},{11,13},{1... | collective-permute-start | bytes 589832 | tf_op jit(solution)/shard_map/ppermute | solution.py:22
  4.9 0.7 %collective-permute-start.1 = (bf16[128,768]{1,0:T(8,128)(2,1)}, bf16[128,768]{1,0:T(8,128)(2,1)S(1)}, u32[]{:S(2)}, u32[]{:S(2)}) collective-permute-start(bf16[128,768]{1,0:T(8,128)(2,1)} %features.1), channel_id=1, source_target_pairs={{0,2},{1,3},{2,0},{3,1},{4,6},{5,7},{6,4},{7,5},{8,10},{9,11},{10,... | collective-permute-start | bytes 589832 | tf_op jit(solution)/shard_map/ppermute | solution.py:22
  5.6 0.3 collective-permute-start.4
  5.9 1.5 %collective-permute-start.2 = (bf16[128,768]{1,0:T(8,128)(2,1)}, bf16[128,768]{1,0:T(8,128)(2,1)S(1)}, u32[]{:S(2)}, u32[]{:S(2)}) collective-permute-start(bf16[128,768]{1,0:T(8,128)(2,1)} %features.1), channel_id=1, source_target_pairs={{0,4},{1,5},{2,6},{3,7},{4,0},{5,1},{6,2},{7,3},{8,12},{9,13},{10,... | collective-permute-start | bytes 589832 | tf_op jit(solution)/shard_map/ppermute | solution.py:22
  7.5 2.9 %collective-permute-start.3 = (bf16[128,768]{1,0:T(8,128)(2,1)}, bf16[128,768]{1,0:T(8,128)(2,1)S(1)}, u32[]{:S(2)}, u32[]{:S(2)}) collective-permute-start(bf16[128,768]{1,0:T(8,128)(2,1)} %features.1), channel_id=1, source_target_pairs={{0,6},{1,7},{6,0},{7,1},{8,14},{9,15},{14,8},{15,9},{16,22},{17,23... | collective-permute-start | bytes 589832 | tf_op jit(solution)/shard_map/ppermute | solution.py:22
  10.3 3.3 %load.1 = (bf16[128,768]{1,0:T(8,128)(2,1)S(1)}, f32[128,768]{1,0:T(8,128)S(1)}, f32[128,768]{1,0:T(8,128)S(1)}, bf16[3,768,768]{2,1,0:T(8,128)(2,1)S(1)}, bf16[...) custom-call(bf16[128,768]{1,0:T(8,128)(2,1)} %features.1, ...), custom_call_target="tpu_custom_call" | custom-call | tf_op jit(solution)/shard_map/load/pallas_call | solution.py:61
  13.6 3.0 %collective-permute-done.step = bf16[128,768]{1,0:T(8,128)(2,1)S(1)} collective-permute-done((bf16[128,768]{1,0:T(8,128)(2,1)}, bf16[128,768]{1,0:T(8,128)(2,1)S(1)}, u32[]{:S(2)}, u32[]{:S(2)}) %collective-permute-start) | collective-permute-done | bytes 196640 | tf_op jit(solution)/shard_map/ppermute | solution.py:22
  16.6 0.7 %forward.1 = (bf16[128,768]{1,0:T(8,128)(2,1)S(1)}, bf16[128,768]{1,0:T(8,128)(2,1)S(1)}, f32[128,768]{1,0:T(8,128)S(1)}, bf16[128,768]{1,0:T(8,128)(2,1)S(1)}, bf16[128,768]{1,0:T(8,128)(2,1)S(1)}) custom-call(bf16[128,768]{1,0:T(8,128)(2,1)S(1)} %collective-permute-done.1.flip, bf16[128,768]{1,0:T(8,128)(2,1)S(1)} %collective-permute-done.step, ...), custom_call_target="tpu_custom_call" | custom-call | tf_op jit(solution)/shard_map/forward/pallas_call | solution.py:61
  17.3 0.5 collective-permute-done.4.refs_0_
  17.8 0.7 %middle.1 = (bf16[128,768]{1,0:T(8,128)(2,1)S(1)}, bf16[2,96,128]{2,1,0:T(8,128)(2,1)S(1)}, bf16[2,96,128]{2,1,0:T(8,128)(2,1)S(1)}, bf16[2,96,128]{2,1,0:T(8,128)(2,1)S(1)}, bf16[2,96,128]{2,1,0:T(8,128)(2,1)S(1)}) custom-call(bf16[128,768]{1,0:T(8,128)(2,1)S(1)} %collective-permute-done.4.refs_0_, f32[128,768]{1,0:T(8,128)S(1)} %get-tuple-element.49.refs_1_, ...), custom_call_target="tpu_custom_call" | custom-call | tf_op jit(solution)/shard_map/middle/pallas_call | solution.py:61
  18.5 1.2 %collective-permute-done.3.turn = bf16[128,768]{1,0:T(8,128)(2,1)S(1)} collective-permute-done((bf16[128,768]{1,0:T(8,128)(2,1)}, bf16[128,768]{1,0:T(8,128)(2,1)S(1)}, u32[]{:S(2)}, u32[]{:S(2)}) %collective-permute-start.3) | collective-permute-done | bytes 196640 | tf_op jit(solution)/shard_map/ppermute | solution.py:22
  19.6 0.3 line.1
  20.0 2.2 %collective-permute-start.10 = (bf16[2,96,128]{2,1,0:T(8,128)(2,1)S(1)}, bf16[2,96,128]{2,1,0:T(8,128)(2,1)S(1)}, u32[]{:S(2)}, u32[]{:S(2)}) collective-permute-start(bf16[2,96,128]{2,1,0:T(8,128)(2,1)S(1)} %get-tuple-element.65), channel_id=1, source_target_pairs={{0,6},{1,7},{2,4},{3,5},{4,2},{5,3},{6,0},{7,1},{8,14},{9,15},{10,... | collective-permute-start | bytes 147464 | tf_op jit(solution)/shard_map/ppermute | solution.py:22
  22.3 1.3 %collective-permute-start.8 = (bf16[2,96,128]{2,1,0:T(8,128)(2,1)S(1)}, bf16[2,96,128]{2,1,0:T(8,128)(2,1)S(1)}, u32[]{:S(2)}, u32[]{:S(2)}) collective-permute-start(bf16[2,96,128]{2,1,0:T(8,128)(2,1)S(1)} %get-tuple-element.63), channel_id=1, source_target_pairs={{0,2},{1,3},{2,0},{3,1},{4,6},{5,7},{6,4},{7,5},{8,10},{9,11},{10,... | collective-permute-start | bytes 147464 | tf_op jit(solution)/shard_map/ppermute | solution.py:22
  23.6 2.1 %collective-permute-start.6 = (bf16[128,768]{1,0:T(8,128)(2,1)S(1)}, bf16[128,768]{1,0:T(8,128)(2,1)S(1)}, u32[]{:S(2)}, u32[]{:S(2)}) collective-permute-start(bf16[128,768]{1,0:T(8,128)(2,1)S(1)} %get-tuple-element.56.refs_1_), channel_id=1, source_target_pairs={{0,16},{1,17},{2,18},{3,19},{4,20},{5,21},{6,22},{7,23},{8,24},{9,... | collective-permute-start | bytes 589832 | tf_op jit(solution)/shard_map/ppermute | solution.py:22
  25.7 0.6 %collective-permute-done.9.refs_2_ = bf16[2,96,128]{2,1,0:T(8,128)(2,1)S(1)} collective-permute-done((bf16[2,96,128]{2,1,0:T(8,128)(2,1)S(1)}, bf16[2,96,128]{2,1,0:T(8,128)(2,1)S(1)}, u32[]{:S(2)}, u32[]{:S(2)}) %collective-permute-start.9) | collective-permute-done | bytes 49184 | tf_op jit(solution)/shard_map/ppermute | solution.py:22
  26.5 1.3 %collective-permute-done.11.refs_4_ = bf16[4,96,128]{2,1,0:T(8,128)(2,1)S(1)} collective-permute-done((bf16[4,96,128]{2,1,0:T(8,128)(2,1)S(1)}, bf16[4,96,128]{2,1,0:T(8,128)(2,1)S(1)}, u32[]{:S(2)}, u32[]{:S(2)}) %collective-permute-start.11) | collective-permute-done | bytes 98336 | tf_op jit(solution)/shard_map/ppermute | solution.py:22
  28.0 2.7 %collective-permute-start.12 = (bf16[2,96,128]{2,1,0:T(8,128)(2,1)S(1)}, bf16[2,96,128]{2,1,0:T(8,128)(2,1)S(1)}, u32[]{:S(2)}, u32[]{:S(2)}) collective-permute-start(bf16[2,96,128]{2,1,0:T(8,128)(2,1)S(1)} %get-tuple-element.67), channel_id=1, source_target_pairs={{8,0},{9,1},{10,2},{11,3},{12,4},{13,5},{14,6},{15,7},{16,8},{17,9... | collective-permute-start | bytes 147464 | tf_op jit(solution)/shard_map/ppermute | solution.py:22
  30.7 3.1 %collective-permute-start.13 = (bf16[2,96,128]{2,1,0:T(8,128)(2,1)S(1)}, bf16[2,96,128]{2,1,0:T(8,128)(2,1)S(1)}, u32[]{:S(2)}, u32[]{:S(2)}) collective-permute-start(bf16[2,96,128]{2,1,0:T(8,128)(2,1)S(1)} %get-tuple-element.68), channel_id=1, source_target_pairs={{0,8},{1,9},{2,10},{3,11},{4,12},{5,13},{6,14},{7,15},{8,16},{9,17... | collective-permute-start | bytes 147464 | tf_op jit(solution)/shard_map/ppermute | solution.py:22
  33.8 0.4 collective-permute-done.12.ahead
  34.2 2.4 %collective-permute-done.13.behind = bf16[2,96,128]{2,1,0:T(8,128)(2,1)S(1)} collective-permute-done((bf16[2,96,128]{2,1,0:T(8,128)(2,1)S(1)}, bf16[2,96,128]{2,1,0:T(8,128)(2,1)S(1)}, u32[]{:S(2)}, u32[]{:S(2)}) %collective-permute-start.13) | collective-permute-done | bytes 49184 | tf_op jit(solution)/shard_map/ppermute | solution.py:22
  36.7 0.7 %terms.1 = (f32[3,24,768]{2,1,0:T(8,128)S(1)}, bf16[3,24,768]{2,1,0:T(8,128)(2,1)S(1)}, bf16[3,24,768]{2,1,0:T(8,128)(2,1)S(1)}, bf16[3,24,768]{2,1,0:T(8,128)(2,1)S(1)}) custom-call(bf16[2,96,512]{2,1,0:T(8,128)(2,1)S(1)} %get-tuple-element.66.cols, bf16[2,96,128]{2,1,0:T(8,128)(2,1)S(1)} %collective-permute-done.12.ahead, ...), custom_call_target="tpu_custom_call" | custom-call | tf_op jit(solution)/shard_map/terms/pallas_call | solution.py:61
  37.4 1.3 %collective-permute-start.17 = (bf16[3,24,768]{2,1,0:T(8,128)(2,1)S(1)}, bf16[3,24,768]{2,1,0:T(8,128)(2,1)S(1)}, u32[]{:S(2)}, u32[]{:S(2)}) collective-permute-start(bf16[3,24,768]{2,1,0:T(8,128)(2,1)S(1)} %get-tuple-element.78), channel_id=1, source_target_pairs={{0,24},{1,25},{2,26},{3,27},{4,28},{5,29},{6,30},{7,31},{8,16},{9,... | collective-permute-start | bytes 331784 | tf_op jit(solution)/shard_map/ppermute | solution.py:22
  38.6 2.4 %collective-permute-start.16 = (bf16[3,24,768]{2,1,0:T(8,128)(2,1)S(1)}, bf16[3,24,768]{2,1,0:T(8,128)(2,1)S(1)}, u32[]{:S(2)}, u32[]{:S(2)}) collective-permute-start(bf16[3,24,768]{2,1,0:T(8,128)(2,1)S(1)} %get-tuple-element.77), channel_id=1, source_target_pairs={{0,16},{1,17},{2,18},{3,19},{4,20},{5,21},{6,22},{7,23},{8,24},{9,... | collective-permute-start | bytes 331784 | tf_op jit(solution)/shard_map/ppermute | solution.py:22
  41.0 1.3 %collective-permute-start.7 = (bf16[128,768]{1,0:T(8,128)(2,1)S(1)}, bf16[128,768]{1,0:T(8,128)(2,1)S(1)}, u32[]{:S(2)}, u32[]{:S(2)}) collective-permute-start(bf16[128,768]{1,0:T(8,128)(2,1)S(1)} %get-tuple-element.70.middle), channel_id=1, source_target_pairs={{0,2},{1,3},{2,0},{3,1},{4,6},{5,7},{6,4},{7,5},{8,10},{9,11},{10,... | collective-permute-start | bytes 589832 | tf_op jit(solution)/shard_map/ppermute | solution.py:22
  42.3 4.1 %collective-permute-start.14 = (bf16[128,768]{1,0:T(8,128)(2,1)S(1)}, bf16[128,768]{1,0:T(8,128)(2,1)S(1)}, u32[]{:S(2)}, u32[]{:S(2)}) collective-permute-start(bf16[128,768]{1,0:T(8,128)(2,1)S(1)} %get-tuple-element.70.middle), channel_id=1, source_target_pairs={{2,4},{3,5},{4,2},{5,3},{6,8},{7,9},{8,6},{9,7},{10,12},{11,13},{1... | collective-permute-start | bytes 589832 | tf_op jit(solution)/shard_map/ppermute | solution.py:22
  46.4 1.1 %early_backward.1 = (f32[128,768]{1,0:T(8,128)S(1)}, f32[128,768]{1,0:T(8,128)S(1)}, bf16[768,768]{1,0:T(8,128)(2,1)S(1)}, bf16[768,768]{1,0:T(8,128)(2,1)S(1)}) custom-call(bf16[128,768]{1,0:T(8,128)(2,1)S(1)} %get-tuple-element.70.middle, bf16[128,768]{1,0:T(8,128)(2,1)S(1)} %get-tuple-element.71.features, bf16[3,768,768]{2,1,0:T(8,128)(2,1)S(1)} %get-tuple-element.46.taps), custom_call_target="tpu_custom_call" | custom-call | tf_op jit(solution)/shard_map/early_backward/pallas_call | solution.py:61
  47.5 1.2 %second_forward.1 = bf16[128,768]{1,0:T(8,128)(2,1)} custom-call(bf16[128,768]{1,0:T(8,128)(2,1)S(1)} %collective-permute-done.6.refs_0_, bf16[128,768]{1,0:T(8,128)(2,1)S(1)} %get-tuple-element.56.refs_1_, bf16[128,768]{1,0:T(8,128)(2,1)S(1)} %get-tuple-element.58.refs_2_, bf16[3,768,768]{2,1,0:T(8,128)(2,1)S(1)} %get-tuple-element.52.refs_4_.refs_3_), custom_call_target="tpu_custom_call" | custom-call | tf_op jit(solution)/shard_map/second_forward/pallas_call | solution.py:61
  48.6 0.2 collective-permute-done.16
  48.9 0.7 %add_bitcast_fusion = f32[3,768,24]{1,2,0:T(8,128)} fusion(f32[3,24,768]{2,1,0:T(8,128)S(1)} %get-tuple-element.69, bf16[3,24,768]{2,1,0:T(8,128)(2,1)S(1)} %collective-permute-done.17, bf16[3,24,768]{2,1,0:T(8,128)(2,1)S(1)} %collective-permute-done.16, bf16[3,24,768]{2,1,0:T(8,128)(2,1)S(1)} %collective-permute-done.15), kind=kLoop, calls=%fused_computation | loop fusion | flops 331776 | bytes 774144 | tf_op jit(solution)/shard_map/transpose | solution.py:288
  49.6 4.2 %collective-permute-done.14.step = bf16[128,768]{1,0:T(8,128)(2,1)S(1)} collective-permute-done((bf16[128,768]{1,0:T(8,128)(2,1)S(1)}, bf16[128,768]{1,0:T(8,128)(2,1)S(1)}, u32[]{:S(2)}, u32[]{:S(2)}) %collective-permute-start.14) | collective-permute-done | bytes 196640 | tf_op jit(solution)/shard_map/ppermute | solution.py:22
  53.8 1.2 %first_backward.1 = bf16[128,768]{1,0:T(8,128)(2,1)} custom-call(bf16[128,768]{1,0:T(8,128)(2,1)S(1)} %get-tuple-element.70.middle, bf16[128,768]{1,0:T(8,128)(2,1)S(1)} %collective-permute-done.7.flip, bf16[128,768]{1,0:T(8,128)(2,1)S(1)} %collective-permute-done.14.step, f32[128,768]{1,0:T(8,128)S(1)} %get-tuple-element.72.partial, ...), custom_call_target="tpu_custom_call" | custom-call | tf_op jit(solution)/shard_map/first_backward/pallas_call | solution.py:61
  (19 shorter events, 0.4 us)
Async XLA Ops:
  0.6 16.0 %collective-permute-start = (bf16[128,768]{1,0:T(8,128)(2,1)}, bf16[128,768]{1,0:T(8,128)(2,1)S(1)}, u32[]{:S(2)}, u32[]{:S(2)}) collective-permute-start(bf16[128,768]{1,0:T(8,128)(2,1)} %features.1), channel_id=1, source_target_pairs={{2,4},{3,5},{4,2},{5,3},{6,8},{7,9},{8,6},{9,7},{10,12},{11,13},{1... | collective-permute-start | bytes 589832 | tf_op jit(solution)/shard_map/ppermute | solution.py:22
  4.9 11.7 %collective-permute-start.1 = (bf16[128,768]{1,0:T(8,128)(2,1)}, bf16[128,768]{1,0:T(8,128)(2,1)S(1)}, u32[]{:S(2)}, u32[]{:S(2)}) collective-permute-start(bf16[128,768]{1,0:T(8,128)(2,1)} %features.1), channel_id=1, source_target_pairs={{0,2},{1,3},{2,0},{3,1},{4,6},{5,7},{6,4},{7,5},{8,10},{9,11},{10,... | collective-permute-start | bytes 589832 | tf_op jit(solution)/shard_map/ppermute | solution.py:22
  5.6 12.2 %collective-permute-start.4 = (bf16[128,768]{1,0:T(8,128)(2,1)}, bf16[128,768]{1,0:T(8,128)(2,1)S(1)}, u32[]{:S(2)}, u32[]{:S(2)}) collective-permute-start(bf16[128,768]{1,0:T(8,128)(2,1)} %up.1), channel_id=1, source_target_pairs={{0,16},{1,17},{2,18},{3,19},{4,20},{5,21},{6,22},{7,23},{8,24},{9,... | collective-permute-start | bytes 589832 | tf_op jit(solution)/shard_map/ppermute | solution.py:22
  5.9 12.5 %collective-permute-start.2 = (bf16[128,768]{1,0:T(8,128)(2,1)}, bf16[128,768]{1,0:T(8,128)(2,1)S(1)}, u32[]{:S(2)}, u32[]{:S(2)}) collective-permute-start(bf16[128,768]{1,0:T(8,128)(2,1)} %features.1), channel_id=1, source_target_pairs={{0,4},{1,5},{2,6},{3,7},{4,0},{5,1},{6,2},{7,3},{8,12},{9,13},{10,... | collective-permute-start | bytes 589832 | tf_op jit(solution)/shard_map/ppermute | solution.py:22
  7.5 12.2 %collective-permute-start.3 = (bf16[128,768]{1,0:T(8,128)(2,1)}, bf16[128,768]{1,0:T(8,128)(2,1)S(1)}, u32[]{:S(2)}, u32[]{:S(2)}) collective-permute-start(bf16[128,768]{1,0:T(8,128)(2,1)} %features.1), channel_id=1, source_target_pairs={{0,6},{1,7},{6,0},{7,1},{8,14},{9,15},{14,8},{15,9},{16,22},{17,23... | collective-permute-start | bytes 589832 | tf_op jit(solution)/shard_map/ppermute | solution.py:22
  19.9 13.9 %collective-permute-start.5 = (bf16[512,768]{1,0:T(8,128)(2,1)S(1)}, bf16[512,768]{1,0:T(8,128)(2,1)S(1)}, u32[]{:S(2)}, u32[]{:S(2)}) collective-permute-start(bf16[512,768]{1,0:T(8,128)(2,1)S(1)} %line.1), channel_id=1, source_target_pairs={{0,1},{1,0},{2,3},{3,2},{4,5},{5,4},{6,7},{7,6},{8,9},{9,8},{10,11... | collective-permute-start | bytes 2359304 | tf_op jit(solution)/shard_map/ppermute | solution.py:22
  20.0 5.7 %collective-permute-start.10 = (bf16[2,96,128]{2,1,0:T(8,128)(2,1)S(1)}, bf16[2,96,128]{2,1,0:T(8,128)(2,1)S(1)}, u32[]{:S(2)}, u32[]{:S(2)}) collective-permute-start(bf16[2,96,128]{2,1,0:T(8,128)(2,1)S(1)} %get-tuple-element.65), channel_id=1, source_target_pairs={{0,6},{1,7},{2,4},{3,5},{4,2},{5,3},{6,0},{7,1},{8,14},{9,15},{10,... | collective-permute-start | bytes 147464 | tf_op jit(solution)/shard_map/ppermute | solution.py:22
  22.3 4.1 %collective-permute-start.9 = (bf16[2,96,128]{2,1,0:T(8,128)(2,1)S(1)}, bf16[2,96,128]{2,1,0:T(8,128)(2,1)S(1)}, u32[]{:S(2)}, u32[]{:S(2)}) collective-permute-start(bf16[2,96,128]{2,1,0:T(8,128)(2,1)S(1)} %get-tuple-element.64), channel_id=1, source_target_pairs={{0,4},{1,5},{2,6},{3,7},{4,0},{5,1},{6,2},{7,3},{8,12},{9,13},{10,... | collective-permute-start | bytes 147464 | tf_op jit(solution)/shard_map/ppermute | solution.py:22
  22.3 4.1 %collective-permute-start.8 = (bf16[2,96,128]{2,1,0:T(8,128)(2,1)S(1)}, bf16[2,96,128]{2,1,0:T(8,128)(2,1)S(1)}, u32[]{:S(2)}, u32[]{:S(2)}) collective-permute-start(bf16[2,96,128]{2,1,0:T(8,128)(2,1)S(1)} %get-tuple-element.63), channel_id=1, source_target_pairs={{0,2},{1,3},{2,0},{3,1},{4,6},{5,7},{6,4},{7,5},{8,10},{9,11},{10,... | collective-permute-start | bytes 147464 | tf_op jit(solution)/shard_map/ppermute | solution.py:22
  23.6 10.2 %collective-permute-start.6 = (bf16[128,768]{1,0:T(8,128)(2,1)S(1)}, bf16[128,768]{1,0:T(8,128)(2,1)S(1)}, u32[]{:S(2)}, u32[]{:S(2)}) collective-permute-start(bf16[128,768]{1,0:T(8,128)(2,1)S(1)} %get-tuple-element.56.refs_1_), channel_id=1, source_target_pairs={{0,16},{1,17},{2,18},{3,19},{4,20},{5,21},{6,22},{7,23},{8,24},{9,... | collective-permute-start | bytes 589832 | tf_op jit(solution)/shard_map/ppermute | solution.py:22
  26.4 1.4 %collective-permute-start.11 = (bf16[4,96,128]{2,1,0:T(8,128)(2,1)S(1)}, bf16[4,96,128]{2,1,0:T(8,128)(2,1)S(1)}, u32[]{:S(2)}, u32[]{:S(2)}) collective-permute-start(bf16[4,96,128]{2,1,0:T(8,128)(2,1)S(1)} %pad_maximum_fusion), channel_id=1, source_target_pairs={{0,1},{1,0},{2,3},{3,2},{4,5},{5,4},{6,7},{7,6},{8,9},{9,8},{10,11... | collective-permute-start | bytes 294920 | tf_op jit(solution)/shard_map/ppermute | solution.py:22
  28.0 6.3 %collective-permute-start.12 = (bf16[2,96,128]{2,1,0:T(8,128)(2,1)S(1)}, bf16[2,96,128]{2,1,0:T(8,128)(2,1)S(1)}, u32[]{:S(2)}, u32[]{:S(2)}) collective-permute-start(bf16[2,96,128]{2,1,0:T(8,128)(2,1)S(1)} %get-tuple-element.67), channel_id=1, source_target_pairs={{8,0},{9,1},{10,2},{11,3},{12,4},{13,5},{14,6},{15,7},{16,8},{17,9... | collective-permute-start | bytes 147464 | tf_op jit(solution)/shard_map/ppermute | solution.py:22
  30.7 6.0 %collective-permute-start.13 = (bf16[2,96,128]{2,1,0:T(8,128)(2,1)S(1)}, bf16[2,96,128]{2,1,0:T(8,128)(2,1)S(1)}, u32[]{:S(2)}, u32[]{:S(2)}) collective-permute-start(bf16[2,96,128]{2,1,0:T(8,128)(2,1)S(1)} %get-tuple-element.68), channel_id=1, source_target_pairs={{0,8},{1,9},{2,10},{3,11},{4,12},{5,13},{6,14},{7,15},{8,16},{9,17... | collective-permute-start | bytes 147464 | tf_op jit(solution)/shard_map/ppermute | solution.py:22
  37.4 11.3 %collective-permute-start.17 = (bf16[3,24,768]{2,1,0:T(8,128)(2,1)S(1)}, bf16[3,24,768]{2,1,0:T(8,128)(2,1)S(1)}, u32[]{:S(2)}, u32[]{:S(2)}) collective-permute-start(bf16[3,24,768]{2,1,0:T(8,128)(2,1)S(1)} %get-tuple-element.78), channel_id=1, source_target_pairs={{0,24},{1,25},{2,26},{3,27},{4,28},{5,29},{6,30},{7,31},{8,16},{9,... | collective-permute-start | bytes 331784 | tf_op jit(solution)/shard_map/ppermute | solution.py:22
  38.6 10.2 %collective-permute-start.16 = (bf16[3,24,768]{2,1,0:T(8,128)(2,1)S(1)}, bf16[3,24,768]{2,1,0:T(8,128)(2,1)S(1)}, u32[]{:S(2)}, u32[]{:S(2)}) collective-permute-start(bf16[3,24,768]{2,1,0:T(8,128)(2,1)S(1)} %get-tuple-element.77), channel_id=1, source_target_pairs={{0,16},{1,17},{2,18},{3,19},{4,20},{5,21},{6,22},{7,23},{8,24},{9,... | collective-permute-start | bytes 331784 | tf_op jit(solution)/shard_map/ppermute | solution.py:22
  41.0 7.8 %collective-permute-start.15 = (bf16[3,24,768]{2,1,0:T(8,128)(2,1)S(1)}, bf16[3,24,768]{2,1,0:T(8,128)(2,1)S(1)}, u32[]{:S(2)}, u32[]{:S(2)}) collective-permute-start(bf16[3,24,768]{2,1,0:T(8,128)(2,1)S(1)} %get-tuple-element.76), channel_id=1, source_target_pairs={{0,8},{1,9},{2,10},{3,11},{4,12},{5,13},{6,14},{7,15},{8,0},{9,1},... | collective-permute-start | bytes 331784 | tf_op jit(solution)/shard_map/ppermute | solution.py:22
  41.0 8.6 %collective-permute-start.7 = (bf16[128,768]{1,0:T(8,128)(2,1)S(1)}, bf16[128,768]{1,0:T(8,128)(2,1)S(1)}, u32[]{:S(2)}, u32[]{:S(2)}) collective-permute-start(bf16[128,768]{1,0:T(8,128)(2,1)S(1)} %get-tuple-element.70.middle), channel_id=1, source_target_pairs={{0,2},{1,3},{2,0},{3,1},{4,6},{5,7},{6,4},{7,5},{8,10},{9,11},{10,... | collective-permute-start | bytes 589832 | tf_op jit(solution)/shard_map/ppermute | solution.py:22
  42.3 11.5 %collective-permute-start.14 = (bf16[128,768]{1,0:T(8,128)(2,1)S(1)}, bf16[128,768]{1,0:T(8,128)(2,1)S(1)}, u32[]{:S(2)}, u32[]{:S(2)}) collective-permute-start(bf16[128,768]{1,0:T(8,128)(2,1)S(1)} %get-tuple-element.70.middle), channel_id=1, source_target_pairs={{2,4},{3,5},{4,2},{5,3},{6,8},{7,9},{8,6},{9,7},{10,12},{11,13},{1... | collective-permute-start | bytes 589832 | tf_op jit(solution)/shard_map/ppermute | solution.py:22
